TPU v7x, 512 devices: a whole 4x8x8 slice. The times are simulated.
512 devices in a mesh: dp: 2 (over core), ctx: 64 (over z, y), head: 4 (over x).
Axes of the slice: x: 4, y: 8, z: 8, core: 2. Of those that a mesh axis runs over, the one named last changes fastest.
Arguments:
- queries: bfloat16 [2, 8192, 2560], P('dp', 'ctx', 'head'), may hold values from -25 to 25
- keys: bfloat16 [2, 8192, 2560], P('dp', 'ctx', 'head'), may hold values from -25 to 25
- values: bfloat16 [2, 8192, 2560], P('dp', 'ctx', 'head'), may hold values from -6 to 6
- grad_y: bfloat16 [2, 8192, 2560], P('dp', 'ctx', 'head'), may hold values from -6 to 6
- out_gain: float32 [2560], P('head'), may hold values from 0.1 to 1.9
- offsets: int32 [2, 20], P(None, 'head'), may hold values from 0 to 63, as said below
Outputs:
- attended: bfloat16 [2, 8192, 2560], P('dp', 'ctx', 'head')
- query_grad: bfloat16 [2, 8192, 2560], P('dp', 'ctx', 'head')
- key_grad: bfloat16 [2, 8192, 2560], P('dp', 'ctx', 'head')
- value_grad: bfloat16 [2, 8192, 2560], P('dp', 'ctx', 'head')
- gain_grad: float32 [2560], P('head')
Inputs may be any that keep to these rules, and one draw needn't show every extreme that they name: Row 0 holds offsets below 8, row 1 offsets below 64.
All inputs are finite; a program needn't handle non-finite values.
Results may differ from a plain program's by a relative error of at most 0.011.
Values may be sent and summed in bfloat16 or wider, within the bound.
A program may use at most 64 MiB of HBM per device.

v0:
```python
import math

import jax
import jax.numpy as jnp
from jax import lax
from jax.sharding import PartitionSpec as P

HEAD_DIM = 128
SPAN = 4
R1 = 8


EPS = 1e-06


def swapped(block, axis, bit):
    count = lax.axis_size(axis)
    route = []
    for low in range(count):
        high = low | 1 << bit
        if high != low and high < count:
            route += [(low, high), (high, low)]
    return lax.ppermute(block, axis, route)


def pick_rows(source_rows, dilation, shifts):
    row_count, head_count, head_width = source_rows.shape
    grouped = source_rows.reshape(row_count // dilation, dilation, head_count, head_width)
    hit_mask = jnp.arange(dilation, dtype=jnp.int32).reshape(1, dilation, 1, 1) == shifts.reshape(
        1, 1, head_count, 1
    )
    chosen = jnp.where(hit_mask, grouped, jnp.zeros((), source_rows.dtype))
    return jnp.sum(chosen, axis=1, dtype=source_rows.dtype)


def place_rows(row_values, dilation, shifts):
    row_count, head_count, head_width = row_values.shape
    hit_mask = jnp.arange(dilation, dtype=jnp.int32).reshape(1, dilation, 1, 1) == shifts.reshape(
        1, 1, head_count, 1
    )
    spread = jnp.where(hit_mask, row_values[:, None], jnp.zeros((), row_values.dtype))
    return spread.reshape(row_count * dilation, head_count, head_width)


def level_scores(q_rows, k_rows):
    score_scale = 1.0 / math.sqrt(q_rows.shape[-1])
    return (
        jnp.einsum("qhe,khe->hqk", q_rows, k_rows, preferred_element_type=jnp.float32) * score_scale
    )


def attend(q_rows, k_rows, v_rows):
    scores = level_scores(q_rows, k_rows)
    row_max = jnp.max(scores, axis=-1, keepdims=True)
    log_total = row_max[..., 0] + jnp.log(jnp.sum(jnp.exp(scores - row_max), axis=-1))
    soft_rows = jnp.exp(scores - log_total[..., None]).astype(jnp.bfloat16)
    level_out = jnp.einsum("hqk,khe->qhe", soft_rows, v_rows, preferred_element_type=jnp.float32)
    return (level_out, log_total.T)


def score_grads(q_rows, k_rows, v_rows, log_total, grad_low, row_shift):
    score_scale = 1.0 / math.sqrt(q_rows.shape[-1])
    scores = level_scores(q_rows, k_rows)
    exact_soft = jnp.exp(scores - log_total.T[..., None])
    prob_grad = jnp.einsum("qhe,khe->hqk", grad_low, v_rows, preferred_element_type=jnp.float32)
    score_grad = (exact_soft * (prob_grad + row_shift.T[..., None]) * score_scale).astype(
        jnp.bfloat16
    )
    return (score_grad, exact_soft.astype(jnp.bfloat16))


def key_parts(score_grad, soft_low, q_rows, grad_low):
    k_part = jnp.einsum("hqk,qhe->khe", score_grad, q_rows, preferred_element_type=jnp.float32)
    v_part = jnp.einsum("hqk,qhe->khe", soft_low, grad_low, preferred_element_type=jnp.float32)
    return (k_part, v_part)


def query_part(score_grad, k_rows):
    return jnp.einsum("hqk,khe->qhe", score_grad, k_rows, preferred_element_type=jnp.float32)


def shards(queries, keys, values, grad_y, out_gain, offsets):
    tokens = queries.shape[1]
    flat_width = queries.shape[2]
    head_count = flat_width // HEAD_DIM
    row_shape = (tokens, head_count, HEAD_DIM)
    q_own = queries[0].reshape(row_shape)
    k_own = keys[0].reshape(row_shape)
    v_own = values[0].reshape(row_shape)
    ctx_size = lax.axis_size("ctx")
    span_bits = SPAN.bit_length() - 1
    my_place = lax.axis_index("ctx")
    mid_shift = offsets[0]
    top_shift = offsets[1]
    positions = jnp.arange(tokens, dtype=jnp.int32)
    mid_hit = (positions % R1)[:, None] == mid_shift[None, :]
    top_hit = (positions % ctx_size)[:, None] == top_shift[None, :]
    mid_q = pick_rows(q_own, R1, mid_shift)
    mid_k = pick_rows(k_own, R1, mid_shift)
    mid_v = pick_rows(v_own, R1, mid_shift)
    top_q = pick_rows(q_own, ctx_size, top_shift)
    top_k = pick_rows(k_own, ctx_size, top_shift)
    top_v = pick_rows(v_own, ctx_size, top_shift)
    mid_keys = mid_k.reshape(-1, flat_width)
    mid_vals = mid_v.reshape(-1, flat_width)
    top_keys = top_k.reshape(-1, flat_width)
    top_vals = top_v.reshape(-1, flat_width)

    def append_peer(mine, received, level_bit):
        upper_side = my_place >> level_bit & 1 == 1
        return jnp.where(
            upper_side, jnp.concatenate([received, mine], 0), jnp.concatenate([mine, received], 0)
        )

    for level_bit in range(span_bits):
        received = swapped((mid_keys, mid_vals), "ctx", level_bit)
        mid_keys = append_peer(mid_keys, received[0], level_bit)
        mid_vals = append_peer(mid_vals, received[1], level_bit)
    top_keys, top_vals = (
        lax.all_gather(top_keys, "ctx", axis=0, tiled=True),
        lax.all_gather(top_vals, "ctx", axis=0, tiled=True),
    )
    mid_keys = mid_keys.reshape(-1, head_count, HEAD_DIM)
    mid_vals = mid_vals.reshape(-1, head_count, HEAD_DIM)
    top_keys = top_keys.reshape(-1, head_count, HEAD_DIM)
    top_vals = top_vals.reshape(-1, head_count, HEAD_DIM)
    base_out, base_total = attend(q_own, k_own, v_own)
    mid_out, mid_total = attend(mid_q, mid_keys, mid_vals)
    top_out, top_total = attend(top_q, top_keys, top_vals)
    mid_full = place_rows(mid_total[..., None], R1, mid_shift)[..., 0]
    top_full = place_rows(top_total[..., None], ctx_size, top_shift)[..., 0]
    row_max = jnp.maximum(base_total, jnp.where(mid_hit, mid_full, base_total))
    row_max = jnp.maximum(row_max, jnp.where(top_hit, top_full, base_total))
    base_expo = jnp.exp(base_total - row_max)
    mid_expo = jnp.where(mid_hit, jnp.exp(mid_full - row_max), 0.0)
    top_expo = jnp.where(top_hit, jnp.exp(top_full - row_max), 0.0)
    denom = base_expo + mid_expo + top_expo
    base_share = base_expo / denom
    mid_share = mid_expo / denom
    top_share = top_expo / denom
    attn = (
        base_share[..., None] * base_out
        + mid_share[..., None] * place_rows(mid_out, R1, mid_shift)
        + top_share[..., None] * place_rows(top_out, ctx_size, top_shift)
    )
    inv_rms = lax.rsqrt(jnp.mean(attn * attn, axis=-1, keepdims=True) + EPS)
    normed = attn * inv_rms
    gain_rows = out_gain.reshape(head_count, HEAD_DIM)
    attended = (normed * gain_rows).astype(jnp.bfloat16).reshape(1, tokens, flat_width)
    grad_full = grad_y[0].reshape(row_shape).astype(jnp.float32)
    gain_part = jnp.sum(grad_full * normed, axis=0).reshape(flat_width)
    gain_grad = lax.psum(gain_part, ("dp", "ctx"))
    grad_norm = grad_full * gain_rows
    grad_attn = inv_rms * (
        grad_norm - normed * jnp.mean(grad_norm * normed, axis=-1, keepdims=True)
    )
    inner = jnp.sum(grad_attn * attn, axis=-1)
    base_low = (base_share[..., None] * grad_attn).astype(jnp.bfloat16)
    base_shift = -(base_share * inner)
    base_grad, base_soft = score_grads(q_own, k_own, v_own, base_total, base_low, base_shift)
    base_dq = query_part(base_grad, k_own)
    base_dk, base_dv = key_parts(base_grad, base_soft, q_own, base_low)
    mid_sel = pick_rows(mid_share[..., None], R1, mid_shift)[..., 0]
    mid_low = (mid_sel[..., None] * pick_rows(grad_attn, R1, mid_shift)).astype(jnp.bfloat16)
    mid_row_shift = -(mid_sel * pick_rows(inner[..., None], R1, mid_shift)[..., 0])
    mid_grad, mid_soft = score_grads(mid_q, mid_keys, mid_vals, mid_total, mid_low, mid_row_shift)
    mid_dq = query_part(mid_grad, mid_keys)
    mid_dk, mid_dv = key_parts(mid_grad, mid_soft, mid_q, mid_low)
    mid_dk = mid_dk.reshape(-1, flat_width)
    mid_dv = mid_dv.reshape(-1, flat_width)
    for level_bit in reversed(range(span_bits)):
        half_rows = mid_dk.shape[0] // 2
        upper_side = my_place >> level_bit & 1 == 1
        keep_k = jnp.where(upper_side, mid_dk[half_rows:], mid_dk[:half_rows])
        keep_v = jnp.where(upper_side, mid_dv[half_rows:], mid_dv[:half_rows])
        send_k = jnp.where(upper_side, mid_dk[:half_rows], mid_dk[half_rows:])
        send_v = jnp.where(upper_side, mid_dv[:half_rows], mid_dv[half_rows:])
        received = (
            swapped(send_k.astype(jnp.bfloat16), "ctx", level_bit).astype(send_k.dtype),
            swapped(send_v.astype(jnp.bfloat16), "ctx", level_bit).astype(send_v.dtype),
        )
        mid_dk = keep_k + received[0]
        mid_dv = keep_v + received[1]
    mid_dk = mid_dk.reshape(-1, head_count, HEAD_DIM)
    mid_dv = mid_dv.reshape(-1, head_count, HEAD_DIM)
    top_sel = pick_rows(top_share[..., None], ctx_size, top_shift)[..., 0]
    top_low = (top_sel[..., None] * pick_rows(grad_attn, ctx_size, top_shift)).astype(jnp.bfloat16)
    top_row_shift = -(top_sel * pick_rows(inner[..., None], ctx_size, top_shift)[..., 0])
    top_grad, top_soft = score_grads(top_q, top_keys, top_vals, top_total, top_low, top_row_shift)
    top_dq = query_part(top_grad, top_keys)
    gathered_dk, gathered_dv = key_parts(top_grad, top_soft, top_q, top_low)
    summed = (
        lax.psum_scatter(
            gathered_dk.reshape(-1, flat_width), "ctx", scatter_dimension=0, tiled=True
        ),
        lax.psum_scatter(
            gathered_dv.reshape(-1, flat_width), "ctx", scatter_dimension=0, tiled=True
        ),
    )
    top_dk = summed[0].reshape(-1, head_count, HEAD_DIM)
    top_dv = summed[1].reshape(-1, head_count, HEAD_DIM)
    query_grad = (
        base_dq + place_rows(mid_dq, R1, mid_shift) + place_rows(top_dq, ctx_size, top_shift)
    )
    key_grad = base_dk + place_rows(mid_dk, R1, mid_shift) + place_rows(top_dk, ctx_size, top_shift)
    value_grad = (
        base_dv + place_rows(mid_dv, R1, mid_shift) + place_rows(top_dv, ctx_size, top_shift)
    )
    out_shape = (1, tokens, flat_width)
    return (
        attended,
        query_grad.astype(jnp.bfloat16).reshape(out_shape),
        key_grad.astype(jnp.bfloat16).reshape(out_shape),
        value_grad.astype(jnp.bfloat16).reshape(out_shape),
        gain_grad,
    )


def solution(mesh):
    in_specs = (
        P("dp", "ctx", "head"),
        P("dp", "ctx", "head"),
        P("dp", "ctx", "head"),
        P("dp", "ctx", "head"),
        P("head"),
        P(None, "head"),
    )
    out_specs = (
        P("dp", "ctx", "head"),
        P("dp", "ctx", "head"),
        P("dp", "ctx", "head"),
        P("dp", "ctx", "head"),
        P("head"),
    )
    return jax.shard_map(shards, mesh=mesh, in_specs=in_specs, out_specs=out_specs, check_vma=False)
```

profile of v0, /device:TPU:260, one launch (start us, length us, event | category | flops | bytes accessed | tf_op | source)
XLA Modules:
  0.0 442.6 jit_solution(7934693849912801585)
XLA Ops:
  7.2 0.8 slice_bitcast_fusion.1
  8.0 1.5 fusion.26
  9.6 3.5 collective-permute-start
  13.1 2.5 collective-permute-start.2
  16.4 0.7 copy-done.2
  17.8 49.4 %all-gather = bf16[64,2,640]{2,1,0:T(2,128)(2,1)S(1)} all-gather(bf16[1,2,640]{2,1,0:T(2,128)(2,1)S(1)} %reshape.367), channel_id=1, replica_groups=mesh['dp'=2,'ctx'=64,'head'=4] {'ctx'}, dimensions={0}, use_global_device_ids=true | all-gather | bytes 166400 | tf_op jit(solution)/shard_map/all_gather | solution.py:120
  67.8 47.3 %all-gather.1 = bf16[64,2,640]{2,1,0:T(2,128)(2,1)S(1)} all-gather(bf16[1,2,640]{2,1,0:T(2,128)(2,1)S(1)} %reshape.369), channel_id=1, replica_groups=mesh['dp'=2,'ctx'=64,'head'=4] {'ctx'}, dimensions={0}, use_global_device_ids=true | all-gather | bytes 166400 | tf_op jit(solution)/shard_map/all_gather | solution.py:121
  116.2 0.5 copy-done.4
  117.2 1.3 dynamic-slice
  119.2 3.8 collective-permute-start.1
  123.0 2.9 collective-permute-start.3
  126.0 0.5 collective-permute-done.1
  127.6 2.3 collective-permute-done.3
  130.0 0.5 multiply_reduce_fusion.3
  130.6 0.7 copy-done.5
  131.3 0.3 multiply_reduce_fusion
  133.1 1.0 fusion.50
  134.1 1.0 fusion.47
  135.1 0.4 fusion.14
  135.6 0.3 convolution_bitcast_fusion.4
  136.2 2.9 collective-permute-start.6
  139.5 3.8 collective-permute-start.4
  143.5 0.8 copy.198
  144.3 278.0 %psum.7 = f32[640]{0:T(1024)} all-reduce(f32[640]{0:T(1024)S(1)} %bitcast.253), channel_id=1, replica_groups=mesh['dp'=2,'ctx'=64,'head'=4] {'dp','ctx'}, use_global_device_ids=true, to_apply=%region_24.25 | all-reduce | flops 640 | bytes 5120 | tf_op jit(solution)/shard_map/psum | solution.py:152
  422.4 1.9 collective-permute-start.7
  424.4 3.9 collective-permute-start.5
  428.3 1.7 collective-permute-done.5
  430.1 1.2 constant_dynamic-slice_fusion.1
  432.3 0.8 copy.200
  433.6 0.8 copy.199
  434.4 0.3 fusion.13
  434.9 0.8 copy.201
  (105 shorter events, 9.2 us)
Async XLA Ops:
  7.2 422.9 %all-reduce.5.cloned.1.call-start = ((), (), s32[]{:S(2)}) async-start(), calls=%async_computation | async-start | bytes 1310720
  8.0 7.6 %copy-start = (bf16[1,128,640]{2,1,0:T(8,128)(2,1)S(1)}, bf16[1,128,640]{2,1,0:T(8,128)(2,1)}, u32[]{:S(2)}) copy-start(bf16[1,128,640]{2,1,0:T(8,128)(2,1)} %param.6) | copy-start | bytes 491524
  9.6 109.5 %collective-permute-start = (bf16[16,640]{1,0:T(8,128)(2,1)S(1)}, bf16[16,640]{1,0:T(8,128)(2,1)S(1)}, u32[]{:S(2)}, u32[]{:S(2)}) collective-permute-start(bf16[16,640]{1,0:T(8,128)(2,1)S(1)} %copy_bitcast_fusion.7), channel_id=1, source_target_pairs={{0,4},{4,0},{8,12},{12,8},{16,20},{20,16},{24,28},{28,24},{32,36},... | collective-permute-start | bytes 61448 | tf_op jit(solution)/shard_map/ppermute | solution.py:23
  13.1 2.7 copy-start.1
  13.1 106.0 %collective-permute-start.2 = (bf16[16,640]{1,0:T(8,128)(2,1)S(1)}, bf16[16,640]{1,0:T(8,128)(2,1)S(1)}, u32[]{:S(2)}, u32[]{:S(2)}) collective-permute-start(bf16[16,640]{1,0:T(8,128)(2,1)S(1)} %copy_bitcast_fusion.6), channel_id=1, source_target_pairs={{0,4},{4,0},{8,12},{12,8},{16,20},{20,16},{24,28},{28,24},{32,36},... | collective-permute-start | bytes 61448 | tf_op jit(solution)/shard_map/ppermute | solution.py:23
  16.2 0.9 copy-start.2
  115.8 0.9 copy-start.4
  119.2 7.2 %collective-permute-start.1 = (bf16[32,640]{1,0:T(8,128)(2,1)S(1)}, bf16[32,640]{1,0:T(8,128)(2,1)S(1)}, u32[]{:S(2)}, u32[]{:S(2)}) collective-permute-start(bf16[32,640]{1,0:T(8,128)(2,1)S(1)} %maximum_select_fusion.2), channel_id=1, source_target_pairs={{0,8},{8,0},{4,12},{12,4},{16,24},{24,16},{20,28},{28,20},{32,40},... | collective-permute-start | bytes 122888 | tf_op jit(solution)/shard_map/ppermute | solution.py:23
  123.0 6.8 %collective-permute-start.3 = (bf16[32,640]{1,0:T(8,128)(2,1)S(1)}, bf16[32,640]{1,0:T(8,128)(2,1)S(1)}, u32[]{:S(2)}, u32[]{:S(2)}) collective-permute-start(bf16[32,640]{1,0:T(8,128)(2,1)S(1)} %maximum_select_fusion.4), channel_id=1, source_target_pairs={{0,8},{8,0},{4,12},{12,4},{16,24},{24,16},{20,28},{28,20},{32,40},... | collective-permute-start | bytes 122888 | tf_op jit(solution)/shard_map/ppermute | solution.py:23
  130.6 0.7 copy-start.5
  136.2 286.2 %collective-permute-start.6 = (bf16[32,640]{1,0:T(8,128)(2,1)S(1)}, bf16[32,640]{1,0:T(8,128)(2,1)S(1)}, u32[]{:S(2)}, u32[]{:S(2)}) collective-permute-start(bf16[32,640]{1,0:T(8,128)(2,1)S(1)} %copy_bitcast_fusion), channel_id=1, source_target_pairs={{0,8},{8,0},{4,12},{12,4},{16,24},{24,16},{20,28},{28,20},{32,40},... | collective-permute-start | bytes 122888 | tf_op jit(solution)/shard_map/ppermute | solution.py:23
  139.5 284.9 %collective-permute-start.4 = (bf16[32,640]{1,0:T(8,128)(2,1)S(1)}, bf16[32,640]{1,0:T(8,128)(2,1)S(1)}, u32[]{:S(2)}, u32[]{:S(2)}) collective-permute-start(bf16[32,640]{1,0:T(8,128)(2,1)S(1)} %copy_bitcast_fusion.1), channel_id=1, source_target_pairs={{0,8},{8,0},{4,12},{12,4},{16,24},{24,16},{20,28},{28,20},{32,40},... | collective-permute-start | bytes 122888 | tf_op jit(solution)/shard_map/ppermute | solution.py:23
  422.4 5.9 %collective-permute-start.7 = (bf16[16,640]{1,0:T(8,128)(2,1)S(1)}, bf16[16,640]{1,0:T(8,128)(2,1)S(1)}, u32[]{:S(2)}, u32[]{:S(2)}) collective-permute-start(bf16[16,640]{1,0:T(8,128)(2,1)S(1)} %select_convert_fusion.2), channel_id=1, source_target_pairs={{0,4},{4,0},{8,12},{12,8},{16,20},{20,16},{24,28},{28,24},{32,36},... | collective-permute-start | bytes 61448 | tf_op jit(solution)/shard_map/ppermute | solution.py:23
  424.4 5.7 %collective-permute-start.5 = (bf16[16,640]{1,0:T(8,128)(2,1)S(1)}, bf16[16,640]{1,0:T(8,128)(2,1)S(1)}, u32[]{:S(2)}, u32[]{:S(2)}) collective-permute-start(bf16[16,640]{1,0:T(8,128)(2,1)S(1)} %select_convert_fusion.3), channel_id=1, source_target_pairs={{0,4},{4,0},{8,12},{12,8},{16,20},{20,16},{24,28},{28,24},{32,36},... | collective-permute-start | bytes 61448 | tf_op jit(solution)/shard_map/ppermute | solution.py:23
  430.1 1.2 copy-start.3
Sparse Core Ops, SparseCore 0:
  144.4 154.1 all-reduce.4
where the time goes:
time: 444 us; the launch traced here: 443 us
  blocking collectives  375 us (84%)
  starting transfers between devices  25.3 us (6%)
  between operations  15.2 us (3%)
  local copies, waits for them, and re-layouts  12.3 us (3%)
  matrix products  6.13 us (1%)
  waiting for transfers between devices  4.5 us (1%)
    psum x1, blocking collectives, shards(): gain_grad = lax.psum(gain_part, ('dp', 'ctx'))  278 us
    all_gather x1, blocking collectives, shards(): lax.all_gather(top_keys, 'ctx', axis=0, tiled=True)  49.4 us
    all_gather x1, blocking collectives, shards(): lax.all_gather(top_vals, 'ctx', axis=0, tiled=True)  47.3 us
    ppermute x8, starting transfers between devices, swapped(): return lax.ppermute(block, axis, route)  25.3 us
  transfers between devices with their start and end apart: 9, of which 3 were waited for; matrix products, arithmetic and copies ran while one was open for 2% of the time, Pallas kernels for 0%

commit v1 on v0

--- a/solution.py
+++ b/solution.py
@@ -13,14 +13,16 @@
 EPS = 1e-06
 
 
-def swapped(block, axis, bit):
+def group_gather(block, axis, group):
     count = lax.axis_size(axis)
-    route = []
-    for low in range(count):
-        high = low | 1 << bit
-        if high != low and high < count:
-            route += [(low, high), (high, low)]
-    return lax.ppermute(block, axis, route)
+    pieces = [block]
+    for shift in range(1, group):
+        route = []
+        for src in range(count):
+            base = src - src % group
+            route.append((src, base + (src % group + shift) % group))
+        pieces.append(lax.ppermute(block, axis, route))
+    return jnp.concatenate(pieces, 0)
 
 
 def pick_rows(source_rows, dilation, shifts):
@@ -77,6 +79,25 @@
 
 def query_part(score_grad, k_rows):
     return jnp.einsum("hqk,khe->qhe", score_grad, k_rows, preferred_element_type=jnp.float32)
+
+
+def split_qkv(packed, head_count):
+    width = head_count * HEAD_DIM
+    shape = (packed.shape[0], head_count, HEAD_DIM)
+    return tuple(packed[:, i * width : (i + 1) * width].reshape(shape) for i in range(3))
+
+
+def pack_grads(grad_low, row_shift):
+    rows = grad_low.shape[0]
+    return jnp.concatenate(
+        [grad_low.astype(jnp.float32).reshape(rows, -1), row_shift.astype(jnp.float32)], 1
+    )
+
+
+def unpack_grads(packed, head_count):
+    width = head_count * HEAD_DIM
+    grad_low = packed[:, :width].astype(jnp.bfloat16).reshape(-1, head_count, HEAD_DIM)
+    return grad_low, packed[:, width:]
 
 
 def shards(queries, keys, values, grad_y, out_gain, offsets):
@@ -88,45 +109,33 @@
     k_own = keys[0].reshape(row_shape)
     v_own = values[0].reshape(row_shape)
     ctx_size = lax.axis_size("ctx")
-    span_bits = SPAN.bit_length() - 1
     my_place = lax.axis_index("ctx")
     mid_shift = offsets[0]
     top_shift = offsets[1]
     positions = jnp.arange(tokens, dtype=jnp.int32)
     mid_hit = (positions % R1)[:, None] == mid_shift[None, :]
     top_hit = (positions % ctx_size)[:, None] == top_shift[None, :]
-    mid_q = pick_rows(q_own, R1, mid_shift)
-    mid_k = pick_rows(k_own, R1, mid_shift)
-    mid_v = pick_rows(v_own, R1, mid_shift)
-    top_q = pick_rows(q_own, ctx_size, top_shift)
-    top_k = pick_rows(k_own, ctx_size, top_shift)
-    top_v = pick_rows(v_own, ctx_size, top_shift)
-    mid_keys = mid_k.reshape(-1, flat_width)
-    mid_vals = mid_v.reshape(-1, flat_width)
-    top_keys = top_k.reshape(-1, flat_width)
-    top_vals = top_v.reshape(-1, flat_width)
-
-    def append_peer(mine, received, level_bit):
-        upper_side = my_place >> level_bit & 1 == 1
-        return jnp.where(
-            upper_side, jnp.concatenate([received, mine], 0), jnp.concatenate([mine, received], 0)
-        )
-
-    for level_bit in range(span_bits):
-        received = swapped((mid_keys, mid_vals), "ctx", level_bit)
-        mid_keys = append_peer(mid_keys, received[0], level_bit)
-        mid_vals = append_peer(mid_vals, received[1], level_bit)
-    top_keys, top_vals = (
-        lax.all_gather(top_keys, "ctx", axis=0, tiled=True),
-        lax.all_gather(top_vals, "ctx", axis=0, tiled=True),
-    )
-    mid_keys = mid_keys.reshape(-1, head_count, HEAD_DIM)
-    mid_vals = mid_vals.reshape(-1, head_count, HEAD_DIM)
-    top_keys = top_keys.reshape(-1, head_count, HEAD_DIM)
-    top_vals = top_vals.reshape(-1, head_count, HEAD_DIM)
+    mid_pack = jnp.concatenate(
+        [pick_rows(x, R1, mid_shift).reshape(-1, flat_width) for x in (q_own, k_own, v_own)], 1
+    )
+    top_pack = jnp.concatenate(
+        [pick_rows(x, ctx_size, top_shift).reshape(-1, flat_width) for x in (q_own, k_own, v_own)],
+        1,
+    )
+    mid_rows = mid_pack.shape[0]
+    top_rows = top_pack.shape[0]
+    mid_all = group_gather(mid_pack, "ctx", SPAN)
+    top_all = lax.all_gather(top_pack, "ctx", axis=0, tiled=True)
+    mid_q, mid_k, mid_v = split_qkv(mid_all, head_count)
+    top_q, top_k, top_v = split_qkv(top_all, head_count)
+    top_start = my_place * top_rows
     base_out, base_total = attend(q_own, k_own, v_own)
-    mid_out, mid_total = attend(mid_q, mid_keys, mid_vals)
-    top_out, top_total = attend(top_q, top_keys, top_vals)
+    mid_out_all, mid_total_all = attend(mid_q, mid_k, mid_v)
+    top_out_all, top_total_all = attend(top_q, top_k, top_v)
+    mid_out = mid_out_all[:mid_rows]
+    mid_total = mid_total_all[:mid_rows]
+    top_out = lax.dynamic_slice_in_dim(top_out_all, top_start, top_rows, 0)
+    top_total = lax.dynamic_slice_in_dim(top_total_all, top_start, top_rows, 0)
     mid_full = place_rows(mid_total[..., None], R1, mid_shift)[..., 0]
     top_full = place_rows(top_total[..., None], ctx_size, top_shift)[..., 0]
     row_max = jnp.maximum(base_total, jnp.where(mid_hit, mid_full, base_total))
@@ -160,45 +169,36 @@
     base_grad, base_soft = score_grads(q_own, k_own, v_own, base_total, base_low, base_shift)
     base_dq = query_part(base_grad, k_own)
     base_dk, base_dv = key_parts(base_grad, base_soft, q_own, base_low)
+
     mid_sel = pick_rows(mid_share[..., None], R1, mid_shift)[..., 0]
     mid_low = (mid_sel[..., None] * pick_rows(grad_attn, R1, mid_shift)).astype(jnp.bfloat16)
     mid_row_shift = -(mid_sel * pick_rows(inner[..., None], R1, mid_shift)[..., 0])
-    mid_grad, mid_soft = score_grads(mid_q, mid_keys, mid_vals, mid_total, mid_low, mid_row_shift)
-    mid_dq = query_part(mid_grad, mid_keys)
-    mid_dk, mid_dv = key_parts(mid_grad, mid_soft, mid_q, mid_low)
-    mid_dk = mid_dk.reshape(-1, flat_width)
-    mid_dv = mid_dv.reshape(-1, flat_width)
-    for level_bit in reversed(range(span_bits)):
-        half_rows = mid_dk.shape[0] // 2
-        upper_side = my_place >> level_bit & 1 == 1
-        keep_k = jnp.where(upper_side, mid_dk[half_rows:], mid_dk[:half_rows])
-        keep_v = jnp.where(upper_side, mid_dv[half_rows:], mid_dv[:half_rows])
-        send_k = jnp.where(upper_side, mid_dk[:half_rows], mid_dk[half_rows:])
-        send_v = jnp.where(upper_side, mid_dv[:half_rows], mid_dv[half_rows:])
-        received = (
-            swapped(send_k.astype(jnp.bfloat16), "ctx", level_bit).astype(send_k.dtype),
-            swapped(send_v.astype(jnp.bfloat16), "ctx", level_bit).astype(send_v.dtype),
-        )
-        mid_dk = keep_k + received[0]
-        mid_dv = keep_v + received[1]
-    mid_dk = mid_dk.reshape(-1, head_count, HEAD_DIM)
-    mid_dv = mid_dv.reshape(-1, head_count, HEAD_DIM)
     top_sel = pick_rows(top_share[..., None], ctx_size, top_shift)[..., 0]
     top_low = (top_sel[..., None] * pick_rows(grad_attn, ctx_size, top_shift)).astype(jnp.bfloat16)
     top_row_shift = -(top_sel * pick_rows(inner[..., None], ctx_size, top_shift)[..., 0])
-    top_grad, top_soft = score_grads(top_q, top_keys, top_vals, top_total, top_low, top_row_shift)
-    top_dq = query_part(top_grad, top_keys)
-    gathered_dk, gathered_dv = key_parts(top_grad, top_soft, top_q, top_low)
-    summed = (
-        lax.psum_scatter(
-            gathered_dk.reshape(-1, flat_width), "ctx", scatter_dimension=0, tiled=True
-        ),
-        lax.psum_scatter(
-            gathered_dv.reshape(-1, flat_width), "ctx", scatter_dimension=0, tiled=True
-        ),
-    )
-    top_dk = summed[0].reshape(-1, head_count, HEAD_DIM)
-    top_dv = summed[1].reshape(-1, head_count, HEAD_DIM)
+
+    mid_low_all, mid_shift_all = unpack_grads(
+        group_gather(pack_grads(mid_low, mid_row_shift), "ctx", SPAN), head_count
+    )
+    top_low_all, top_shift_all = unpack_grads(
+        lax.all_gather(pack_grads(top_low, top_row_shift), "ctx", axis=0, tiled=True), head_count
+    )
+
+    mid_grad, mid_soft = score_grads(
+        mid_q, mid_k, mid_v, mid_total_all, mid_low_all, mid_shift_all
+    )
+    mid_dq = query_part(mid_grad[:, :mid_rows], mid_k)
+    mid_dk, mid_dv = key_parts(
+        mid_grad[:, :, :mid_rows], mid_soft[:, :, :mid_rows], mid_q, mid_low_all
+    )
+    top_grad, top_soft = score_grads(
+        top_q, top_k, top_v, top_total_all, top_low_all, top_shift_all
+    )
+    own_grad = lax.dynamic_slice_in_dim(top_grad, top_start, top_rows, 1)
+    top_dq = query_part(own_grad, top_k)
+    key_grad_cols = lax.dynamic_slice_in_dim(top_grad, top_start, top_rows, 2)
+    key_soft_cols = lax.dynamic_slice_in_dim(top_soft, top_start, top_rows, 2)
+    top_dk, top_dv = key_parts(key_grad_cols, key_soft_cols, top_q, top_low_all)
     query_grad = (
         base_dq + place_rows(mid_dq, R1, mid_shift) + place_rows(top_dq, ctx_size, top_shift)
     )

time: 444 us -> 429 us (0.966)
  the two profiles are of different devices: /device:TPU:260 before, /device:TPU:256 now
where the time goes in v1:
time: 429 us
  blocking collectives  377 us (88%)
  local copies, waits for them, and re-layouts  19.9 us (5%)
  starting transfers between devices  18.3 us (4%)
  other arithmetic  7.42 us (2%)
  matrix products  4.56 us (1%)
    psum x1, blocking collectives, shards(): gain_grad = lax.psum(gain_part, ('dp', 'ctx'))  278 us
    all_gather x1, blocking collectives, shards(): top_all = lax.all_gather(top_pack, 'ctx', axis=0, tiled=True)  50 us
    all_gather x1, blocking collectives, shards(): lax.all_gather(pack_grads(top_low, top_row_shift), 'ctx', axis=0, tiled=T...  49.2 us
    ppermute x6, starting transfers between devices, group_gather(): pieces.append(lax.ppermute(block, axis, route))  18.3 us
    unnamed x69, local copies, waits for them, and re-layouts  13.1 us
  transfers between devices with their start and end apart: 6, of which 0 were waited for; matrix products, arithmetic and copies ran while one was open for 2% of the time, Pallas kernels for 0%

profile of v1, /device:TPU:256, one launch (start us, length us, event | category | flops | bytes accessed | tf_op | source)
XLA Modules:
  0.0 428.5 jit_solution(14037007713612233846)
XLA Ops:
  0.6 0.8 slice_bitcast_fusion.5
  1.4 0.6 copy-done.23
  2.0 1.5 fusion.24
  3.6 5.5 %collective-permute-start.2 = (bf16[16,1920]{1,0:T(8,128)(2,1)S(1)}, bf16[16,1920]{1,0:T(8,128)(2,1)S(1)}, u32[]{:S(2)}, u32[]{:S(2)}) collective-permute-start(bf16[16,1920]{1,0:T(8,128)(2,1)S(1)} %bitcast_dynamic-update-slice_fusion), channel_id=1, source_target_pairs={{0,12},{4,0},{8,4},{12,8},{16,28},{20,16},{24,20},{28,24},{32,44},... | collective-permute-start | bytes 184328 | tf_op jit(solution)/shard_map/ppermute | solution.py:24
  9.1 1.9 collective-permute-start.1
  11.0 2.9 collective-permute-start
  14.1 0.7 copy-done.1
  15.1 0.7 copy-done.2
  17.2 0.7 broadcast_in_dim.285
  17.9 0.6 broadcast_in_dim.278
  19.2 50.0 %all-gather = bf16[64,2,1920]{2,1,0:T(2,128)(2,1)S(1)} all-gather(bf16[1,2,1920]{2,1,0:T(2,128)(2,1)S(1)} %maximum_bitcast_fusion.1), channel_id=1, replica_groups=mesh['dp'=2,'ctx'=64,'head'=4] {'ctx'}, dimensions={0}, use_global_device_ids=true | all-gather | bytes 499200 | tf_op jit(solution)/shard_map/all_gather | solution.py:128
  71.0 0.7 broadcast_in_dim.289
  72.8 0.5 copy-done.9
  75.5 0.7 copy-done.13
  76.1 0.8 multiply_reduce_fusion
  76.9 0.7 copy-done.15
  78.0 0.6 negate_bitcast_fusion
  79.1 0.6 pad_maximum_fusion.2
  79.7 2.6 collective-permute-start.5
  82.3 3.1 collective-permute-start.4
  85.4 2.3 collective-permute-start.3
  88.7 49.2 %all-gather.1 = f32[64,2,645]{2,1,0:T(2,128)S(1)} all-gather(f32[1,2,645]{2,1,0:T(2,128)S(1)} %maximum_bitcast_fusion.2), channel_id=1, replica_groups=mesh['dp'=2,'ctx'=64,'head'=4] {'ctx'}, dimensions={0}, use_global_device_ids=true | all-gather | bytes 335400 | tf_op jit(solution)/shard_map/all_gather | solution.py:184
  138.2 0.7 slice.99
  141.7 0.8 copy.357
  143.2 277.9 %psum.7 = f32[640]{0:T(1024)} all-reduce(f32[640]{0:T(1024)S(1)} %bitcast.273), channel_id=1, replica_groups=mesh['dp'=2,'ctx'=64,'head'=4] {'dp','ctx'}, use_global_device_ids=true, to_apply=%region_22.23 | all-reduce | flops 640 | bytes 5120 | tf_op jit(solution)/shard_map/psum | solution.py:161
  421.1 0.9 pad_maximum_fusion.1
  422.1 0.8 maximum_bitcast_fusion
  423.0 0.5 copy-done.10
  424.1 0.6 copy-done.12
  425.1 0.8 copy.359
  426.4 0.8 copy.358
  427.7 0.8 copy.360
  (144 shorter events, 15.0 us)
Async XLA Ops:
  1.4 0.6 copy-start.23
  1.4 15.2 %copy-start.25 = (s32[5]{0:T(128)}, s32[5]{0:T(128)S(1)}, u32[]{:S(2)}) copy-start(s32[5]{0:T(128)S(1)} %get-tuple-element.62) | copy-start | bytes 64
  2.0 15.9 %copy-start.14 = (pred[8,5]{0,1:T(8,128)(4,1)}, pred[8,5]{0,1:T(8,128)(4,1)S(1)}, u32[]{:S(2)}) copy-start(pred[8,5]{0,1:T(8,128)(4,1)S(1)} %iota_compare_fusion.1) | copy-start | bytes 124
  2.0 11.9 %copy-start = (bf16[1,128,640]{2,1,0:T(8,128)(2,1)S(1)}, bf16[1,128,640]{2,1,0:T(8,128)(2,1)}, u32[]{:S(2)}) copy-start(bf16[1,128,640]{2,1,0:T(8,128)(2,1)} %param.6) | copy-start | bytes 491524
  3.6 68.8 %collective-permute-start.2 = (bf16[16,1920]{1,0:T(8,128)(2,1)S(1)}, bf16[16,1920]{1,0:T(8,128)(2,1)S(1)}, u32[]{:S(2)}, u32[]{:S(2)}) collective-permute-start(bf16[16,1920]{1,0:T(8,128)(2,1)S(1)} %bitcast_dynamic-update-slice_fusion), channel_id=1, source_target_pairs={{0,12},{4,0},{8,4},{12,8},{16,28},{20,16},{24,20},{28,24},{32,44},... | collective-permute-start | bytes 184328 | tf_op jit(solution)/shard_map/ppermute | solution.py:24
  9.1 63.3 %collective-permute-start.1 = (bf16[16,1920]{1,0:T(8,128)(2,1)S(1)}, bf16[16,1920]{1,0:T(8,128)(2,1)S(1)}, u32[]{:S(2)}, u32[]{:S(2)}) collective-permute-start(bf16[16,1920]{1,0:T(8,128)(2,1)S(1)} %bitcast_dynamic-update-slice_fusion), channel_id=1, source_target_pairs={{0,8},{4,12},{8,0},{12,4},{16,24},{20,28},{24,16},{28,20},{32,40},... | collective-permute-start | bytes 184328 | tf_op jit(solution)/shard_map/ppermute | solution.py:24
  11.0 61.3 %collective-permute-start = (bf16[16,1920]{1,0:T(8,128)(2,1)S(1)}, bf16[16,1920]{1,0:T(8,128)(2,1)S(1)}, u32[]{:S(2)}, u32[]{:S(2)}) collective-permute-start(bf16[16,1920]{1,0:T(8,128)(2,1)S(1)} %bitcast_dynamic-update-slice_fusion), channel_id=1, source_target_pairs={{0,4},{4,8},{8,12},{12,0},{16,20},{20,24},{24,28},{28,16},{32,36},... | collective-permute-start | bytes 184328 | tf_op jit(solution)/shard_map/ppermute | solution.py:24
  14.0 0.9 copy-start.1
  14.9 0.9 copy-start.2
  16.4 2.2 copy-start.6
  70.3 0.6 copy-start.7
  72.4 1.0 copy-start.4
  72.7 0.6 copy-start.9
  73.5 0.7 copy-start.19
  73.5 0.7 copy-start.26
  73.7 0.7 copy-start.18
  73.7 0.7 copy-start.11
  73.8 0.7 copy-start.24
  75.4 0.7 copy-start.13
  76.9 0.7 copy-start.15
  79.7 341.3 %collective-permute-start.5 = (f32[16,645]{1,0:T(8,128)}, f32[16,645]{1,0:T(8,128)}, u32[]{:S(2)}, u32[]{:S(2)}) collective-permute-start(f32[16,645]{1,0:T(8,128)} %pad_maximum_fusion.2), channel_id=1, source_target_pairs={{0,12},{4,0},{8,4},{12,8},{16,28},{20,16},{24,20},{28,24},{32,44},... | collective-permute-start | bytes 123848 | tf_op jit(solution)/shard_map/ppermute | solution.py:24
  82.3 338.8 %collective-permute-start.4 = (f32[16,645]{1,0:T(8,128)}, f32[16,645]{1,0:T(8,128)}, u32[]{:S(2)}, u32[]{:S(2)}) collective-permute-start(f32[16,645]{1,0:T(8,128)} %pad_maximum_fusion.2), channel_id=1, source_target_pairs={{0,8},{4,12},{8,0},{12,4},{16,24},{20,28},{24,16},{28,20},{32,40},... | collective-permute-start | bytes 123848 | tf_op jit(solution)/shard_map/ppermute | solution.py:24
  85.4 335.7 %collective-permute-start.3 = (f32[16,645]{1,0:T(8,128)}, f32[16,645]{1,0:T(8,128)}, u32[]{:S(2)}, u32[]{:S(2)}) collective-permute-start(f32[16,645]{1,0:T(8,128)} %pad_maximum_fusion.2), channel_id=1, source_target_pairs={{0,4},{4,8},{8,12},{12,0},{16,20},{20,24},{24,28},{28,16},{32,36},... | collective-permute-start | bytes 123848 | tf_op jit(solution)/shard_map/ppermute | solution.py:24
  87.7 0.6 copy-start.22
  138.2 0.7 copy-start.16
  138.9 0.9 copy-start.3
  140.0 0.7 copy-start.8
  141.7 0.8 copy-start.20
  142.5 0.7 copy-start.17
  422.1 0.9 copy-start.5
  422.8 0.7 copy-start.10
  424.1 0.6 copy-start.12
  (1 other events, 0.5 us)

commit v2 on v1

--- a/solution.py
+++ b/solution.py
@@ -158,7 +158,6 @@
     attended = (normed * gain_rows).astype(jnp.bfloat16).reshape(1, tokens, flat_width)
     grad_full = grad_y[0].reshape(row_shape).astype(jnp.float32)
     gain_part = jnp.sum(grad_full * normed, axis=0).reshape(flat_width)
-    gain_grad = lax.psum(gain_part, ("dp", "ctx"))
     grad_norm = grad_full * gain_rows
     grad_attn = inv_rms * (
         grad_norm - normed * jnp.mean(grad_norm * normed, axis=-1, keepdims=True)
@@ -180,9 +179,13 @@
     mid_low_all, mid_shift_all = unpack_grads(
         group_gather(pack_grads(mid_low, mid_row_shift), "ctx", SPAN), head_count
     )
+    top_grads = pack_grads(top_low, top_row_shift)
+    gain_row = jnp.pad(gain_part, (0, top_grads.shape[1] - flat_width))[None]
+    gathered = lax.all_gather(jnp.concatenate([top_grads, gain_row], 0), "ctx", axis=0)
     top_low_all, top_shift_all = unpack_grads(
-        lax.all_gather(pack_grads(top_low, top_row_shift), "ctx", axis=0, tiled=True), head_count
-    )
+        gathered[:, :top_rows].reshape(-1, top_grads.shape[1]), head_count
+    )
+    gain_grad = lax.psum(jnp.sum(gathered[:, top_rows, :flat_width], axis=0), "dp")
 
     mid_grad, mid_soft = score_grads(
         mid_q, mid_k, mid_v, mid_total_all, mid_low_all, mid_shift_all

time: 429 us -> 160 us (0.37)
  the two profiles are of different devices: /device:TPU:256 before, /device:TPU:1 now
where the time goes in v2:
time: 160 us
  blocking collectives  111 us (69%)
  starting transfers between devices  19 us (12%)
  local copies, waits for them, and re-layouts  15.2 us (10%)
  other arithmetic  7.09 us (4%)
  matrix products  6.04 us (4%)
    all_gather x1, blocking collectives, shards(): top_all = lax.all_gather(top_pack, 'ctx', axis=0, tiled=True)  44.2 us
    all_gather x1, blocking collectives, shards(): lax.all_gather(jnp.concatenate([top_grads, gain_row], 0), 'ctx', axis=0)  38.9 us
    psum x1, blocking collectives, shards(): lax.psum(jnp.sum(gathered[:, top_rows, :flat_width], axis=0), 'dp')  28 us
    ppermute x6, starting transfers between devices, group_gather(): pieces.append(lax.ppermute(block, axis, route))  19 us
    unnamed x34, local copies, waits for them, and re-layouts  7.85 us
  transfers between devices with their start and end apart: 6, of which 0 were waited for; matrix products, arithmetic and copies ran while one was open for 7% of the time, Pallas kernels for 0%

profile of v2, /device:TPU:1, one launch (start us, length us, event | category | flops | bytes accessed | tf_op | source)
XLA Modules:
  0.0 159.5 jit_solution(9887099655481750333)
XLA Ops:
  0.6 0.8 slice_bitcast_fusion.5
  1.5 1.5 fusion.24
  3.0 6.1 %collective-permute-start.2 = (bf16[16,1920]{1,0:T(8,128)(2,1)S(1)}, bf16[16,1920]{1,0:T(8,128)(2,1)S(1)}, u32[]{:S(2)}, u32[]{:S(2)}) collective-permute-start(bf16[16,1920]{1,0:T(8,128)(2,1)S(1)} %bitcast_dynamic-update-slice_fusion), channel_id=1, source_target_pairs={{0,12},{4,0},{8,4},{12,8},{16,28},{20,16},{24,20},{28,24},{32,44},... | collective-permute-start | bytes 184328 | tf_op jit(solution)/shard_map/ppermute | solution.py:24
  9.1 1.9 %collective-permute-start.1 = (bf16[16,1920]{1,0:T(8,128)(2,1)S(1)}, bf16[16,1920]{1,0:T(8,128)(2,1)S(1)}, u32[]{:S(2)}, u32[]{:S(2)}) collective-permute-start(bf16[16,1920]{1,0:T(8,128)(2,1)S(1)} %bitcast_dynamic-update-slice_fusion), channel_id=1, source_target_pairs={{0,8},{4,12},{8,0},{12,4},{16,24},{20,28},{24,16},{28,20},{32,40},... | collective-permute-start | bytes 184328 | tf_op jit(solution)/shard_map/ppermute | solution.py:24
  11.0 2.3 %collective-permute-start = (bf16[16,1920]{1,0:T(8,128)(2,1)S(1)}, bf16[16,1920]{1,0:T(8,128)(2,1)S(1)}, u32[]{:S(2)}, u32[]{:S(2)}) collective-permute-start(bf16[16,1920]{1,0:T(8,128)(2,1)S(1)} %bitcast_dynamic-update-slice_fusion), channel_id=1, source_target_pairs={{0,4},{4,8},{8,12},{12,0},{16,20},{20,24},{24,28},{28,16},{32,36},... | collective-permute-start | bytes 184328 | tf_op jit(solution)/shard_map/ppermute | solution.py:24
  13.6 0.7 copy-done.1
  14.5 0.7 copy-done.2
  16.4 0.3 copy-done.8
  17.4 44.2 %all-gather.1 = bf16[64,2,1920]{2,1,0:T(2,128)(2,1)S(1)} all-gather(bf16[1,2,1920]{2,1,0:T(2,128)(2,1)S(1)} %maximum_bitcast_fusion.2), channel_id=1, replica_groups=mesh['dp'=2,'ctx'=64,'head'=4] {'ctx'}, dimensions={0}, use_global_device_ids=true | all-gather | bytes 499200 | tf_op jit(solution)/shard_map/all_gather | solution.py:128
  65.3 0.5 multiply_reduce_fusion.3
  65.8 0.7 copy-done.9
  66.5 0.8 multiply_reduce_fusion.2
  68.2 0.6 pad_maximum_fusion.2
  68.9 3.9 %collective-permute-start.5 = (f32[16,645]{1,0:T(8,128)}, f32[16,645]{1,0:T(8,128)}, u32[]{:S(2)}, u32[]{:S(2)}) collective-permute-start(f32[16,645]{1,0:T(8,128)} %pad_maximum_fusion.2), channel_id=1, source_target_pairs={{0,12},{4,0},{8,4},{12,8},{16,28},{20,16},{24,20},{28,24},{32,44},... | collective-permute-start | bytes 123848 | tf_op jit(solution)/shard_map/ppermute | solution.py:24
  72.8 2.8 %collective-permute-start.4 = (f32[16,645]{1,0:T(8,128)}, f32[16,645]{1,0:T(8,128)}, u32[]{:S(2)}, u32[]{:S(2)}) collective-permute-start(f32[16,645]{1,0:T(8,128)} %pad_maximum_fusion.2), channel_id=1, source_target_pairs={{0,8},{4,12},{8,0},{12,4},{16,24},{20,28},{24,16},{28,20},{32,40},... | collective-permute-start | bytes 123848 | tf_op jit(solution)/shard_map/ppermute | solution.py:24
  75.6 1.9 %collective-permute-start.3 = (f32[16,645]{1,0:T(8,128)}, f32[16,645]{1,0:T(8,128)}, u32[]{:S(2)}, u32[]{:S(2)}) collective-permute-start(f32[16,645]{1,0:T(8,128)} %pad_maximum_fusion.2), channel_id=1, source_target_pairs={{0,4},{4,8},{8,12},{12,0},{16,20},{20,24},{24,28},{28,16},{32,36},... | collective-permute-start | bytes 123848 | tf_op jit(solution)/shard_map/ppermute | solution.py:24
  78.2 38.9 %all-gather.2 = f32[64,3,645]{2,1,0:T(4,128)S(1)} all-gather(f32[1,3,645]{2,1,0:T(4,128)S(1)} %maximum_bitcast_fusion.1), channel_id=2, replica_groups=mesh['dp'=2,'ctx'=64,'head'=4] {'ctx'}, dimensions={0}, use_global_device_ids=true | all-gather | bytes 503100 | tf_op jit(solution)/shard_map/all_gather | solution.py:184
  117.2 1.0 reshape.365
  118.2 0.8 slice_bitcast_fusion.3
  119.1 1.0 slice.110
  120.3 0.9 convolution_bitcast_fusion.9
  121.7 0.4 convolution_bitcast_fusion.8
  122.1 0.4 fusion.17
  122.7 0.7 copy-done.4
  123.5 0.8 copy.357
  124.5 28.0 %psum.7 = f32[640]{0:T(1024)} all-reduce(f32[640]{0:T(1024)S(1)} %slice_reduce_fusion), channel_id=1, replica_groups=mesh['dp'=2,'ctx'=64,'head'=4] {'dp'}, use_global_device_ids=true, to_apply=%region_23.24 | all-reduce | flops 640 | bytes 5120 | tf_op jit(solution)/shard_map/psum | solution.py:188
  152.5 0.9 pad_maximum_fusion.1
  153.4 0.9 convolution_bitcast_fusion.5
  154.2 0.8 maximum_bitcast_fusion
  156.1 0.8 copy.359
  157.4 0.8 copy.358
  158.7 0.8 copy.360
  (114 shorter events, 10.7 us)
Async XLA Ops:
  1.5 11.9 %copy-start = (bf16[1,128,640]{2,1,0:T(8,128)(2,1)S(1)}, bf16[1,128,640]{2,1,0:T(8,128)(2,1)}, u32[]{:S(2)}) copy-start(bf16[1,128,640]{2,1,0:T(8,128)(2,1)} %param.6) | copy-start | bytes 491524
  3.0 60.7 %collective-permute-start.2 = (bf16[16,1920]{1,0:T(8,128)(2,1)S(1)}, bf16[16,1920]{1,0:T(8,128)(2,1)S(1)}, u32[]{:S(2)}, u32[]{:S(2)}) collective-permute-start(bf16[16,1920]{1,0:T(8,128)(2,1)S(1)} %bitcast_dynamic-update-slice_fusion), channel_id=1, source_target_pairs={{0,12},{4,0},{8,4},{12,8},{16,28},{20,16},{24,20},{28,24},{32,44},... | collective-permute-start | bytes 184328 | tf_op jit(solution)/shard_map/ppermute | solution.py:24
  9.1 54.7 %collective-permute-start.1 = (bf16[16,1920]{1,0:T(8,128)(2,1)S(1)}, bf16[16,1920]{1,0:T(8,128)(2,1)S(1)}, u32[]{:S(2)}, u32[]{:S(2)}) collective-permute-start(bf16[16,1920]{1,0:T(8,128)(2,1)S(1)} %bitcast_dynamic-update-slice_fusion), channel_id=1, source_target_pairs={{0,8},{4,12},{8,0},{12,4},{16,24},{20,28},{24,16},{28,20},{32,40},... | collective-permute-start | bytes 184328 | tf_op jit(solution)/shard_map/ppermute | solution.py:24
  11.0 52.7 %collective-permute-start = (bf16[16,1920]{1,0:T(8,128)(2,1)S(1)}, bf16[16,1920]{1,0:T(8,128)(2,1)S(1)}, u32[]{:S(2)}, u32[]{:S(2)}) collective-permute-start(bf16[16,1920]{1,0:T(8,128)(2,1)S(1)} %bitcast_dynamic-update-slice_fusion), channel_id=1, source_target_pairs={{0,4},{4,8},{8,12},{12,0},{16,20},{20,24},{24,28},{28,16},{32,36},... | collective-permute-start | bytes 184328 | tf_op jit(solution)/shard_map/ppermute | solution.py:24
  13.4 0.9 copy-start.1
  14.3 0.9 copy-start.2
  15.8 0.9 copy-start.8
  62.7 0.7 copy-start.3
  63.8 0.6 copy-start.6
  64.1 0.6 copy-start.5
  65.8 0.7 copy-start.9
  68.9 83.7 %collective-permute-start.5 = (f32[16,645]{1,0:T(8,128)}, f32[16,645]{1,0:T(8,128)}, u32[]{:S(2)}, u32[]{:S(2)}) collective-permute-start(f32[16,645]{1,0:T(8,128)} %pad_maximum_fusion.2), channel_id=1, source_target_pairs={{0,12},{4,0},{8,4},{12,8},{16,28},{20,16},{24,20},{28,24},{32,44},... | collective-permute-start | bytes 123848 | tf_op jit(solution)/shard_map/ppermute | solution.py:24
  72.8 79.7 %collective-permute-start.4 = (f32[16,645]{1,0:T(8,128)}, f32[16,645]{1,0:T(8,128)}, u32[]{:S(2)}, u32[]{:S(2)}) collective-permute-start(f32[16,645]{1,0:T(8,128)} %pad_maximum_fusion.2), channel_id=1, source_target_pairs={{0,8},{4,12},{8,0},{12,4},{16,24},{20,28},{24,16},{28,20},{32,40},... | collective-permute-start | bytes 123848 | tf_op jit(solution)/shard_map/ppermute | solution.py:24
  75.6 76.9 %collective-permute-start.3 = (f32[16,645]{1,0:T(8,128)}, f32[16,645]{1,0:T(8,128)}, u32[]{:S(2)}, u32[]{:S(2)}) collective-permute-start(f32[16,645]{1,0:T(8,128)} %pad_maximum_fusion.2), channel_id=1, source_target_pairs={{0,4},{4,8},{8,12},{12,0},{16,20},{20,24},{24,28},{28,16},{32,36},... | collective-permute-start | bytes 123848 | tf_op jit(solution)/shard_map/ppermute | solution.py:24
  122.4 0.9 copy-start.4
  154.2 1.0 copy-start.7

commit v3 on v2

--- a/solution.py
+++ b/solution.py
@@ -1,8 +1,11 @@
+import functools
 import math
 
 import jax
 import jax.numpy as jnp
 from jax import lax
+from jax.experimental import pallas as pl
+from jax.experimental.pallas import tpu as pltpu
 from jax.sharding import PartitionSpec as P
 
 HEAD_DIM = 128
@@ -13,16 +16,76 @@
 EPS = 1e-06
 
 
-def group_gather(block, axis, group):
-    count = lax.axis_size(axis)
-    pieces = [block]
-    for shift in range(1, group):
-        route = []
-        for src in range(count):
-            base = src - src % group
-            route.append((src, base + (src % group + shift) % group))
-        pieces.append(lax.ppermute(block, axis, route))
-    return jnp.concatenate(pieces, 0)
+def gather_kernel(group, mid_x, top_x, mid_out, top_out, send_mid, recv_mid, send_top, recv_top):
+    count = lax.axis_size("ctx")
+    me = lax.axis_index("ctx")
+    row = lax.axis_index("dp")
+    col = lax.axis_index("head")
+    base = me - me % group
+    barrier = pltpu.get_barrier_semaphore()
+
+    def greet(j, carry):
+        peer = lax.rem(me + j, count)
+        pl.semaphore_signal(
+            barrier, 1, device_id=(row, peer, col), device_id_type=pl.DeviceIdType.MESH
+        )
+        return carry
+
+    lax.fori_loop(1, count, greet, 0)
+    pl.semaphore_wait(barrier, count - 1)
+
+    def mid_copy(j):
+        peer = base + lax.rem(me % group + j, group)
+        return pltpu.make_async_remote_copy(
+            mid_x, mid_out.at[j], send_mid.at[j], recv_mid.at[j],
+            device_id=(row, peer, col), device_id_type=pl.DeviceIdType.MESH,
+        )
+
+    def top_copy(j):
+        peer = lax.rem(me + j, count)
+        return pltpu.make_async_remote_copy(
+            top_x, top_out.at[j], send_top.at[j], recv_top.at[j],
+            device_id=(row, peer, col), device_id_type=pl.DeviceIdType.MESH,
+        )
+
+    for j in range(1, group):
+        mid_copy(j).start()
+
+    def start_top(j, carry):
+        top_copy(j).start()
+        return carry
+
+    lax.fori_loop(1, count, start_top, 0)
+    mid_out[0] = mid_x[...]
+    top_out[0] = top_x[...]
+    for j in range(1, group):
+        mid_copy(j).wait()
+
+    def wait_top(j, carry):
+        top_copy(j).wait()
+        return carry
+
+    lax.fori_loop(1, count, wait_top, 0)
+
+
+def ctx_gather(mid_x, top_x, group, tag):
+    count = lax.axis_size("ctx")
+    return pl.pallas_call(
+        functools.partial(gather_kernel, group),
+        out_shape=(
+            jax.ShapeDtypeStruct((group,) + mid_x.shape, mid_x.dtype),
+            jax.ShapeDtypeStruct((count,) + top_x.shape, top_x.dtype),
+        ),
+        in_specs=[pl.BlockSpec(memory_space=pltpu.VMEM)] * 2,
+        out_specs=(pl.BlockSpec(memory_space=pltpu.VMEM),) * 2,
+        scratch_shapes=[
+            pltpu.SemaphoreType.DMA((group,)),
+            pltpu.SemaphoreType.DMA((group,)),
+            pltpu.SemaphoreType.DMA((count,)),
+            pltpu.SemaphoreType.DMA((count,)),
+        ],
+        compiler_params=pltpu.CompilerParams(collective_id=tag, has_side_effects=True),
+    )(mid_x, top_x)
 
 
 def pick_rows(source_rows, dilation, shifts):
@@ -89,15 +152,16 @@
 
 def pack_grads(grad_low, row_shift):
     rows = grad_low.shape[0]
+    pad = jnp.zeros((rows, HEAD_DIM - row_shift.shape[1]), jnp.float32)
     return jnp.concatenate(
-        [grad_low.astype(jnp.float32).reshape(rows, -1), row_shift.astype(jnp.float32)], 1
+        [grad_low.astype(jnp.float32).reshape(rows, -1), row_shift.astype(jnp.float32), pad], 1
     )
 
 
 def unpack_grads(packed, head_count):
     width = head_count * HEAD_DIM
     grad_low = packed[:, :width].astype(jnp.bfloat16).reshape(-1, head_count, HEAD_DIM)
-    return grad_low, packed[:, width:]
+    return grad_low, packed[:, width : width + head_count]
 
 
 def shards(queries, keys, values, grad_y, out_gain, offsets):
@@ -109,7 +173,6 @@
     k_own = keys[0].reshape(row_shape)
     v_own = values[0].reshape(row_shape)
     ctx_size = lax.axis_size("ctx")
-    my_place = lax.axis_index("ctx")
     mid_shift = offsets[0]
     top_shift = offsets[1]
     positions = jnp.arange(tokens, dtype=jnp.int32)
@@ -124,18 +187,18 @@
     )
     mid_rows = mid_pack.shape[0]
     top_rows = top_pack.shape[0]
-    mid_all = group_gather(mid_pack, "ctx", SPAN)
-    top_all = lax.all_gather(top_pack, "ctx", axis=0, tiled=True)
+    mid_all, top_all = ctx_gather(mid_pack, top_pack, SPAN, 0)
+    mid_all = mid_all.reshape(-1, mid_pack.shape[1])
+    top_all = top_all.reshape(-1, top_pack.shape[1])
     mid_q, mid_k, mid_v = split_qkv(mid_all, head_count)
     top_q, top_k, top_v = split_qkv(top_all, head_count)
-    top_start = my_place * top_rows
     base_out, base_total = attend(q_own, k_own, v_own)
     mid_out_all, mid_total_all = attend(mid_q, mid_k, mid_v)
     top_out_all, top_total_all = attend(top_q, top_k, top_v)
     mid_out = mid_out_all[:mid_rows]
     mid_total = mid_total_all[:mid_rows]
-    top_out = lax.dynamic_slice_in_dim(top_out_all, top_start, top_rows, 0)
-    top_total = lax.dynamic_slice_in_dim(top_total_all, top_start, top_rows, 0)
+    top_out = top_out_all[:top_rows]
+    top_total = top_total_all[:top_rows]
     mid_full = place_rows(mid_total[..., None], R1, mid_shift)[..., 0]
     top_full = place_rows(top_total[..., None], ctx_size, top_shift)[..., 0]
     row_max = jnp.maximum(base_total, jnp.where(mid_hit, mid_full, base_total))
@@ -176,12 +239,14 @@
     top_low = (top_sel[..., None] * pick_rows(grad_attn, ctx_size, top_shift)).astype(jnp.bfloat16)
     top_row_shift = -(top_sel * pick_rows(inner[..., None], ctx_size, top_shift)[..., 0])
 
-    mid_low_all, mid_shift_all = unpack_grads(
-        group_gather(pack_grads(mid_low, mid_row_shift), "ctx", SPAN), head_count
-    )
     top_grads = pack_grads(top_low, top_row_shift)
     gain_row = jnp.pad(gain_part, (0, top_grads.shape[1] - flat_width))[None]
-    gathered = lax.all_gather(jnp.concatenate([top_grads, gain_row], 0), "ctx", axis=0)
+    mid_gathered, gathered = ctx_gather(
+        pack_grads(mid_low, mid_row_shift), jnp.concatenate([top_grads, gain_row], 0), SPAN, 1
+    )
+    mid_low_all, mid_shift_all = unpack_grads(
+        mid_gathered.reshape(-1, mid_gathered.shape[-1]), head_count
+    )
     top_low_all, top_shift_all = unpack_grads(
         gathered[:, :top_rows].reshape(-1, top_grads.shape[1]), head_count
     )
@@ -197,11 +262,10 @@
     top_grad, top_soft = score_grads(
         top_q, top_k, top_v, top_total_all, top_low_all, top_shift_all
     )
-    own_grad = lax.dynamic_slice_in_dim(top_grad, top_start, top_rows, 1)
-    top_dq = query_part(own_grad, top_k)
-    key_grad_cols = lax.dynamic_slice_in_dim(top_grad, top_start, top_rows, 2)
-    key_soft_cols = lax.dynamic_slice_in_dim(top_soft, top_start, top_rows, 2)
-    top_dk, top_dv = key_parts(key_grad_cols, key_soft_cols, top_q, top_low_all)
+    top_dq = query_part(top_grad[:, :top_rows], top_k)
+    top_dk, top_dv = key_parts(
+        top_grad[:, :, :top_rows], top_soft[:, :, :top_rows], top_q, top_low_all
+    )
     query_grad = (
         base_dq + place_rows(mid_dq, R1, mid_shift) + place_rows(top_dq, ctx_size, top_shift)
     )

time: 160 us -> 107 us (0.67)
  blocking collectives: 111 us -> 5.75 us
  Pallas kernels: 0 us -> 67.5 us
  starting transfers between devices: 19 us -> 0 us
    all_gather x2 -> x0, blocking collectives: 83.1 us -> none  [the longest x1 44.2 us: shards(): top_all = lax.all_gather(top_pack, 'ctx', axis=0, tiled=True)]
    pallas_call x0 -> x2, Pallas kernels: none -> 67.5 us  [ctx_gather(): pl.pallas_call(functools.partial(gather_kernel, group), out_shape=(jax.Sh...]
    psum x1, blocking collectives: 28 us -> 5.75 us  [shards(): lax.psum(jnp.sum(gathered[:, top_rows, :flat_width], axis=0), 'dp')]
    ppermute x6 -> x0, starting transfers between devices: 19 us -> none  [group_gather(): pieces.append(lax.ppermute(block, axis, route))]
    unnamed x34 -> x33, local copies, waits for them, and re-layouts: 7.85 us -> 11.1 us
  transfers between devices with their start and end apart: 6 -> 0, of which waited for: 0 -> 0; matrix products, arithmetic and copies ran while one was open for 7% -> 0% of each run, Pallas kernels for 0% -> 0%
where the time goes in v3:
time: 107 us; the launch traced here: 106 us
  Pallas kernels  67.5 us (63%)
  local copies, waits for them, and re-layouts  16.6 us (16%)
  other arithmetic  7.91 us (7%)
  matrix products  7.55 us (7%)
  blocking collectives  5.75 us (5%)
    pallas_call x2, Pallas kernels, ctx_gather(): pl.pallas_call(functools.partial(gather_kernel, group), out_shape=(jax.Sh...  67.5 us
    unnamed x33, local copies, waits for them, and re-layouts  11.1 us
    psum x1, blocking collectives, shards(): lax.psum(jnp.sum(gathered[:, top_rows, :flat_width], axis=0), 'dp')  5.75 us
    reduce_sum x6, other arithmetic, pick_rows(): return jnp.sum(chosen, axis=1, dtype=source_rows.dtype)  2.46 us

profile of v3, /device:TPU:1, one launch (start us, length us, event | category | flops | bytes accessed | tf_op | source)
XLA Modules:
  0.0 106.4 jit_solution(14136185313748533293)
XLA Ops:
  0.6 0.7 copy-done.8
  1.9 1.5 %fusion.30 = (bf16[16,5,128]{2,0,1:T(8,128)(2,1)S(1)}, bf16[16,5,128]{2,0,1:T(8,128)(2,1)S(1)}, bf16[16,5,128]{2,0,1:T(8,128)(2,1)S(1)}) fusion(pred[8,5]{0,1:T(8,128)(4,1)S(1)} %iota_compare_fusion.1, bf16[1,128,640]{2,1,0:T(8,128)(2,1)} %param.8, bf16[1,128,640]{2,1,0:T(8,128)(2,1)} %param.7, bf16[1,128,640]{2,1,0:T(8,128)(2,1)} %param.6), kind=kLoop, calls=%fused_computation.76 | loop fusion | flops 460800 | bytes 553000 | tf_op jit(solution)/shard_map/reduce_sum | solution.py:98
  3.4 0.6 pad_maximum_fusion.mid_x
  4.6 0.8 copy-done
  5.6 0.7 copy-done.1
  6.5 0.7 copy-done.2
  8.3 0.6 pad_maximum_fusion.2.top_x
  9.3 36.0 %shard_map.101 = (bf16[4,16,1920]{2,1,0:T(8,128)(2,1)}, bf16[64,2,1920]{2,1,0:T(2,128)(2,1)}) custom-call(bf16[16,1920]{1,0:T(8,128)(2,1)} %pad_maximum_fusion.mid_x, bf16[2,1920]{1,0:T(2,128)(2,1)} %pad_maximum_fusion.2.top_x), custom_call_target="tpu_custom_call" | custom-call | tf_op jit(solution)/shard_map/pallas_call | solution.py:73
  45.3 1.0 slice_bitcast_fusion
  47.0 0.5 copy-done.3
  49.6 0.5 multiply_reduce_fusion.3
  50.1 0.7 copy-done.7
  50.8 0.3 multiply_reduce_fusion
  51.8 0.4 fusion.17
  52.7 0.7 pad_maximum_fusion.1.top_x
  53.7 0.6 maximum_maximum_fusion.mid_x
  54.5 0.8 copy.235
  55.3 31.5 %shard_map.102 = (f32[4,16,768]{2,1,0:T(8,128)}, f32[64,3,768]{2,1,0:T(4,128)}) custom-call(f32[16,768]{1,0:T(8,128)} %maximum_maximum_fusion.mid_x, f32[3,768]{1,0:T(4,128)} %pad_maximum_fusion.1.top_x), custom_call_target="tpu_custom_call" | custom-call | tf_op jit(solution)/shard_map/pallas_call | solution.py:73
  86.9 1.1 convolution_bitcast_fusion.6
  87.9 1.3 %slice_reduce_fusion = f32[640]{0:T(1024)S(1)} fusion(f32[64,3,768]{2,1,0:T(4,128)} %get-tuple-element.12), kind=kLoop, calls=%fused_computation.77 | loop fusion | flops 40320 | bytes 166400 | tf_op jit(solution)/shard_map/reduce_sum | solution.py:253
  89.2 1.3 %slice.89 = f32[64,2,768]{2,1,0:T(2,128)S(1)} slice(f32[64,3,768]{2,1,0:T(4,128)} %get-tuple-element.12), slice={[0:64], [0:2], [0:768]} | slice | bytes 786432 | tf_op jit(solution)/shard_map/slice | solution.py:251
  90.8 5.7 %psum.7 = f32[640]{0:T(1024)} all-reduce(f32[640]{0:T(1024)S(1)} %slice_reduce_fusion), channel_id=1, replica_groups=mesh['dp'=2,'ctx'=64,'head'=4] {'dp'}, use_global_device_ids=true, to_apply=%region_23.24 | all-reduce | flops 640 | bytes 5120 | tf_op jit(solution)/shard_map/psum | solution.py:253
  96.5 0.8 slice_bitcast_fusion.4
  97.4 1.1 %fusion.20 = bf16[5,64,64]{1,2,0:T(8,128)(2,1)S(1)} fusion(f32[5,64,64]{1,2,0:T(8,128)S(1)} %get-tuple-element.64, f32[5,64]{1,0:T(8,128)S(1)} %copy.212, f32[5,64]{1,0:T(8,128)S(1)} %log_add_fusion.1, bf16[8,5,8,128]{3,2,1,0:T(8,128)(2,1)S(1)} %get-tuple-element.51, f32[64,768]{1,0:T(8,128)} %bitcast.262), kind=kOutput, calls=%fused_computation.32 | convolution fusion | flops 5345280 | bytes 289280 | tf_op jit(solution)/shard_map/qhe,khe->hqk/dot_general | solution.py:130
  98.5 0.8 convolution_bitcast_fusion.7
  99.2 0.8 convolution_bitcast_fusion.8
  101.5 0.6 copy-done.6
  102.5 0.8 copy.237
  103.3 0.3 fusion.15
  103.6 0.5 copy-done.5
  104.6 0.8 copy.236
  105.5 0.8 copy.238
  (101 shorter events, 10.0 us)
Async XLA Ops:
  0.6 0.7 copy-start.8
  3.4 0.9 copy-start.4
  4.5 0.9 copy-start
  5.4 0.9 copy-start.1
  6.3 0.9 copy-start.2
  46.5 1.0 copy-start.3
  50.1 0.7 copy-start.7
  101.3 0.8 copy-start.6
  103.3 0.8 copy-start.5

commit v4 on v3

--- a/solution.py
+++ b/solution.py
@@ -88,6 +88,10 @@
     )(mid_x, top_x)
 
 
+def lane_dense(block):
+    return block.reshape(-1, HEAD_DIM)
+
+
 def pick_rows(source_rows, dilation, shifts):
     row_count, head_count, head_width = source_rows.shape
     grouped = source_rows.reshape(row_count // dilation, dilation, head_count, head_width)
@@ -187,7 +191,7 @@
     )
     mid_rows = mid_pack.shape[0]
     top_rows = top_pack.shape[0]
-    mid_all, top_all = ctx_gather(mid_pack, top_pack, SPAN, 0)
+    mid_all, top_all = ctx_gather(mid_pack, lane_dense(top_pack), SPAN, 0)
     mid_all = mid_all.reshape(-1, mid_pack.shape[1])
     top_all = top_all.reshape(-1, top_pack.shape[1])
     mid_q, mid_k, mid_v = split_qkv(mid_all, head_count)
@@ -241,9 +245,11 @@
 
     top_grads = pack_grads(top_low, top_row_shift)
     gain_row = jnp.pad(gain_part, (0, top_grads.shape[1] - flat_width))[None]
+    top_block = jnp.concatenate([top_grads, gain_row], 0)
     mid_gathered, gathered = ctx_gather(
-        pack_grads(mid_low, mid_row_shift), jnp.concatenate([top_grads, gain_row], 0), SPAN, 1
-    )
+        pack_grads(mid_low, mid_row_shift), lane_dense(top_block), SPAN, 1
+    )
+    gathered = gathered.reshape((-1,) + top_block.shape)
     mid_low_all, mid_shift_all = unpack_grads(
         mid_gathered.reshape(-1, mid_gathered.shape[-1]), head_count
     )

time: 107 us -> 99.4 us (0.929)
  Pallas kernels: 67.5 us -> 64 us
  other arithmetic: 7.91 us -> 5.62 us
  matrix products: 7.55 us -> 5.47 us
    pallas_call x2, Pallas kernels: 67.5 us -> 64 us  [ctx_gather(): pl.pallas_call(functools.partial(gather_kernel, group), out_shape=(jax.Sh...]
    reshape x0 -> x3, local copies, waits for them, and re-layouts: none -> 2.66 us  [the longest x1 1.42 us: shards(): gathered = gathered.reshape((-1,) + top_block.shape)]
    unnamed x33 -> x29, local copies, waits for them, and re-layouts: 11.1 us -> 9.62 us
    slice x1, local copies, waits for them, and re-layouts: 1.27 us -> 0.14 us  [shards(): gathered[:, :top_rows].reshape(-1, top_grads.shape[1])]
    reduce_sum x1, other arithmetic: 1.31 us -> 0.21 us  [shards(): jnp.sum(gathered[:, top_rows, :flat_width], axis=0)]
where the time goes in v4:
time: 99.4 us; the launch traced here: 98.9 us
  Pallas kernels  64 us (64%)
  local copies, waits for them, and re-layouts  16.6 us (17%)
  blocking collectives  6.04 us (6%)
  other arithmetic  5.62 us (6%)
  matrix products  5.47 us (6%)
  between operations  1.09 us (1%)
    pallas_call x2, Pallas kernels, ctx_gather(): pl.pallas_call(functools.partial(gather_kernel, group), out_shape=(jax.Sh...  64 us
    unnamed x29, local copies, waits for them, and re-layouts  9.62 us
    psum x1, blocking collectives, shards(): lax.psum(jnp.sum(gathered[:, top_rows, :flat_width], axis=0), 'dp')  6.04 us
    reduce_sum x6, other arithmetic, pick_rows(): return jnp.sum(chosen, axis=1, dtype=source_rows.dtype)  2.47 us

profile of v4, /device:TPU:1, one launch (start us, length us, event | category | flops | bytes accessed | tf_op | source)
XLA Modules:
  0.0 98.9 jit_solution(862378589971694878)
XLA Ops:
  0.6 0.7 copy-done.7
  1.9 1.5 %fusion.30 = (bf16[16,5,128]{2,0,1:T(8,128)(2,1)S(1)}, bf16[16,5,128]{2,0,1:T(8,128)(2,1)S(1)}, bf16[16,5,128]{2,0,1:T(8,128)(2,1)S(1)}) fusion(pred[8,5]{0,1:T(8,128)(4,1)S(1)} %iota_compare_fusion.1, bf16[1,128,640]{2,1,0:T(8,128)(2,1)} %param.8, bf16[1,128,640]{2,1,0:T(8,128)(2,1)} %param.7, bf16[1,128,640]{2,1,0:T(8,128)(2,1)} %param.6), kind=kLoop, calls=%fused_computation.77 | loop fusion | flops 460800 | bytes 553000 | tf_op jit(solution)/shard_map/reduce_sum | solution.py:102
  3.4 0.6 pad_maximum_fusion.mid_x
  4.0 0.3 copy-done.5
  4.6 0.8 copy-done
  5.6 0.7 copy-done.1
  6.5 0.7 copy-done.2
  8.0 0.3 select_reduce_fusion.2
  8.3 0.6 reshape.372.top_x
  9.0 0.3 fusion.66
  9.3 36.6 %shard_map.101 = (bf16[4,16,1920]{2,1,0:T(8,128)(2,1)}, bf16[64,30,128]{2,1,0:T(8,128)(2,1)}) custom-call(bf16[16,1920]{1,0:T(8,128)(2,1)} %pad_maximum_fusion.mid_x, bf16[30,128]{1,0:T(8,128)(2,1)} %reshape.372.top_x), custom_call_target="tpu_custom_call" | custom-call | tf_op jit(solution)/shard_map/pallas_call | solution.py:73
  45.9 1.0 %slice_bitcast_fusion = (bf16[8,5,8,128]{3,2,1,0:T(8,128)(2,1)S(1)}, bf16[8,5,8,128]{3,2,1,0:T(8,128)(2,1)S(1)}, bf16[8,5,8,128]{3,2,1,0:T(8,128)(2,1)S(1)}) fusion(bf16[64,1920]{1,0:T(8,128)(2,1)} %bitcast.267), kind=kLoop, calls=%fused_computation.91 | loop fusion | bytes 491520
  47.6 0.5 copy-done.4
  48.2 0.5 reshape.376
  49.3 0.3 fusion.64
  50.7 0.5 multiply_reduce_fusion.3
  51.2 0.7 copy-done.6
  51.9 0.3 multiply_reduce_fusion
  52.9 0.4 fusion.17
  53.8 0.6 reshape.385.top_x
  54.8 0.6 maximum_maximum_fusion.mid_x
  55.6 0.8 copy.233
  56.4 27.4 %shard_map.102 = (f32[4,16,768]{2,1,0:T(8,128)}, f32[64,18,128]{2,1,0:T(8,128)}) custom-call(f32[16,768]{1,0:T(8,128)} %maximum_maximum_fusion.mid_x, f32[18,128]{1,0:T(8,128)} %reshape.385.top_x), custom_call_target="tpu_custom_call" | custom-call | tf_op jit(solution)/shard_map/pallas_call | solution.py:73
  83.8 1.1 %convolution_bitcast_fusion.6 = f32[16,5,128]{2,0,1:T(8,128)S(1)} fusion(bf16[5,64,64]{1,2,0:T(8,128)(2,1)S(1)} %fusion.31, f32[64,768]{1,0:T(8,128)} %bitcast.259), kind=kOutput, calls=%fused_computation.33 | convolution fusion | flops 1310720 | bytes 143360 | tf_op jit(solution)/shard_map/hqk,qhe->khe/dot_general | solution.py:143
  85.5 1.4 %reshape.388 = f32[64,3,768]{2,1,0:T(4,128)S(1)} reshape(f32[64,18,128]{2,1,0:T(8,128)} %get-tuple-element.12) | data formatting | bytes 1179648 | tf_op jit(solution)/shard_map/reshape | solution.py:252
  87.3 0.3 reshape.389
  87.6 6.0 %psum.7 = f32[640]{0:T(1024)} all-reduce(f32[640]{0:T(1024)S(1)} %slice_reduce_fusion), channel_id=1, replica_groups=mesh['dp'=2,'ctx'=64,'head'=4] {'dp'}, use_global_device_ids=true, to_apply=%region_23.24 | all-reduce | flops 640 | bytes 5120 | tf_op jit(solution)/shard_map/psum | solution.py:259
  95.5 0.8 copy.235
  96.3 0.3 fusion.15
  96.6 0.3 fusion.13
  97.1 0.8 copy.234
  98.0 0.8 copy.236
  (102 shorter events, 9.1 us)
Async XLA Ops:
  0.6 0.7 copy-start.7
  3.4 0.9 copy-start.5
  4.5 0.9 copy-start
  5.4 0.9 copy-start.1
  6.3 0.9 copy-start.2
  47.1 1.0 %copy-start.4 = (bf16[64,30,128]{2,1,0:T(8,128)(2,1)S(1)}, bf16[64,30,128]{2,1,0:T(8,128)(2,1)}, u32[]{:S(2)}) copy-start(bf16[64,30,128]{2,1,0:T(8,128)(2,1)} %get-tuple-element.10) | copy-start | bytes 1474564
  51.2 0.7 copy-start.6
  83.8 1.1 %copy-start.3 = (f32[4,16,768]{2,1,0:T(8,128)S(1)}, f32[4,16,768]{2,1,0:T(8,128)}, u32[]{:S(2)}) copy-start(f32[4,16,768]{2,1,0:T(8,128)} %get-tuple-element.11) | copy-start | bytes 589828

commit v5 on v4

--- a/solution.py
+++ b/solution.py
@@ -11,78 +11,97 @@
 HEAD_DIM = 128
 SPAN = 4
 R1 = 8
+RING = 8
 
 
 EPS = 1e-06
 
 
-def gather_kernel(group, mid_x, top_x, mid_out, top_out, send_mid, recv_mid, send_top, recv_top):
+def gather_kernel(
+    group, inner, mid_x, top_x, mid_out, top_out, stage,
+    send_mid, recv_mid, send_a, recv_a, send_b, recv_b, local_sem,
+):
     count = lax.axis_size("ctx")
+    outer = count // inner
     me = lax.axis_index("ctx")
     row = lax.axis_index("dp")
     col = lax.axis_index("head")
+    lo = me % inner
+    hi = me // inner
     base = me - me % group
+    mesh_ids = pl.DeviceIdType.MESH
+
+    def inner_peer(j):
+        return hi * inner + lax.rem(lo + j, inner)
+
+    def outer_peer(j):
+        return lax.rem(hi + j, outer) * inner + lo
+
     barrier = pltpu.get_barrier_semaphore()
-
-    def greet(j, carry):
-        peer = lax.rem(me + j, count)
-        pl.semaphore_signal(
-            barrier, 1, device_id=(row, peer, col), device_id_type=pl.DeviceIdType.MESH
-        )
-        return carry
-
-    lax.fori_loop(1, count, greet, 0)
-    pl.semaphore_wait(barrier, count - 1)
+    for j in range(1, inner):
+        pl.semaphore_signal(barrier, 1, device_id=(row, inner_peer(j), col), device_id_type=mesh_ids)
+    for j in range(1, outer):
+        pl.semaphore_signal(barrier, 1, device_id=(row, outer_peer(j), col), device_id_type=mesh_ids)
+    pl.semaphore_wait(barrier, inner + outer - 2)
 
     def mid_copy(j):
         peer = base + lax.rem(me % group + j, group)
         return pltpu.make_async_remote_copy(
             mid_x, mid_out.at[j], send_mid.at[j], recv_mid.at[j],
-            device_id=(row, peer, col), device_id_type=pl.DeviceIdType.MESH,
+            device_id=(row, peer, col), device_id_type=mesh_ids,
         )
 
-    def top_copy(j):
-        peer = lax.rem(me + j, count)
+    def copy_a(j):
         return pltpu.make_async_remote_copy(
-            top_x, top_out.at[j], send_top.at[j], recv_top.at[j],
-            device_id=(row, peer, col), device_id_type=pl.DeviceIdType.MESH,
+            top_x, stage.at[j], send_a.at[j], recv_a.at[j],
+            device_id=(row, inner_peer(j), col), device_id_type=mesh_ids,
         )
 
+    def copy_b(j):
+        return pltpu.make_async_remote_copy(
+            stage, top_out.at[j], send_b.at[j], recv_b.at[j],
+            device_id=(row, outer_peer(j), col), device_id_type=mesh_ids,
+        )
+
+    for j in range(1, inner):
+        copy_a(j).start()
     for j in range(1, group):
         mid_copy(j).start()
-
-    def start_top(j, carry):
-        top_copy(j).start()
-        return carry
-
-    lax.fori_loop(1, count, start_top, 0)
+    own = pltpu.make_async_copy(top_x, stage.at[0], local_sem)
+    own.start()
     mid_out[0] = mid_x[...]
-    top_out[0] = top_x[...]
+    own.wait()
+    for j in range(1, inner):
+        copy_a(j).wait()
+    for j in range(1, outer):
+        copy_b(j).start()
+    top_out[0] = stage[...]
     for j in range(1, group):
         mid_copy(j).wait()
-
-    def wait_top(j, carry):
-        top_copy(j).wait()
-        return carry
-
-    lax.fori_loop(1, count, wait_top, 0)
+    for j in range(1, outer):
+        copy_b(j).wait()
 
 
 def ctx_gather(mid_x, top_x, group, tag):
     count = lax.axis_size("ctx")
+    inner = RING
     return pl.pallas_call(
-        functools.partial(gather_kernel, group),
+        functools.partial(gather_kernel, group, inner),
         out_shape=(
             jax.ShapeDtypeStruct((group,) + mid_x.shape, mid_x.dtype),
-            jax.ShapeDtypeStruct((count,) + top_x.shape, top_x.dtype),
+            jax.ShapeDtypeStruct((count // inner, inner) + top_x.shape, top_x.dtype),
         ),
         in_specs=[pl.BlockSpec(memory_space=pltpu.VMEM)] * 2,
         out_specs=(pl.BlockSpec(memory_space=pltpu.VMEM),) * 2,
         scratch_shapes=[
+            pltpu.VMEM((inner,) + top_x.shape, top_x.dtype),
             pltpu.SemaphoreType.DMA((group,)),
             pltpu.SemaphoreType.DMA((group,)),
-            pltpu.SemaphoreType.DMA((count,)),
-            pltpu.SemaphoreType.DMA((count,)),
+            pltpu.SemaphoreType.DMA((inner,)),
+            pltpu.SemaphoreType.DMA((inner,)),
+            pltpu.SemaphoreType.DMA((count // inner,)),
+            pltpu.SemaphoreType.DMA((count // inner,)),
+            pltpu.SemaphoreType.DMA,
         ],
         compiler_params=pltpu.CompilerParams(collective_id=tag, has_side_effects=True),
     )(mid_x, top_x)

time: 99.4 us -> 89.5 us (0.900)
  Pallas kernels: 64 us -> 53.2 us
    pallas_call x2, Pallas kernels: 64 us -> 53.2 us  [ctx_gather(): pl.pallas_call(functools.partial(gather_kernel, group, inner), out_shape=...]
where the time goes in v5:
time: 89.5 us; the launch traced here: 88.9 us
  Pallas kernels  53.2 us (59%)
  local copies, waits for them, and re-layouts  16.6 us (19%)
  blocking collectives  6.9 us (8%)
  other arithmetic  5.62 us (6%)
  matrix products  5.47 us (6%)
  between operations  1.09 us (1%)
    pallas_call x2, Pallas kernels, ctx_gather(): pl.pallas_call(functools.partial(gather_kernel, group, inner), out_shape=...  53.2 us
    unnamed x29, local copies, waits for them, and re-layouts  9.62 us
    psum x1, blocking collectives, shards(): lax.psum(jnp.sum(gathered[:, top_rows, :flat_width], axis=0), 'dp')  6.9 us
    reduce_sum x6, other arithmetic, pick_rows(): return jnp.sum(chosen, axis=1, dtype=source_rows.dtype)  2.47 us

profile of v5, /device:TPU:1, one launch (start us, length us, event | category | flops | bytes accessed | tf_op | source)
XLA Modules:
  0.0 88.9 jit_solution(8197086648967573982)
XLA Ops:
  0.6 0.7 copy-done.7
  1.9 1.5 %fusion.30 = (bf16[16,5,128]{2,0,1:T(8,128)(2,1)S(1)}, bf16[16,5,128]{2,0,1:T(8,128)(2,1)S(1)}, bf16[16,5,128]{2,0,1:T(8,128)(2,1)S(1)}) fusion(pred[8,5]{0,1:T(8,128)(4,1)S(1)} %iota_compare_fusion.1, bf16[1,128,640]{2,1,0:T(8,128)(2,1)} %param.8, bf16[1,128,640]{2,1,0:T(8,128)(2,1)} %param.7, bf16[1,128,640]{2,1,0:T(8,128)(2,1)} %param.6), kind=kLoop, calls=%fused_computation.77 | loop fusion | flops 460800 | bytes 553000 | tf_op jit(solution)/shard_map/reduce_sum | solution.py:121
  3.4 0.6 pad_maximum_fusion.mid_x
  4.0 0.3 copy-done.5
  4.6 0.8 copy-done
  5.6 0.7 copy-done.1
  6.5 0.7 copy-done.2
  8.0 0.3 select_reduce_fusion.2
  8.3 0.6 reshape.372.top_x
  9.0 0.3 fusion.66
  9.3 31.2 %shard_map.101 = (bf16[4,16,1920]{2,1,0:T(8,128)(2,1)}, bf16[8,8,30,128]{3,2,1,0:T(8,128)(2,1)}) custom-call(bf16[16,1920]{1,0:T(8,128)(2,1)} %pad_maximum_fusion.mid_x, bf16[30,128]{1,0:T(8,128)(2,1)} %reshape.372.top_x), custom_call_target="tpu_custom_call" | custom-call | tf_op jit(solution)/shard_map/pallas_call | solution.py:88
  40.5 1.0 %slice_bitcast_fusion = (bf16[8,5,8,128]{3,2,1,0:T(8,128)(2,1)S(1)}, bf16[8,5,8,128]{3,2,1,0:T(8,128)(2,1)S(1)}, bf16[8,5,8,128]{3,2,1,0:T(8,128)(2,1)S(1)}) fusion(bf16[64,1920]{1,0:T(8,128)(2,1)} %bitcast.267), kind=kLoop, calls=%fused_computation.91 | loop fusion | bytes 491520
  42.2 0.5 copy-done.4
  42.8 0.5 reshape.376
  43.9 0.3 fusion.64
  45.2 0.5 multiply_reduce_fusion.3
  45.8 0.7 copy-done.6
  46.5 0.3 multiply_reduce_fusion
  47.5 0.4 fusion.17
  48.4 0.6 reshape.385.top_x
  49.4 0.6 maximum_maximum_fusion.mid_x
  50.2 0.8 copy.233
  51.0 22.0 %shard_map.102 = (f32[4,16,768]{2,1,0:T(8,128)}, f32[8,8,18,128]{3,2,1,0:T(8,128)}) custom-call(f32[16,768]{1,0:T(8,128)} %maximum_maximum_fusion.mid_x, f32[18,128]{1,0:T(8,128)} %reshape.385.top_x), custom_call_target="tpu_custom_call" | custom-call | tf_op jit(solution)/shard_map/pallas_call | solution.py:88
  73.0 1.1 %convolution_bitcast_fusion.6 = f32[16,5,128]{2,0,1:T(8,128)S(1)} fusion(bf16[5,64,64]{1,2,0:T(8,128)(2,1)S(1)} %fusion.31, f32[64,768]{1,0:T(8,128)} %bitcast.259), kind=kOutput, calls=%fused_computation.33 | convolution fusion | flops 1310720 | bytes 143360 | tf_op jit(solution)/shard_map/hqk,qhe->khe/dot_general | solution.py:162
  74.7 1.4 %reshape.388 = f32[64,3,768]{2,1,0:T(4,128)S(1)} reshape(f32[8,8,18,128]{3,2,1,0:T(8,128)} %get-tuple-element.12) | data formatting | bytes 1179648 | tf_op jit(solution)/shard_map/reshape | solution.py:271
  76.5 0.3 reshape.389
  76.8 6.9 %psum.7 = f32[640]{0:T(1024)} all-reduce(f32[640]{0:T(1024)S(1)} %slice_reduce_fusion), channel_id=1, replica_groups=mesh['dp'=2,'ctx'=64,'head'=4] {'dp'}, use_global_device_ids=true, to_apply=%region_23.24 | all-reduce | flops 640 | bytes 5120 | tf_op jit(solution)/shard_map/psum | solution.py:278
  85.5 0.8 copy.235
  86.3 0.3 fusion.15
  86.6 0.3 fusion.13
  87.1 0.8 copy.234
  88.1 0.8 copy.236
  (102 shorter events, 9.1 us)
Async XLA Ops:
  0.6 0.7 copy-start.7
  3.4 0.9 %copy-start.5 = (bf16[1,128,640]{2,1,0:T(8,128)(2,1)S(1)}, bf16[1,128,640]{2,1,0:T(8,128)(2,1)}, u32[]{:S(2)}) copy-start(bf16[1,128,640]{2,1,0:T(8,128)(2,1)} %param.9) | copy-start | bytes 491524
  4.5 0.9 %copy-start = (bf16[1,128,640]{2,1,0:T(8,128)(2,1)S(1)}, bf16[1,128,640]{2,1,0:T(8,128)(2,1)}, u32[]{:S(2)}) copy-start(bf16[1,128,640]{2,1,0:T(8,128)(2,1)} %param.6) | copy-start | bytes 491524
  5.4 0.9 %copy-start.1 = (bf16[1,128,640]{2,1,0:T(8,128)(2,1)S(1)}, bf16[1,128,640]{2,1,0:T(8,128)(2,1)}, u32[]{:S(2)}) copy-start(bf16[1,128,640]{2,1,0:T(8,128)(2,1)} %param.7) | copy-start | bytes 491524
  6.3 0.9 %copy-start.2 = (bf16[1,128,640]{2,1,0:T(8,128)(2,1)S(1)}, bf16[1,128,640]{2,1,0:T(8,128)(2,1)}, u32[]{:S(2)}) copy-start(bf16[1,128,640]{2,1,0:T(8,128)(2,1)} %param.8) | copy-start | bytes 491524
  41.7 1.0 %copy-start.4 = (bf16[8,8,30,128]{3,2,1,0:T(8,128)(2,1)S(1)}, bf16[8,8,30,128]{3,2,1,0:T(8,128)(2,1)}, u32[]{:S(2)}) copy-start(bf16[8,8,30,128]{3,2,1,0:T(8,128)(2,1)} %get-tuple-element.10) | copy-start | bytes 1474564
  45.8 0.7 copy-start.6
  73.0 1.1 %copy-start.3 = (f32[4,16,768]{2,1,0:T(8,128)S(1)}, f32[4,16,768]{2,1,0:T(8,128)}, u32[]{:S(2)}) copy-start(f32[4,16,768]{2,1,0:T(8,128)} %get-tuple-element.11) | copy-start | bytes 589828

commit v6 on v5

--- a/solution.py
+++ b/solution.py
@@ -173,18 +173,31 @@
     return tuple(packed[:, i * width : (i + 1) * width].reshape(shape) for i in range(3))
 
 
-def pack_grads(grad_low, row_shift):
+def split_wide(values):
+    high = values.astype(jnp.bfloat16)
+    low = (values - high.astype(jnp.float32)).astype(jnp.bfloat16)
+    return high, low
+
+
+def join_wide(high, low):
+    return high.astype(jnp.float32) + low.astype(jnp.float32)
+
+
+def pack_grads(grad_low, row_shift, width):
     rows = grad_low.shape[0]
-    pad = jnp.zeros((rows, HEAD_DIM - row_shift.shape[1]), jnp.float32)
+    high, low = split_wide(row_shift)
+    used = grad_low.shape[1] * grad_low.shape[2] + 2 * row_shift.shape[1]
     return jnp.concatenate(
-        [grad_low.astype(jnp.float32).reshape(rows, -1), row_shift.astype(jnp.float32), pad], 1
+        [grad_low.reshape(rows, -1), high, low, jnp.zeros((rows, width - used), jnp.bfloat16)], 1
     )
 
 
 def unpack_grads(packed, head_count):
     width = head_count * HEAD_DIM
-    grad_low = packed[:, :width].astype(jnp.bfloat16).reshape(-1, head_count, HEAD_DIM)
-    return grad_low, packed[:, width : width + head_count]
+    grad_low = packed[:, :width].reshape(-1, head_count, HEAD_DIM)
+    return grad_low, join_wide(
+        packed[:, width : width + head_count], packed[:, width + head_count : width + 2 * head_count]
+    )
 
 
 def shards(queries, keys, values, grad_y, out_gain, offsets):
@@ -262,20 +275,35 @@
     top_low = (top_sel[..., None] * pick_rows(grad_attn, ctx_size, top_shift)).astype(jnp.bfloat16)
     top_row_shift = -(top_sel * pick_rows(inner[..., None], ctx_size, top_shift)[..., 0])
 
-    top_grads = pack_grads(top_low, top_row_shift)
-    gain_row = jnp.pad(gain_part, (0, top_grads.shape[1] - flat_width))[None]
-    top_block = jnp.concatenate([top_grads, gain_row], 0)
+    gain_high, gain_low = split_wide(gain_part)
+    shift_high, shift_low = split_wide(top_row_shift.reshape(-1))
+    top_flat = jnp.concatenate(
+        [top_low.reshape(-1), gain_high, gain_low, shift_high, shift_low]
+    )
+    tile = 16 * HEAD_DIM
+    top_flat = jnp.pad(top_flat, (0, -top_flat.shape[0] % tile))
     mid_gathered, gathered = ctx_gather(
-        pack_grads(mid_low, mid_row_shift), lane_dense(top_block), SPAN, 1
-    )
-    gathered = gathered.reshape((-1,) + top_block.shape)
+        pack_grads(mid_low, mid_row_shift, flat_width + HEAD_DIM),
+        lane_dense(top_flat),
+        SPAN,
+        1,
+    )
     mid_low_all, mid_shift_all = unpack_grads(
         mid_gathered.reshape(-1, mid_gathered.shape[-1]), head_count
     )
-    top_low_all, top_shift_all = unpack_grads(
-        gathered[:, :top_rows].reshape(-1, top_grads.shape[1]), head_count
-    )
-    gain_grad = lax.psum(jnp.sum(gathered[:, top_rows, :flat_width], axis=0), "dp")
+    gathered = gathered.reshape(ctx_size, -1)
+    grad_width = top_rows * flat_width
+    top_low_all = gathered[:, :grad_width].reshape(-1, head_count, HEAD_DIM)
+    gain_cols = gathered[:, grad_width : grad_width + 2 * flat_width]
+    gain_grad = lax.psum(
+        jnp.sum(join_wide(gain_cols[:, :flat_width], gain_cols[:, flat_width:]), axis=0), "dp"
+    )
+    shift_start = grad_width + 2 * flat_width
+    shift_count = top_rows * head_count
+    top_shift_all = join_wide(
+        gathered[:, shift_start : shift_start + shift_count],
+        gathered[:, shift_start + shift_count : shift_start + 2 * shift_count],
+    ).reshape(-1, head_count)
 
     mid_grad, mid_soft = score_grads(
         mid_q, mid_k, mid_v, mid_total_all, mid_low_all, mid_shift_all

time: 89.5 us -> 89.3 us (level)
  Pallas kernels: 53.2 us -> 51.8 us
    unnamed x29 -> x49, local copies, waits for them, and re-layouts: 9.62 us -> 11.4 us
    reshape x2, local copies, waits for them, and re-layouts: 1.7 us -> 0.29 us  [the longest x1 0.22 us: shards(): top_low_all = gathered[:, :grad_width].reshape(-1, head_count, HEAD_DIM)]
    pallas_call x2, Pallas kernels: 53.2 us -> 51.8 us  [ctx_gather(): pl.pallas_call(functools.partial(gather_kernel, group, inner), out_shape=...]
where the time goes in v6:
time: 89.3 us; the launch traced here: 88.7 us
  Pallas kernels  51.8 us (58%)
  local copies, waits for them, and re-layouts  17.1 us (19%)
  blocking collectives  7.13 us (8%)
  matrix products  6.04 us (7%)
  other arithmetic  5.55 us (6%)
  between operations  1.14 us (1%)
    pallas_call x2, Pallas kernels, ctx_gather(): pl.pallas_call(functools.partial(gather_kernel, group, inner), out_shape=...  51.8 us
    unnamed x49, local copies, waits for them, and re-layouts  11.4 us
    psum x1, blocking collectives, shards(): lax.psum(jnp.sum(join_wide(gain_cols[:, :flat_width], gain_cols[:, flat_w...  7.13 us
    reduce_sum x6, other arithmetic, pick_rows(): return jnp.sum(chosen, axis=1, dtype=source_rows.dtype)  2.46 us
    dot_general x3, matrix products, key_parts(): jnp.einsum('hqk,qhe->khe', soft_low, grad_low, preferred_element_type=jnp...  2.19 us

profile of v6, /device:TPU:1, one launch (start us, length us, event | category | flops | bytes accessed | tf_op | source)
XLA Modules:
  0.0 88.7 jit_solution(4051470558253065201)
XLA Ops:
  0.6 0.7 copy-done.18
  1.9 1.5 %fusion.30 = (bf16[16,5,128]{2,0,1:T(8,128)(2,1)S(1)}, bf16[16,5,128]{2,0,1:T(8,128)(2,1)S(1)}, bf16[16,5,128]{2,0,1:T(8,128)(2,1)S(1)}) fusion(pred[8,5]{0,1:T(8,128)(4,1)S(1)} %iota_compare_fusion.1, bf16[1,128,640]{2,1,0:T(8,128)(2,1)} %param.8, bf16[1,128,640]{2,1,0:T(8,128)(2,1)} %param.7, bf16[1,128,640]{2,1,0:T(8,128)(2,1)} %param.6), kind=kLoop, calls=%fused_computation.76 | loop fusion | flops 460800 | bytes 553000 | tf_op jit(solution)/shard_map/reduce_sum | solution.py:121
  3.4 0.6 pad_maximum_fusion.mid_x
  4.0 0.3 copy-done.8
  4.6 0.8 copy-done
  5.6 0.7 copy-done.1
  6.5 0.7 copy-done.2
  8.0 0.3 select_reduce_fusion.2
  8.3 0.6 reshape.373.top_x
  9.3 31.2 %shard_map.101 = (bf16[4,16,1920]{2,1,0:T(8,128)(2,1)}, bf16[8,8,30,128]{3,2,1,0:T(8,128)(2,1)}) custom-call(bf16[16,1920]{1,0:T(8,128)(2,1)} %pad_maximum_fusion.mid_x, bf16[30,128]{1,0:T(8,128)(2,1)} %reshape.373.top_x), custom_call_target="tpu_custom_call" | custom-call | tf_op jit(solution)/shard_map/pallas_call | solution.py:88
  40.5 1.0 %slice_bitcast_fusion.1 = (bf16[8,5,8,128]{3,2,1,0:T(8,128)(2,1)S(1)}, bf16[8,5,8,128]{3,2,1,0:T(8,128)(2,1)S(1)}, bf16[8,5,8,128]{3,2,1,0:T(8,128)(2,1)S(1)}) fusion(bf16[64,1920]{1,0:T(8,128)(2,1)} %bitcast.270), kind=kLoop, calls=%fused_computation.93 | loop fusion | bytes 491520
  42.4 0.4 copy-done.5
  42.8 0.5 reshape.377
  43.9 0.3 fusion.67
  45.5 0.5 multiply_reduce_fusion.3
  46.0 0.7 copy-done.14
  46.7 0.3 multiply_reduce_fusion
  47.7 0.4 fusion.17
  48.7 0.6 pad_bitcast_fusion.top_x
  49.7 0.7 maximum_maximum_fusion.mid_x
  50.5 0.8 copy.230
  51.4 20.6 %shard_map.102 = (bf16[4,16,768]{2,1,0:T(8,128)(2,1)}, bf16[8,8,32,128]{3,2,1,0:T(8,128)(2,1)}) custom-call(bf16[16,768]{1,0:T(8,128)(2,1)} %maximum_maximum_fusion.mid_x, bf16[32,128]{1,0:T(8,128)(2,1)} %pad_bitcast_fusion.top_x), custom_call_target="tpu_custom_call" | custom-call | tf_op jit(solution)/shard_map/pallas_call | solution.py:88
  72.0 1.7 %convolution_bitcast_fusion.6 = f32[16,5,128]{2,0,1:T(8,128)} fusion(bf16[5,64,64]{1,2,0:T(8,128)(2,1)} %copy-done.5, bf16[64,768]{1,0:T(8,128)(2,1)} %bitcast.278), kind=kOutput, calls=%fused_computation.33 | convolution fusion | flops 1310720 | bytes 143360 | tf_op jit(solution)/shard_map/hqk,qhe->khe/dot_general | solution.py:162
  74.7 7.1 %psum.7 = f32[640]{0:T(1024)} all-reduce(f32[640]{0:T(1024)S(1)} %add_reduce_fusion), channel_id=1, replica_groups=mesh['dp'=2,'ctx'=64,'head'=4] {'dp'}, use_global_device_ids=true, to_apply=%region_23.24 | all-reduce | flops 640 | bytes 5120 | tf_op jit(solution)/shard_map/psum | solution.py:298
  82.3 0.5 copy-done.10
  83.6 0.5 copy-done.16
  84.3 0.7 copy-done.13
  85.4 0.8 copy.232
  86.2 0.3 fusion.15
  86.5 0.3 fusion.13
  86.9 0.8 copy.231
  87.9 0.8 copy.233
  (123 shorter events, 9.9 us)
Async XLA Ops:
  0.6 0.7 copy-start.18
  1.6 43.6 %copy-start.15 = (pred[128,5]{0,1:T(8,128)(4,1)}, pred[128,5]{0,1:T(8,128)(4,1)S(1)}, u32[]{:S(2)}) copy-start(pred[128,5]{0,1:T(8,128)(4,1)S(1)} %broadcast_in_dim.290) | copy-start | bytes 1924
  1.9 43.6 %copy-start.12 = (pred[128,5]{0,1:T(8,128)(4,1)}, pred[128,5]{0,1:T(8,128)(4,1)S(1)}, u32[]{:S(2)}) copy-start(pred[128,5]{0,1:T(8,128)(4,1)S(1)} %broadcast_in_dim.281) | copy-start | bytes 1924
  3.4 0.9 %copy-start.8 = (bf16[1,128,640]{2,1,0:T(8,128)(2,1)S(1)}, bf16[1,128,640]{2,1,0:T(8,128)(2,1)}, u32[]{:S(2)}) copy-start(bf16[1,128,640]{2,1,0:T(8,128)(2,1)} %param.9) | copy-start | bytes 491524
  4.5 0.9 %copy-start = (bf16[1,128,640]{2,1,0:T(8,128)(2,1)S(1)}, bf16[1,128,640]{2,1,0:T(8,128)(2,1)}, u32[]{:S(2)}) copy-start(bf16[1,128,640]{2,1,0:T(8,128)(2,1)} %param.6) | copy-start | bytes 491524
  5.4 0.9 %copy-start.1 = (bf16[1,128,640]{2,1,0:T(8,128)(2,1)S(1)}, bf16[1,128,640]{2,1,0:T(8,128)(2,1)}, u32[]{:S(2)}) copy-start(bf16[1,128,640]{2,1,0:T(8,128)(2,1)} %param.7) | copy-start | bytes 491524
  6.3 0.9 %copy-start.2 = (bf16[1,128,640]{2,1,0:T(8,128)(2,1)S(1)}, bf16[1,128,640]{2,1,0:T(8,128)(2,1)}, u32[]{:S(2)}) copy-start(bf16[1,128,640]{2,1,0:T(8,128)(2,1)} %param.8) | copy-start | bytes 491524
  41.5 0.6 copy-start.6
  41.7 1.1 %copy-start.3 = (bf16[8,8,30,128]{3,2,1,0:T(8,128)(2,1)S(1)}, bf16[8,8,30,128]{3,2,1,0:T(8,128)(2,1)}, u32[]{:S(2)}) copy-start(bf16[8,8,30,128]{3,2,1,0:T(8,128)(2,1)} %get-tuple-element.10) | copy-start | bytes 1474564
  42.2 0.6 copy-start.5
  44.3 0.6 copy-start.9
  46.0 0.7 copy-start.14
  50.5 23.3 %copy-start.7 = (bf16[8,5,8,128]{3,2,1,0:T(8,128)(2,1)S(1)}, bf16[8,5,8,128]{3,2,1,0:T(8,128)(2,1)}, u32[]{:S(2)}) copy-start(bf16[8,5,8,128]{3,2,1,0:T(8,128)(2,1)} %copy-done.6) | copy-start | bytes 245764
  72.0 1.8 %copy-start.17 = (bf16[4,16,768]{2,1,0:T(8,128)(2,1)S(1)}, bf16[4,16,768]{2,1,0:T(8,128)(2,1)}, u32[]{:S(2)}) copy-start(bf16[4,16,768]{2,1,0:T(8,128)(2,1)} %get-tuple-element.11) | copy-start | bytes 294916
  72.0 2.4 %copy-start.4 = (bf16[8,8,32,128]{3,2,1,0:T(8,128)(2,1)S(1)}, bf16[8,8,32,128]{3,2,1,0:T(8,128)(2,1)}, u32[]{:S(2)}) copy-start(bf16[8,8,32,128]{3,2,1,0:T(8,128)(2,1)} %get-tuple-element.12) | copy-start | bytes 1572868
  82.0 0.7 copy-start.10
  83.4 0.7 copy-start.16
  84.3 0.7 copy-start.13
  85.3 0.8 copy-start.11

commit v7 on v5

--- a/solution.py
+++ b/solution.py
@@ -37,12 +37,14 @@
     def outer_peer(j):
         return lax.rem(hi + j, outer) * inner + lo
 
+    right = outer_peer(1)
+    left = outer_peer(outer - 1)
     barrier = pltpu.get_barrier_semaphore()
     for j in range(1, inner):
         pl.semaphore_signal(barrier, 1, device_id=(row, inner_peer(j), col), device_id_type=mesh_ids)
-    for j in range(1, outer):
-        pl.semaphore_signal(barrier, 1, device_id=(row, outer_peer(j), col), device_id_type=mesh_ids)
-    pl.semaphore_wait(barrier, inner + outer - 2)
+    for peer in (right, left):
+        pl.semaphore_signal(barrier, 1, device_id=(row, peer, col), device_id_type=mesh_ids)
+    pl.semaphore_wait(barrier, inner + 1)
 
     def mid_copy(j):
         peer = base + lax.rem(me % group + j, group)
@@ -57,11 +59,22 @@
             device_id=(row, inner_peer(j), col), device_id_type=mesh_ids,
         )
 
-    def copy_b(j):
+    def ring_copy(slot, source, peer):
         return pltpu.make_async_remote_copy(
-            stage, top_out.at[j], send_b.at[j], recv_b.at[j],
-            device_id=(row, outer_peer(j), col), device_id_type=mesh_ids,
+            source, top_out.at[slot], send_b.at[slot], recv_b.at[slot],
+            device_id=(row, peer, col), device_id_type=mesh_ids,
         )
+
+    right_steps = outer // 2
+    left_steps = outer - 1 - right_steps
+
+    def right_copy(step):
+        source = stage if step == 1 else top_out.at[step - 1]
+        return ring_copy(step, source, right)
+
+    def left_copy(step):
+        source = stage if step == 1 else top_out.at[outer - step + 1]
+        return ring_copy(outer - step, source, left)
 
     for j in range(1, inner):
         copy_a(j).start()
@@ -73,13 +86,25 @@
     own.wait()
     for j in range(1, inner):
         copy_a(j).wait()
-    for j in range(1, outer):
-        copy_b(j).start()
+    right_copy(1).start()
+    if left_steps >= 1:
+        left_copy(1).start()
     top_out[0] = stage[...]
+    for step in range(2, right_steps + 1):
+        right_copy(step - 1).wait_recv()
+        right_copy(step).start()
+        if step <= left_steps:
+            left_copy(step - 1).wait_recv()
+            left_copy(step).start()
+    right_copy(right_steps).wait_recv()
+    if left_steps >= 1:
+        left_copy(left_steps).wait_recv()
+    for step in range(1, right_steps + 1):
+        right_copy(step).wait_send()
+    for step in range(1, left_steps + 1):
+        left_copy(step).wait_send()
     for j in range(1, group):
         mid_copy(j).wait()
-    for j in range(1, outer):
-        copy_b(j).wait()
 
 
 def ctx_gather(mid_x, top_x, group, tag):

time: 89.5 us -> 93.3 us (1.042)
  blocking collectives: 6.9 us -> 12.5 us
  Pallas kernels: 53.2 us -> 51.4 us
    psum x1, blocking collectives: 6.9 us -> 12.5 us  [shards(): lax.psum(jnp.sum(gathered[:, top_rows, :flat_width], axis=0), 'dp')]
    pallas_call x2, Pallas kernels: 53.2 us -> 51.4 us  [ctx_gather(): pl.pallas_call(functools.partial(gather_kernel, group, inner), out_shape=...]
where the time goes in v7:
time: 93.3 us; the launch traced here: 92.8 us
  Pallas kernels  51.4 us (55%)
  local copies, waits for them, and re-layouts  16.6 us (18%)
  blocking collectives  12.5 us (13%)
  other arithmetic  5.62 us (6%)
  matrix products  5.48 us (6%)
  between operations  1.09 us (1%)
    pallas_call x2, Pallas kernels, ctx_gather(): pl.pallas_call(functools.partial(gather_kernel, group, inner), out_shape=...  51.4 us
    psum x1, blocking collectives, shards(): lax.psum(jnp.sum(gathered[:, top_rows, :flat_width], axis=0), 'dp')  12.5 us
    unnamed x29, local copies, waits for them, and re-layouts  9.62 us
    reduce_sum x6, other arithmetic, pick_rows(): return jnp.sum(chosen, axis=1, dtype=source_rows.dtype)  2.47 us

profile of v7, /device:TPU:1, one launch (start us, length us, event | category | flops | bytes accessed | tf_op | source)
XLA Modules:
  0.0 92.8 jit_solution(3662886470783297520)
XLA Ops:
  0.6 0.7 copy-done.7
  1.9 1.5 %fusion.30 = (bf16[16,5,128]{2,0,1:T(8,128)(2,1)S(1)}, bf16[16,5,128]{2,0,1:T(8,128)(2,1)S(1)}, bf16[16,5,128]{2,0,1:T(8,128)(2,1)S(1)}) fusion(pred[8,5]{0,1:T(8,128)(4,1)S(1)} %iota_compare_fusion.1, bf16[1,128,640]{2,1,0:T(8,128)(2,1)} %param.8, bf16[1,128,640]{2,1,0:T(8,128)(2,1)} %param.7, bf16[1,128,640]{2,1,0:T(8,128)(2,1)} %param.6), kind=kLoop, calls=%fused_computation.77 | loop fusion | flops 460800 | bytes 553000 | tf_op jit(solution)/shard_map/reduce_sum | solution.py:146
  3.4 0.6 pad_maximum_fusion.mid_x
  4.0 0.3 copy-done.5
  4.6 0.8 copy-done
  5.6 0.7 copy-done.1
  6.5 0.7 copy-done.2
  8.0 0.3 select_reduce_fusion.2
  8.3 0.6 reshape.372.top_x
  9.0 0.3 fusion.66
  9.3 29.0 %shard_map.101 = (bf16[4,16,1920]{2,1,0:T(8,128)(2,1)}, bf16[8,8,30,128]{3,2,1,0:T(8,128)(2,1)}) custom-call(bf16[16,1920]{1,0:T(8,128)(2,1)} %pad_maximum_fusion.mid_x, bf16[30,128]{1,0:T(8,128)(2,1)} %reshape.372.top_x), custom_call_target="tpu_custom_call" | custom-call | tf_op jit(solution)/shard_map/pallas_call | solution.py:113
  38.3 1.0 %slice_bitcast_fusion = (bf16[8,5,8,128]{3,2,1,0:T(8,128)(2,1)S(1)}, bf16[8,5,8,128]{3,2,1,0:T(8,128)(2,1)S(1)}, bf16[8,5,8,128]{3,2,1,0:T(8,128)(2,1)S(1)}) fusion(bf16[64,1920]{1,0:T(8,128)(2,1)} %bitcast.267), kind=kLoop, calls=%fused_computation.91 | loop fusion | bytes 491520
  40.0 0.5 copy-done.4
  40.5 0.5 reshape.376
  41.6 0.3 fusion.64
  43.0 0.5 multiply_reduce_fusion.3
  43.5 0.7 copy-done.6
  44.2 0.3 multiply_reduce_fusion
  45.2 0.4 fusion.17
  46.1 0.6 reshape.385.top_x
  47.1 0.6 maximum_maximum_fusion.mid_x
  47.9 0.8 copy.233
  48.8 22.5 %shard_map.102 = (f32[4,16,768]{2,1,0:T(8,128)}, f32[8,8,18,128]{3,2,1,0:T(8,128)}) custom-call(f32[16,768]{1,0:T(8,128)} %maximum_maximum_fusion.mid_x, f32[18,128]{1,0:T(8,128)} %reshape.385.top_x), custom_call_target="tpu_custom_call" | custom-call | tf_op jit(solution)/shard_map/pallas_call | solution.py:113
  71.2 1.1 %convolution_bitcast_fusion.6 = f32[16,5,128]{2,0,1:T(8,128)S(1)} fusion(bf16[5,64,64]{1,2,0:T(8,128)(2,1)S(1)} %fusion.31, f32[64,768]{1,0:T(8,128)} %bitcast.259), kind=kOutput, calls=%fused_computation.33 | convolution fusion | flops 1310720 | bytes 143360 | tf_op jit(solution)/shard_map/hqk,qhe->khe/dot_general | solution.py:187
  73.0 1.4 %reshape.388 = f32[64,3,768]{2,1,0:T(4,128)S(1)} reshape(f32[8,8,18,128]{3,2,1,0:T(8,128)} %get-tuple-element.12) | data formatting | bytes 1179648 | tf_op jit(solution)/shard_map/reshape | solution.py:296
  74.8 0.3 reshape.389
  75.0 12.5 %psum.7 = f32[640]{0:T(1024)} all-reduce(f32[640]{0:T(1024)S(1)} %slice_reduce_fusion), channel_id=1, replica_groups=mesh['dp'=2,'ctx'=64,'head'=4] {'dp'}, use_global_device_ids=true, to_apply=%region_23.24 | all-reduce | flops 640 | bytes 5120 | tf_op jit(solution)/shard_map/psum | solution.py:303
  89.4 0.8 copy.235
  90.2 0.3 fusion.15
  90.5 0.3 fusion.13
  91.0 0.8 copy.234
  92.0 0.8 copy.236
  (102 shorter events, 9.1 us)
Async XLA Ops:
  0.6 0.7 copy-start.7
  3.4 0.9 %copy-start.5 = (bf16[1,128,640]{2,1,0:T(8,128)(2,1)S(1)}, bf16[1,128,640]{2,1,0:T(8,128)(2,1)}, u32[]{:S(2)}) copy-start(bf16[1,128,640]{2,1,0:T(8,128)(2,1)} %param.9) | copy-start | bytes 491524
  4.5 0.9 copy-start
  5.4 0.9 copy-start.1
  6.3 0.9 copy-start.2
  39.5 1.0 %copy-start.4 = (bf16[8,8,30,128]{3,2,1,0:T(8,128)(2,1)S(1)}, bf16[8,8,30,128]{3,2,1,0:T(8,128)(2,1)}, u32[]{:S(2)}) copy-start(bf16[8,8,30,128]{3,2,1,0:T(8,128)(2,1)} %get-tuple-element.10) | copy-start | bytes 1474564
  43.5 0.7 copy-start.6
  71.2 1.1 %copy-start.3 = (f32[4,16,768]{2,1,0:T(8,128)S(1)}, f32[4,16,768]{2,1,0:T(8,128)}, u32[]{:S(2)}) copy-start(f32[4,16,768]{2,1,0:T(8,128)} %get-tuple-element.11) | copy-start | bytes 589828

commit v8 on v5

--- a/solution.py
+++ b/solution.py
@@ -65,8 +65,6 @@
 
     for j in range(1, inner):
         copy_a(j).start()
-    for j in range(1, group):
-        mid_copy(j).start()
     own = pltpu.make_async_copy(top_x, stage.at[0], local_sem)
     own.start()
     mid_out[0] = mid_x[...]
@@ -75,6 +73,8 @@
         copy_a(j).wait()
     for j in range(1, outer):
         copy_b(j).start()
+    for j in range(1, group):
+        mid_copy(j).start()
     top_out[0] = stage[...]
     for j in range(1, group):
         mid_copy(j).wait()

time: 89.5 us -> 91.4 us (1.021)
  Pallas kernels: 53.2 us -> 55.1 us
    pallas_call x2, Pallas kernels: 53.2 us -> 55.1 us  [ctx_gather(): pl.pallas_call(functools.partial(gather_kernel, group, inner), out_shape=...]
where the time goes in v8:
time: 91.4 us; the launch traced here: 90.9 us
  Pallas kernels  55.1 us (60%)
  local copies, waits for them, and re-layouts  16.6 us (18%)
  blocking collectives  6.96 us (8%)
  other arithmetic  5.62 us (6%)
  matrix products  5.47 us (6%)
  between operations  1.09 us (1%)
    pallas_call x2, Pallas kernels, ctx_gather(): pl.pallas_call(functools.partial(gather_kernel, group, inner), out_shape=...  55.1 us
    unnamed x29, local copies, waits for them, and re-layouts  9.62 us
    psum x1, blocking collectives, shards(): lax.psum(jnp.sum(gathered[:, top_rows, :flat_width], axis=0), 'dp')  6.96 us
    reduce_sum x6, other arithmetic, pick_rows(): return jnp.sum(chosen, axis=1, dtype=source_rows.dtype)  2.47 us

profile of v8, /device:TPU:1, one launch (start us, length us, event | category | flops | bytes accessed | tf_op | source)
XLA Modules:
  0.0 90.9 jit_solution(6967282493370276105)
XLA Ops:
  0.6 0.7 copy-done.7
  1.9 1.5 %fusion.30 = (bf16[16,5,128]{2,0,1:T(8,128)(2,1)S(1)}, bf16[16,5,128]{2,0,1:T(8,128)(2,1)S(1)}, bf16[16,5,128]{2,0,1:T(8,128)(2,1)S(1)}) fusion(pred[8,5]{0,1:T(8,128)(4,1)S(1)} %iota_compare_fusion.1, bf16[1,128,640]{2,1,0:T(8,128)(2,1)} %param.8, bf16[1,128,640]{2,1,0:T(8,128)(2,1)} %param.7, bf16[1,128,640]{2,1,0:T(8,128)(2,1)} %param.6), kind=kLoop, calls=%fused_computation.77 | loop fusion | flops 460800 | bytes 553000 | tf_op jit(solution)/shard_map/reduce_sum | solution.py:121
  3.4 0.6 pad_maximum_fusion.mid_x
  4.0 0.3 copy-done.5
  4.6 0.8 copy-done
  5.6 0.7 copy-done.1
  6.5 0.7 copy-done.2
  8.0 0.3 select_reduce_fusion.2
  8.3 0.6 reshape.372.top_x
  9.0 0.3 fusion.66
  9.3 31.3 %shard_map.101 = (bf16[4,16,1920]{2,1,0:T(8,128)(2,1)}, bf16[8,8,30,128]{3,2,1,0:T(8,128)(2,1)}) custom-call(bf16[16,1920]{1,0:T(8,128)(2,1)} %pad_maximum_fusion.mid_x, bf16[30,128]{1,0:T(8,128)(2,1)} %reshape.372.top_x), custom_call_target="tpu_custom_call" | custom-call | tf_op jit(solution)/shard_map/pallas_call | solution.py:88
  40.6 1.0 %slice_bitcast_fusion = (bf16[8,5,8,128]{3,2,1,0:T(8,128)(2,1)S(1)}, bf16[8,5,8,128]{3,2,1,0:T(8,128)(2,1)S(1)}, bf16[8,5,8,128]{3,2,1,0:T(8,128)(2,1)S(1)}) fusion(bf16[64,1920]{1,0:T(8,128)(2,1)} %bitcast.267), kind=kLoop, calls=%fused_computation.91 | loop fusion | bytes 491520
  42.3 0.5 copy-done.4
  42.8 0.5 reshape.376
  43.9 0.3 fusion.64
  45.3 0.5 multiply_reduce_fusion.3
  45.8 0.7 copy-done.6
  46.5 0.3 multiply_reduce_fusion
  47.5 0.4 fusion.17
  48.5 0.6 reshape.385.top_x
  49.4 0.6 maximum_maximum_fusion.mid_x
  50.2 0.8 copy.233
  51.1 23.8 %shard_map.102 = (f32[4,16,768]{2,1,0:T(8,128)}, f32[8,8,18,128]{3,2,1,0:T(8,128)}) custom-call(f32[16,768]{1,0:T(8,128)} %maximum_maximum_fusion.mid_x, f32[18,128]{1,0:T(8,128)} %reshape.385.top_x), custom_call_target="tpu_custom_call" | custom-call | tf_op jit(solution)/shard_map/pallas_call | solution.py:88
  74.9 1.1 %convolution_bitcast_fusion.6 = f32[16,5,128]{2,0,1:T(8,128)S(1)} fusion(bf16[5,64,64]{1,2,0:T(8,128)(2,1)S(1)} %fusion.31, f32[64,768]{1,0:T(8,128)} %bitcast.259), kind=kOutput, calls=%fused_computation.33 | convolution fusion | flops 1310720 | bytes 143360 | tf_op jit(solution)/shard_map/hqk,qhe->khe/dot_general | solution.py:162
  76.6 1.4 %reshape.388 = f32[64,3,768]{2,1,0:T(4,128)S(1)} reshape(f32[8,8,18,128]{3,2,1,0:T(8,128)} %get-tuple-element.12) | data formatting | bytes 1179648 | tf_op jit(solution)/shard_map/reshape | solution.py:271
  78.4 0.3 reshape.389
  78.7 7.0 %psum.7 = f32[640]{0:T(1024)} all-reduce(f32[640]{0:T(1024)S(1)} %slice_reduce_fusion), channel_id=1, replica_groups=mesh['dp'=2,'ctx'=64,'head'=4] {'dp'}, use_global_device_ids=true, to_apply=%region_23.24 | all-reduce | flops 640 | bytes 5120 | tf_op jit(solution)/shard_map/psum | solution.py:278
  87.5 0.8 copy.235
  88.3 0.3 fusion.15
  88.6 0.3 fusion.13
  89.0 0.8 copy.234
  90.0 0.8 copy.236
  (102 shorter events, 9.1 us)
Async XLA Ops:
  0.6 0.7 copy-start.7
  3.4 0.9 %copy-start.5 = (bf16[1,128,640]{2,1,0:T(8,128)(2,1)S(1)}, bf16[1,128,640]{2,1,0:T(8,128)(2,1)}, u32[]{:S(2)}) copy-start(bf16[1,128,640]{2,1,0:T(8,128)(2,1)} %param.9) | copy-start | bytes 491524
  4.5 0.9 %copy-start = (bf16[1,128,640]{2,1,0:T(8,128)(2,1)S(1)}, bf16[1,128,640]{2,1,0:T(8,128)(2,1)}, u32[]{:S(2)}) copy-start(bf16[1,128,640]{2,1,0:T(8,128)(2,1)} %param.6) | copy-start | bytes 491524
  5.4 0.9 %copy-start.1 = (bf16[1,128,640]{2,1,0:T(8,128)(2,1)S(1)}, bf16[1,128,640]{2,1,0:T(8,128)(2,1)}, u32[]{:S(2)}) copy-start(bf16[1,128,640]{2,1,0:T(8,128)(2,1)} %param.7) | copy-start | bytes 491524
  6.3 0.9 %copy-start.2 = (bf16[1,128,640]{2,1,0:T(8,128)(2,1)S(1)}, bf16[1,128,640]{2,1,0:T(8,128)(2,1)}, u32[]{:S(2)}) copy-start(bf16[1,128,640]{2,1,0:T(8,128)(2,1)} %param.8) | copy-start | bytes 491524
  41.8 1.0 %copy-start.4 = (bf16[8,8,30,128]{3,2,1,0:T(8,128)(2,1)S(1)}, bf16[8,8,30,128]{3,2,1,0:T(8,128)(2,1)}, u32[]{:S(2)}) copy-start(bf16[8,8,30,128]{3,2,1,0:T(8,128)(2,1)} %get-tuple-element.10) | copy-start | bytes 1474564
  45.8 0.7 copy-start.6
  74.9 1.1 %copy-start.3 = (f32[4,16,768]{2,1,0:T(8,128)S(1)}, f32[4,16,768]{2,1,0:T(8,128)}, u32[]{:S(2)}) copy-start(f32[4,16,768]{2,1,0:T(8,128)} %get-tuple-element.11) | copy-start | bytes 589828

commit v9 on v5

--- a/solution.py
+++ b/solution.py
@@ -18,7 +18,7 @@
 
 
 def gather_kernel(
-    group, inner, mid_x, top_x, mid_out, top_out, stage,
+    group, inner, cores, mid_x, top_x, mid_out, top_out, stage,
     send_mid, recv_mid, send_a, recv_a, send_b, recv_b, local_sem,
 ):
     count = lax.axis_size("ctx")
@@ -26,6 +26,7 @@
     me = lax.axis_index("ctx")
     row = lax.axis_index("dp")
     col = lax.axis_index("head")
+    other = 1 - row
     lo = me % inner
     hi = me // inner
     base = me - me % group
@@ -40,9 +41,14 @@
     barrier = pltpu.get_barrier_semaphore()
     for j in range(1, inner):
         pl.semaphore_signal(barrier, 1, device_id=(row, inner_peer(j), col), device_id_type=mesh_ids)
+    if cores == 2:
+        for j in range(inner):
+            pl.semaphore_signal(
+                barrier, 1, device_id=(other, inner_peer(j), col), device_id_type=mesh_ids
+            )
     for j in range(1, outer):
         pl.semaphore_signal(barrier, 1, device_id=(row, outer_peer(j), col), device_id_type=mesh_ids)
-    pl.semaphore_wait(barrier, inner + outer - 2)
+    pl.semaphore_wait(barrier, inner + outer - 2 + (inner if cores == 2 else 0))
 
     def mid_copy(j):
         peer = base + lax.rem(me % group + j, group)
@@ -51,10 +57,10 @@
             device_id=(row, peer, col), device_id_type=mesh_ids,
         )
 
-    def copy_a(j):
+    def copy_a(c, j):
         return pltpu.make_async_remote_copy(
-            top_x, stage.at[j], send_a.at[j], recv_a.at[j],
-            device_id=(row, inner_peer(j), col), device_id_type=mesh_ids,
+            top_x, stage.at[c, j], send_a.at[c * inner + j], recv_a.at[c * inner + j],
+            device_id=(other if c else row, inner_peer(j), col), device_id_type=mesh_ids,
         )
 
     def copy_b(j):
@@ -63,16 +69,17 @@
             device_id=(row, outer_peer(j), col), device_id_type=mesh_ids,
         )
 
-    for j in range(1, inner):
-        copy_a(j).start()
+    peers_a = [(0, j) for j in range(1, inner)] + [(1, j) for j in range(inner) if cores == 2]
+    for c, j in peers_a:
+        copy_a(c, j).start()
     for j in range(1, group):
         mid_copy(j).start()
-    own = pltpu.make_async_copy(top_x, stage.at[0], local_sem)
+    own = pltpu.make_async_copy(top_x, stage.at[0, 0], local_sem)
     own.start()
     mid_out[0] = mid_x[...]
     own.wait()
-    for j in range(1, inner):
-        copy_a(j).wait()
+    for c, j in peers_a:
+        copy_a(c, j).wait()
     for j in range(1, outer):
         copy_b(j).start()
     top_out[0] = stage[...]
@@ -82,23 +89,23 @@
         copy_b(j).wait()
 
 
-def ctx_gather(mid_x, top_x, group, tag):
+def ctx_gather(mid_x, top_x, group, tag, cores=1):
     count = lax.axis_size("ctx")
     inner = RING
     return pl.pallas_call(
-        functools.partial(gather_kernel, group, inner),
+        functools.partial(gather_kernel, group, inner, cores),
         out_shape=(
             jax.ShapeDtypeStruct((group,) + mid_x.shape, mid_x.dtype),
-            jax.ShapeDtypeStruct((count // inner, inner) + top_x.shape, top_x.dtype),
+            jax.ShapeDtypeStruct((count // inner, cores, inner) + top_x.shape, top_x.dtype),
         ),
         in_specs=[pl.BlockSpec(memory_space=pltpu.VMEM)] * 2,
         out_specs=(pl.BlockSpec(memory_space=pltpu.VMEM),) * 2,
         scratch_shapes=[
-            pltpu.VMEM((inner,) + top_x.shape, top_x.dtype),
+            pltpu.VMEM((cores, inner) + top_x.shape, top_x.dtype),
             pltpu.SemaphoreType.DMA((group,)),
             pltpu.SemaphoreType.DMA((group,)),
-            pltpu.SemaphoreType.DMA((inner,)),
-            pltpu.SemaphoreType.DMA((inner,)),
+            pltpu.SemaphoreType.DMA((cores * inner,)),
+            pltpu.SemaphoreType.DMA((cores * inner,)),
             pltpu.SemaphoreType.DMA((count // inner,)),
             pltpu.SemaphoreType.DMA((count // inner,)),
             pltpu.SemaphoreType.DMA,
@@ -265,17 +272,18 @@
     top_grads = pack_grads(top_low, top_row_shift)
     gain_row = jnp.pad(gain_part, (0, top_grads.shape[1] - flat_width))[None]
     top_block = jnp.concatenate([top_grads, gain_row], 0)
-    mid_gathered, gathered = ctx_gather(
-        pack_grads(mid_low, mid_row_shift), lane_dense(top_block), SPAN, 1
-    )
-    gathered = gathered.reshape((-1,) + top_block.shape)
+    mid_gathered, both = ctx_gather(
+        pack_grads(mid_low, mid_row_shift), lane_dense(top_block), SPAN, 1, cores=2
+    )
+    both = both.reshape(both.shape[:3] + top_block.shape)
+    gathered = both[:, 0].reshape((-1,) + top_block.shape)
     mid_low_all, mid_shift_all = unpack_grads(
         mid_gathered.reshape(-1, mid_gathered.shape[-1]), head_count
     )
     top_low_all, top_shift_all = unpack_grads(
         gathered[:, :top_rows].reshape(-1, top_grads.shape[1]), head_count
     )
-    gain_grad = lax.psum(jnp.sum(gathered[:, top_rows, :flat_width], axis=0), "dp")
+    gain_grad = jnp.sum(both[:, :, :, top_rows, :flat_width], axis=(0, 1, 2))
 
     mid_grad, mid_soft = score_grads(
         mid_q, mid_k, mid_v, mid_total_all, mid_low_all, mid_shift_all

time: 89.5 us -> 108 us (1.21)
  Pallas kernels: 53.2 us -> 74 us
  blocking collectives: 6.9 us -> 0 us
  matrix products: 5.47 us -> 9.55 us
    pallas_call x2, Pallas kernels: 53.2 us -> 74 us  [ctx_gather(): pl.pallas_call(functools.partial(gather_kernel, group, inner, cores), out...]
    psum x1 -> x0, blocking collectives: 6.9 us -> none  [shards(): lax.psum(jnp.sum(gathered[:, top_rows, :flat_width], axis=0), 'dp')]
    unnamed x29 -> x45, local copies, waits for them, and re-layouts: 9.62 us -> 6.39 us
    dot_general x3, matrix products: 0.83 us -> 2.41 us  [score_grads(): jnp.einsum('qhe,khe->hqk', grad_low, v_rows, preferred_element_type=jnp.f...]
    dot_general x3, matrix products: 1.59 us -> 2.86 us  [key_parts(): jnp.einsum('hqk,qhe->khe', soft_low, grad_low, preferred_element_type=jnp...]
where the time goes in v9:
time: 108 us; the launch traced here: 107 us
  Pallas kernels  74 us (69%)
  local copies, waits for them, and re-layouts  16.3 us (15%)
  matrix products  9.55 us (9%)
  other arithmetic  6.39 us (6%)
  between operations  1.27 us (1%)
    pallas_call x2, Pallas kernels, ctx_gather(): pl.pallas_call(functools.partial(gather_kernel, group, inner, cores), out...  74 us
    unnamed x45, local copies, waits for them, and re-layouts  6.39 us
    dot_general x3, matrix products, key_parts(): jnp.einsum('hqk,qhe->khe', soft_low, grad_low, preferred_element_type=jnp...  2.86 us
    reduce_sum x6, other arithmetic, pick_rows(): return jnp.sum(chosen, axis=1, dtype=source_rows.dtype)  2.47 us
    dot_general x3, matrix products, score_grads(): jnp.einsum('qhe,khe->hqk', grad_low, v_rows, preferred_element_type=jnp.f...  2.41 us
    reshape x1, local copies, waits for them, and re-layouts, shards(): both = both.reshape(both.shape[:3] + top_block.shape)  2.35 us

profile of v9, /device:TPU:1, one launch (start us, length us, event | category | flops | bytes accessed | tf_op | source)
XLA Modules:
  0.0 107.4 jit_solution(17986310588501710324)
XLA Ops:
  0.7 0.8 slice_bitcast_fusion.5
  2.0 1.5 %fusion.30 = (bf16[16,5,128]{2,0,1:T(8,128)(2,1)S(1)}, bf16[16,5,128]{2,0,1:T(8,128)(2,1)S(1)}, bf16[16,5,128]{2,0,1:T(8,128)(2,1)S(1)}) fusion(pred[8,5]{0,1:T(8,128)(4,1)S(1)} %iota_compare_fusion.1, bf16[1,128,640]{2,1,0:T(8,128)(2,1)} %param.8, bf16[1,128,640]{2,1,0:T(8,128)(2,1)} %param.7, bf16[1,128,640]{2,1,0:T(8,128)(2,1)} %param.6), kind=kLoop, calls=%fused_computation.78 | loop fusion | flops 460800 | bytes 553000 | tf_op jit(solution)/shard_map/reduce_sum | solution.py:128
  3.5 0.6 pad_maximum_fusion.mid_x
  4.1 1.1 copy.196
  6.5 0.3 select_reduce_fusion.2
  6.9 0.6 reshape.372.top_x
  7.8 31.2 %shard_map.101 = (bf16[4,16,1920]{2,1,0:T(8,128)(2,1)}, bf16[8,1,8,30,128]{4,3,2,1,0:T(8,128)(2,1)}) custom-call(bf16[16,1920]{1,0:T(8,128)(2,1)} %pad_maximum_fusion.mid_x, bf16[30,128]{1,0:T(8,128)(2,1)} %reshape.372.top_x), custom_call_target="tpu_custom_call" | custom-call | tf_op jit(solution)/shard_map/pallas_call | solution.py:95
  39.1 1.0 slice_bitcast_fusion
  40.8 0.5 reshape.376
  42.0 0.3 fusion.64
  43.1 0.4 copy-done.8
  43.8 0.5 multiply_reduce_fusion.3
  44.3 0.3 multiply_reduce_fusion
  45.4 1.0 fusion.17
  46.9 0.6 reshape.385.top_x
  47.9 0.6 maximum_maximum_fusion.mid_x
  48.7 0.8 copy.233
  49.5 42.7 %shard_map.102 = (f32[4,16,768]{2,1,0:T(8,128)}, f32[8,2,8,18,128]{4,3,2,1,0:T(8,128)}) custom-call(f32[16,768]{1,0:T(8,128)} %maximum_maximum_fusion.mid_x, f32[18,128]{1,0:T(8,128)} %reshape.385.top_x), custom_call_target="tpu_custom_call" | custom-call | tf_op jit(solution)/shard_map/pallas_call | solution.py:95
  92.3 1.7 %convolution_bitcast_fusion.6 = f32[16,5,128]{2,0,1:T(8,128)} fusion(bf16[5,64,64]{1,2,0:T(8,128)(2,1)S(1)} %fusion.31, f32[64,768]{1,0:T(8,128)} %bitcast.262), kind=kOutput, calls=%fused_computation.33 | convolution fusion | flops 1310720 | bytes 143360 | tf_op jit(solution)/shard_map/hqk,qhe->khe/dot_general | solution.py:169
  93.9 0.8 slice_bitcast_fusion.4
  94.8 1.1 %fusion.20 = bf16[5,64,64]{1,2,0:T(8,128)(2,1)S(1)} fusion(f32[5,64,64]{1,2,0:T(8,128)S(1)} %get-tuple-element.64, f32[5,64]{1,0:T(8,128)S(1)} %copy.210, f32[5,64]{1,0:T(8,128)S(1)} %log_add_fusion.1, bf16[8,5,8,128]{3,2,1,0:T(8,128)(2,1)S(1)} %get-tuple-element.51, f32[64,768]{1,0:T(8,128)} %bitcast.264), kind=kOutput, calls=%fused_computation.32 | convolution fusion | flops 5345280 | bytes 289280 | tf_op jit(solution)/shard_map/qhe,khe->hqk/dot_general | solution.py:160
  95.9 0.7 convolution_bitcast_fusion.7
  96.6 0.8 convolution_bitcast_fusion.8
  97.5 2.3 %reshape.388 = f32[8,2,8,3,768]{4,3,2,1,0:T(4,128)S(1)} reshape(f32[8,2,8,18,128]{4,3,2,1,0:T(8,128)} %get-tuple-element.12) | data formatting | bytes 2359296 | tf_op jit(solution)/shard_map/reshape | solution.py:278
  99.8 1.0 slice_reduce_fusion
  101.1 0.3 reshape.389
  102.0 0.9 convolution_bitcast_fusion.10
  104.0 0.8 copy.235
  104.9 0.3 fusion.15
  105.2 0.3 fusion.13
  105.6 0.8 copy.234
  106.6 0.8 copy.236
  (121 shorter events, 8.5 us)
Async XLA Ops:
  0.6 5.1 %copy-start.6 = (bf16[1,128,640]{2,1,0:T(8,128)(2,1)S(1)}, bf16[1,128,640]{2,1,0:T(8,128)(2,1)}, u32[]{:S(2)}) copy-start(bf16[1,128,640]{2,1,0:T(8,128)(2,1)} %param.8) | copy-start | bytes 491524
  0.6 4.9 %copy-start.5 = (bf16[1,128,640]{2,1,0:T(8,128)(2,1)S(1)}, bf16[1,128,640]{2,1,0:T(8,128)(2,1)}, u32[]{:S(2)}) copy-start(bf16[1,128,640]{2,1,0:T(8,128)(2,1)} %param.7) | copy-start | bytes 491524
  0.7 4.7 %copy-start.4 = (bf16[1,128,640]{2,1,0:T(8,128)(2,1)S(1)}, bf16[1,128,640]{2,1,0:T(8,128)(2,1)}, u32[]{:S(2)}) copy-start(bf16[1,128,640]{2,1,0:T(8,128)(2,1)} %param.6) | copy-start | bytes 491524
  1.7 41.8 %copy-start.15 = (pred[128,5]{0,1:T(8,128)(4,1)}, pred[128,5]{0,1:T(8,128)(4,1)S(1)}, u32[]{:S(2)}) copy-start(pred[128,5]{0,1:T(8,128)(4,1)S(1)} %broadcast_in_dim.296) | copy-start | bytes 1924
  5.5 2.2 %copy-start.2 = (bf16[1,128,640]{1,2,0:T(8,128)(2,1)}, bf16[1,128,640]{1,2,0:T(8,128)(2,1)S(1)}, u32[]{:S(2)}) copy-start(bf16[1,128,640]{1,2,0:T(8,128)(2,1)S(1)} %copy.170) | copy-start | bytes 491524
  5.7 2.0 %copy-start = (bf16[1,128,640]{1,2,0:T(8,128)(2,1)}, bf16[1,128,640]{1,2,0:T(8,128)(2,1)S(1)}, u32[]{:S(2)}) copy-start(bf16[1,128,640]{1,2,0:T(8,128)(2,1)S(1)} %copy.171) | copy-start | bytes 491524
  39.1 1.8 %copy-start.9 = (bf16[8,1,8,30,128]{4,3,2,1,0:T(8,128)(2,1)S(1)}, bf16[8,1,8,30,128]{4,3,2,1,0:T(8,128)(2,1)}, u32[]{:S(2)}) copy-start(bf16[8,1,8,30,128]{4,3,2,1,0:T(8,128)(2,1)} %get-tuple-element.10) | copy-start | bytes 1474564
  40.8 1.4 %copy-start.10 = (f32[64,5,128]{2,0,1:T(8,128)}, f32[64,5,128]{2,0,1:T(8,128)S(1)}, u32[]{:S(2)}) copy-start(f32[64,5,128]{2,0,1:T(8,128)S(1)} %convolution_bitcast_fusion.5) | copy-start | bytes 491524
  42.3 1.5 %slice-start = ((f32[64,5,128]{2,0,1:T(8,128)}), f32[16,5,128]{2,0,1:T(8,128)S(1)}, s32[]{:S(2)}) async-start(f32[64,5,128]{2,0,1:T(8,128)} %copy-done.10), calls=%async_computation | async-start | bytes 81920 | tf_op jit(solution)/shard_map/slice | solution.py:228
  42.3 2.0 %copy-start.14 = (f32[640]{0:T(1024)S(1)}, f32[640]{0:T(1024)}, u32[]{:S(2)}) copy-start(f32[640]{0:T(1024)} %param.10) | copy-start | bytes 7684
  42.9 0.7 copy-start.8
  101.1 2.3 %copy-start.16 = (pred[128,5]{0,1:T(8,128)(4,1)S(1)}, pred[128,5]{0,1:T(8,128)(4,1)}, u32[]{:S(2)}) copy-start(pred[128,5]{0,1:T(8,128)(4,1)} %copy-done.15) | copy-start | bytes 1924
  101.4 2.2 %copy-start.3 = (bf16[1,128,640]{1,2,0:T(8,128)(2,1)S(1)}, bf16[1,128,640]{1,2,0:T(8,128)(2,1)}, u32[]{:S(2)}) copy-start(bf16[1,128,640]{1,2,0:T(8,128)(2,1)} %copy-done.2) | copy-start | bytes 491524
  101.4 2.2 %copy-start.7 = (bf16[5,128,128]{1,2,0:T(8,128)(2,1)S(1)}, bf16[5,128,128]{1,2,0:T(8,128)(2,1)}, u32[]{:S(2)}) copy-start(bf16[5,128,128]{1,2,0:T(8,128)(2,1)} %fusion.17) | copy-start | bytes 491524
  101.4 2.2 %copy-start.13 = (f32[16,5,128]{2,0,1:T(8,128)S(1)}, f32[16,5,128]{2,0,1:T(8,128)}, u32[]{:S(2)}) copy-start(f32[16,5,128]{2,0,1:T(8,128)} %convolution_bitcast_fusion.7) | copy-start | bytes 122884
  102.0 2.9 %copy-start.11 = (f32[16,5,128]{2,0,1:T(8,128)S(1)}, f32[16,5,128]{2,0,1:T(8,128)}, u32[]{:S(2)}) copy-start(f32[16,5,128]{2,0,1:T(8,128)} %convolution_bitcast_fusion.6) | copy-start | bytes 122884
  103.6 1.6 %copy-start.1 = (bf16[1,128,640]{1,2,0:T(8,128)(2,1)S(1)}, bf16[1,128,640]{1,2,0:T(8,128)(2,1)}, u32[]{:S(2)}) copy-start(bf16[1,128,640]{1,2,0:T(8,128)(2,1)} %copy-done) | copy-start | bytes 491524
  103.6 1.6 %copy-start.12 = (f32[16,5,128]{2,0,1:T(8,128)S(1)}, f32[16,5,128]{2,0,1:T(8,128)}, u32[]{:S(2)}) copy-start(f32[16,5,128]{2,0,1:T(8,128)} %convolution_bitcast_fusion.8) | copy-start | bytes 122884

commit v10 on v6

--- a/solution.py
+++ b/solution.py
@@ -280,8 +280,7 @@
     top_flat = jnp.concatenate(
         [top_low.reshape(-1), gain_high, gain_low, shift_high, shift_low]
     )
-    tile = 16 * HEAD_DIM
-    top_flat = jnp.pad(top_flat, (0, -top_flat.shape[0] % tile))
+    top_flat = jnp.pad(top_flat, (0, -top_flat.shape[0] % HEAD_DIM))
     mid_gathered, gathered = ctx_gather(
         pack_grads(mid_low, mid_row_shift, flat_width + HEAD_DIM),
         lane_dense(top_flat),

time: 89.3 us -> 86.2 us (0.965)
  Pallas kernels: 51.8 us -> 47.4 us
  blocking collectives: 7.13 us -> 10.5 us
  local copies, waits for them, and re-layouts: 17.1 us -> 15.6 us
    pallas_call x2, Pallas kernels: 51.8 us -> 47.4 us  [ctx_gather(): pl.pallas_call(functools.partial(gather_kernel, group, inner), out_shape=...]
    psum x1, blocking collectives: 7.13 us -> 10.5 us  [shards(): lax.psum(jnp.sum(join_wide(gain_cols[:, :flat_width], gain_cols[:, flat_w...]
    unnamed x49 -> x29, local copies, waits for them, and re-layouts: 11.4 us -> 9.88 us
where the time goes in v10:
time: 86.2 us; the launch traced here: 85.6 us
  Pallas kernels  47.4 us (55%)
  local copies, waits for them, and re-layouts  15.6 us (18%)
  blocking collectives  10.5 us (12%)
  other arithmetic  5.59 us (6%)
  matrix products  5.39 us (6%)
  between operations  1.08 us (1%)
    pallas_call x2, Pallas kernels, ctx_gather(): pl.pallas_call(functools.partial(gather_kernel, group, inner), out_shape=...  47.4 us
    psum x1, blocking collectives, shards(): lax.psum(jnp.sum(join_wide(gain_cols[:, :flat_width], gain_cols[:, flat_w...  10.5 us
    unnamed x29, local copies, waits for them, and re-layouts  9.88 us
    reduce_sum x6, other arithmetic, pick_rows(): return jnp.sum(chosen, axis=1, dtype=source_rows.dtype)  2.46 us

profile of v10, /device:TPU:1, one launch (start us, length us, event | category | flops | bytes accessed | tf_op | source)
XLA Modules:
  0.0 85.6 jit_solution(5506245929998160860)
XLA Ops:
  0.6 0.7 copy-done.8
  1.9 1.5 %fusion.30 = (bf16[16,5,128]{2,0,1:T(8,128)(2,1)S(1)}, bf16[16,5,128]{2,0,1:T(8,128)(2,1)S(1)}, bf16[16,5,128]{2,0,1:T(8,128)(2,1)S(1)}) fusion(pred[8,5]{0,1:T(8,128)(4,1)S(1)} %iota_compare_fusion.1, bf16[1,128,640]{2,1,0:T(8,128)(2,1)} %param.8, bf16[1,128,640]{2,1,0:T(8,128)(2,1)} %param.7, bf16[1,128,640]{2,1,0:T(8,128)(2,1)} %param.6), kind=kLoop, calls=%fused_computation.76 | loop fusion | flops 460800 | bytes 553000 | tf_op jit(solution)/shard_map/reduce_sum | solution.py:121
  3.4 0.6 pad_maximum_fusion.mid_x
  4.0 0.3 copy-done.5
  4.6 0.8 copy-done
  5.6 0.7 copy-done.1
  6.5 0.7 copy-done.2
  8.0 0.3 select_reduce_fusion.2
  8.3 0.6 reshape.373.top_x
  9.0 0.3 fusion.69
  9.3 31.2 %shard_map.101 = (bf16[4,16,1920]{2,1,0:T(8,128)(2,1)}, bf16[8,8,30,128]{3,2,1,0:T(8,128)(2,1)}) custom-call(bf16[16,1920]{1,0:T(8,128)(2,1)} %pad_maximum_fusion.mid_x, bf16[30,128]{1,0:T(8,128)(2,1)} %reshape.373.top_x), custom_call_target="tpu_custom_call" | custom-call | tf_op jit(solution)/shard_map/pallas_call | solution.py:88
  40.5 1.0 %slice_bitcast_fusion.1 = (bf16[8,5,8,128]{3,2,1,0:T(8,128)(2,1)S(1)}, bf16[8,5,8,128]{3,2,1,0:T(8,128)(2,1)S(1)}, bf16[8,5,8,128]{3,2,1,0:T(8,128)(2,1)S(1)}) fusion(bf16[64,1920]{1,0:T(8,128)(2,1)} %bitcast.270), kind=kLoop, calls=%fused_computation.93 | loop fusion | bytes 491520
  42.2 0.5 copy-done.3
  42.8 0.5 reshape.377
  43.9 0.3 fusion.67
  45.3 0.5 multiply_reduce_fusion.3
  45.8 0.7 copy-done.6
  46.5 0.3 multiply_reduce_fusion
  47.5 0.4 fusion.17
  48.5 0.6 pad_bitcast_fusion.top_x
  49.5 0.7 maximum_maximum_fusion.mid_x
  50.3 0.8 copy.230
  51.1 16.2 %shard_map.102 = (bf16[4,16,768]{2,1,0:T(8,128)(2,1)}, bf16[8,8,21,128]{3,2,1,0:T(8,128)(2,1)}) custom-call(bf16[16,768]{1,0:T(8,128)(2,1)} %maximum_maximum_fusion.mid_x, bf16[21,128]{1,0:T(8,128)(2,1)} %pad_bitcast_fusion.top_x), custom_call_target="tpu_custom_call" | custom-call | tf_op jit(solution)/shard_map/pallas_call | solution.py:88
  67.4 1.1 %convolution_bitcast_fusion.6 = f32[16,5,128]{2,0,1:T(8,128)S(1)} fusion(bf16[5,64,64]{1,2,0:T(8,128)(2,1)S(1)} %fusion.31, bf16[64,768]{1,0:T(8,128)(2,1)} %bitcast.278), kind=kOutput, calls=%fused_computation.33 | convolution fusion | flops 1310720 | bytes 143360 | tf_op jit(solution)/shard_map/hqk,qhe->khe/dot_general | solution.py:162
  69.2 0.5 copy-done.4
  69.7 10.5 %psum.7 = f32[640]{0:T(1024)} all-reduce(f32[640]{0:T(1024)S(1)} %add_reduce_fusion), channel_id=1, replica_groups=mesh['dp'=2,'ctx'=64,'head'=4] {'dp'}, use_global_device_ids=true, to_apply=%region_23.24 | all-reduce | flops 640 | bytes 5120 | tf_op jit(solution)/shard_map/psum | solution.py:297
  80.7 0.3 fusion.16
  82.2 0.8 copy.232
  83.0 0.3 fusion.15
  83.3 0.3 fusion.13
  83.8 0.8 copy.231
  84.8 0.8 copy.233
  (103 shorter events, 8.9 us)
Async XLA Ops:
  0.6 0.7 copy-start.8
  3.4 0.9 %copy-start.5 = (bf16[1,128,640]{2,1,0:T(8,128)(2,1)S(1)}, bf16[1,128,640]{2,1,0:T(8,128)(2,1)}, u32[]{:S(2)}) copy-start(bf16[1,128,640]{2,1,0:T(8,128)(2,1)} %param.9) | copy-start | bytes 491524
  4.5 0.9 %copy-start = (bf16[1,128,640]{2,1,0:T(8,128)(2,1)S(1)}, bf16[1,128,640]{2,1,0:T(8,128)(2,1)}, u32[]{:S(2)}) copy-start(bf16[1,128,640]{2,1,0:T(8,128)(2,1)} %param.6) | copy-start | bytes 491524
  5.4 0.9 %copy-start.1 = (bf16[1,128,640]{2,1,0:T(8,128)(2,1)S(1)}, bf16[1,128,640]{2,1,0:T(8,128)(2,1)}, u32[]{:S(2)}) copy-start(bf16[1,128,640]{2,1,0:T(8,128)(2,1)} %param.7) | copy-start | bytes 491524
  6.3 0.9 %copy-start.2 = (bf16[1,128,640]{2,1,0:T(8,128)(2,1)S(1)}, bf16[1,128,640]{2,1,0:T(8,128)(2,1)}, u32[]{:S(2)}) copy-start(bf16[1,128,640]{2,1,0:T(8,128)(2,1)} %param.8) | copy-start | bytes 491524
  41.7 1.0 %copy-start.3 = (bf16[8,8,30,128]{3,2,1,0:T(8,128)(2,1)S(1)}, bf16[8,8,30,128]{3,2,1,0:T(8,128)(2,1)}, u32[]{:S(2)}) copy-start(bf16[8,8,30,128]{3,2,1,0:T(8,128)(2,1)} %get-tuple-element.10) | copy-start | bytes 1474564
  45.8 0.7 copy-start.6
  67.4 1.1 %copy-start.7 = (bf16[4,16,768]{2,1,0:T(8,128)(2,1)S(1)}, bf16[4,16,768]{2,1,0:T(8,128)(2,1)}, u32[]{:S(2)}) copy-start(bf16[4,16,768]{2,1,0:T(8,128)(2,1)} %get-tuple-element.11) | copy-start | bytes 294916
  68.6 1.0 %copy-start.4 = (bf16[8,8,21,128]{3,2,1,0:T(8,128)(2,1)S(1)}, bf16[8,8,21,128]{3,2,1,0:T(8,128)(2,1)}, u32[]{:S(2)}) copy-start(bf16[8,8,21,128]{3,2,1,0:T(8,128)(2,1)} %get-tuple-element.12) | copy-start | bytes 1032196

commit v11 on v10

--- a/solution.py
+++ b/solution.py
@@ -17,10 +17,14 @@
 EPS = 1e-06
 
 
-def gather_kernel(
-    group, inner, mid_x, top_x, mid_out, top_out, stage,
-    send_mid, recv_mid, send_a, recv_a, send_b, recv_b, local_sem,
-):
+def gather_kernel(group, inner, has_sum, *refs):
+    if has_sum:
+        (mid_x, top_x, sum_x, mid_out, top_out, sum_out, stage, sum_stage, row_sum,
+         send_mid, recv_mid, send_a, recv_a, send_b, recv_b, local_sem,
+         send_sa, recv_sa, send_sb, recv_sb) = refs
+    else:
+        (mid_x, top_x, mid_out, top_out, stage,
+         send_mid, recv_mid, send_a, recv_a, send_b, recv_b, local_sem) = refs
     count = lax.axis_size("ctx")
     outer = count // inner
     me = lax.axis_index("ctx")
@@ -44,27 +48,31 @@
         pl.semaphore_signal(barrier, 1, device_id=(row, outer_peer(j), col), device_id_type=mesh_ids)
     pl.semaphore_wait(barrier, inner + outer - 2)
 
+    def remote(src, dst, send, recv, peer):
+        return pltpu.make_async_remote_copy(
+            src, dst, send, recv, device_id=(row, peer, col), device_id_type=mesh_ids
+        )
+
     def mid_copy(j):
         peer = base + lax.rem(me % group + j, group)
-        return pltpu.make_async_remote_copy(
-            mid_x, mid_out.at[j], send_mid.at[j], recv_mid.at[j],
-            device_id=(row, peer, col), device_id_type=mesh_ids,
-        )
+        return remote(mid_x, mid_out.at[j], send_mid.at[j], recv_mid.at[j], peer)
 
     def copy_a(j):
-        return pltpu.make_async_remote_copy(
-            top_x, stage.at[j], send_a.at[j], recv_a.at[j],
-            device_id=(row, inner_peer(j), col), device_id_type=mesh_ids,
-        )
+        return remote(top_x, stage.at[j], send_a.at[j], recv_a.at[j], inner_peer(j))
 
     def copy_b(j):
-        return pltpu.make_async_remote_copy(
-            stage, top_out.at[j], send_b.at[j], recv_b.at[j],
-            device_id=(row, outer_peer(j), col), device_id_type=mesh_ids,
-        )
+        return remote(stage, top_out.at[j], send_b.at[j], recv_b.at[j], outer_peer(j))
+
+    def sum_a(j):
+        return remote(sum_x, sum_stage.at[j], send_sa.at[j], recv_sa.at[j], inner_peer(j))
+
+    def sum_b(j):
+        return remote(row_sum, sum_out.at[j], send_sb.at[j], recv_sb.at[j], outer_peer(j))
 
     for j in range(1, inner):
         copy_a(j).start()
+        if has_sum:
+            sum_a(j).start()
     for j in range(1, group):
         mid_copy(j).start()
     own = pltpu.make_async_copy(top_x, stage.at[0], local_sem)
@@ -75,36 +83,65 @@
         copy_a(j).wait()
     for j in range(1, outer):
         copy_b(j).start()
+    if has_sum:
+        total = sum_x[...]
+        for j in range(1, inner):
+            sum_a(j).wait()
+            total = total + sum_stage[j]
+        row_sum[...] = total
+        for j in range(1, outer):
+            sum_b(j).start()
+        sum_out[0] = total
     top_out[0] = stage[...]
     for j in range(1, group):
         mid_copy(j).wait()
     for j in range(1, outer):
         copy_b(j).wait()
-
-
-def ctx_gather(mid_x, top_x, group, tag):
+        if has_sum:
+            sum_b(j).wait()
+
+
+def ctx_gather(mid_x, top_x, group, tag, sum_x=None):
     count = lax.axis_size("ctx")
     inner = RING
-    return pl.pallas_call(
-        functools.partial(gather_kernel, group, inner),
-        out_shape=(
-            jax.ShapeDtypeStruct((group,) + mid_x.shape, mid_x.dtype),
-            jax.ShapeDtypeStruct((count // inner, inner) + top_x.shape, top_x.dtype),
-        ),
-        in_specs=[pl.BlockSpec(memory_space=pltpu.VMEM)] * 2,
-        out_specs=(pl.BlockSpec(memory_space=pltpu.VMEM),) * 2,
-        scratch_shapes=[
-            pltpu.VMEM((inner,) + top_x.shape, top_x.dtype),
-            pltpu.SemaphoreType.DMA((group,)),
-            pltpu.SemaphoreType.DMA((group,)),
+    outer = count // inner
+    has_sum = sum_x is not None
+    operands = (mid_x, top_x) + ((sum_x,) if has_sum else ())
+    out_shape = (
+        jax.ShapeDtypeStruct((group,) + mid_x.shape, mid_x.dtype),
+        jax.ShapeDtypeStruct((outer, inner) + top_x.shape, top_x.dtype),
+    )
+    scratch = [pltpu.VMEM((inner,) + top_x.shape, top_x.dtype)]
+    if has_sum:
+        out_shape += (jax.ShapeDtypeStruct((outer,) + sum_x.shape, sum_x.dtype),)
+        scratch += [
+            pltpu.VMEM((inner,) + sum_x.shape, sum_x.dtype),
+            pltpu.VMEM(sum_x.shape, sum_x.dtype),
+        ]
+    scratch += [
+        pltpu.SemaphoreType.DMA((group,)),
+        pltpu.SemaphoreType.DMA((group,)),
+        pltpu.SemaphoreType.DMA((inner,)),
+        pltpu.SemaphoreType.DMA((inner,)),
+        pltpu.SemaphoreType.DMA((outer,)),
+        pltpu.SemaphoreType.DMA((outer,)),
+        pltpu.SemaphoreType.DMA,
+    ]
+    if has_sum:
+        scratch += [
             pltpu.SemaphoreType.DMA((inner,)),
             pltpu.SemaphoreType.DMA((inner,)),
-            pltpu.SemaphoreType.DMA((count // inner,)),
-            pltpu.SemaphoreType.DMA((count // inner,)),
-            pltpu.SemaphoreType.DMA,
-        ],
+            pltpu.SemaphoreType.DMA((outer,)),
+            pltpu.SemaphoreType.DMA((outer,)),
+        ]
+    return pl.pallas_call(
+        functools.partial(gather_kernel, group, inner, has_sum),
+        out_shape=out_shape,
+        in_specs=[pl.BlockSpec(memory_space=pltpu.VMEM)] * len(operands),
+        out_specs=(pl.BlockSpec(memory_space=pltpu.VMEM),) * len(out_shape),
+        scratch_shapes=scratch,
         compiler_params=pltpu.CompilerParams(collective_id=tag, has_side_effects=True),
-    )(mid_x, top_x)
+    )(*operands)
 
 
 def lane_dense(block):
@@ -275,17 +312,15 @@
     top_low = (top_sel[..., None] * pick_rows(grad_attn, ctx_size, top_shift)).astype(jnp.bfloat16)
     top_row_shift = -(top_sel * pick_rows(inner[..., None], ctx_size, top_shift)[..., 0])
 
-    gain_high, gain_low = split_wide(gain_part)
     shift_high, shift_low = split_wide(top_row_shift.reshape(-1))
-    top_flat = jnp.concatenate(
-        [top_low.reshape(-1), gain_high, gain_low, shift_high, shift_low]
-    )
+    top_flat = jnp.concatenate([top_low.reshape(-1), shift_high, shift_low])
     top_flat = jnp.pad(top_flat, (0, -top_flat.shape[0] % HEAD_DIM))
-    mid_gathered, gathered = ctx_gather(
+    mid_gathered, gathered, gain_rows_sum = ctx_gather(
         pack_grads(mid_low, mid_row_shift, flat_width + HEAD_DIM),
         lane_dense(top_flat),
         SPAN,
         1,
+        sum_x=lane_dense(gain_part),
     )
     mid_low_all, mid_shift_all = unpack_grads(
         mid_gathered.reshape(-1, mid_gathered.shape[-1]), head_count
@@ -293,15 +328,11 @@
     gathered = gathered.reshape(ctx_size, -1)
     grad_width = top_rows * flat_width
     top_low_all = gathered[:, :grad_width].reshape(-1, head_count, HEAD_DIM)
-    gain_cols = gathered[:, grad_width : grad_width + 2 * flat_width]
-    gain_grad = lax.psum(
-        jnp.sum(join_wide(gain_cols[:, :flat_width], gain_cols[:, flat_width:]), axis=0), "dp"
-    )
-    shift_start = grad_width + 2 * flat_width
+    gain_grad = lax.psum(jnp.sum(gain_rows_sum, axis=0).reshape(flat_width), "dp")
     shift_count = top_rows * head_count
     top_shift_all = join_wide(
-        gathered[:, shift_start : shift_start + shift_count],
-        gathered[:, shift_start + shift_count : shift_start + 2 * shift_count],
+        gathered[:, grad_width : grad_width + shift_count],
+        gathered[:, grad_width + shift_count : grad_width + 2 * shift_count],
     ).reshape(-1, head_count)
 
     mid_grad, mid_soft = score_grads(

time: 86.2 us -> 85.1 us (0.987)
  blocking collectives: 10.5 us -> 8.64 us
    psum x1, blocking collectives: 10.5 us -> 8.64 us  [shards(): lax.psum(jnp.sum(gain_rows_sum, axis=0).reshape(flat_width), 'dp')]
    unnamed x29 -> x31, local copies, waits for them, and re-layouts: 9.88 us -> 10 us
where the time goes in v11:
time: 85.1 us; the launch traced here: 84.5 us
  Pallas kernels  47.6 us (56%)
  local copies, waits for them, and re-layouts  15.7 us (18%)
  blocking collectives  8.64 us (10%)
  other arithmetic  6.05 us (7%)
  matrix products  5.38 us (6%)
  between operations  1.09 us (1%)
    pallas_call x2, Pallas kernels, ctx_gather(): pl.pallas_call(functools.partial(gather_kernel, group, inner, has_sum), o...  47.6 us
    unnamed x31, local copies, waits for them, and re-layouts  10 us
    psum x1, blocking collectives, shards(): lax.psum(jnp.sum(gain_rows_sum, axis=0).reshape(flat_width), 'dp')  8.64 us
    reduce_sum x6, other arithmetic, pick_rows(): return jnp.sum(chosen, axis=1, dtype=source_rows.dtype)  2.47 us

profile of v11, /device:TPU:1, one launch (start us, length us, event | category | flops | bytes accessed | tf_op | source)
XLA Modules:
  0.0 84.5 jit_solution(9819047494386831168)
XLA Ops:
  0.6 0.7 copy-done.9
  1.9 1.5 %fusion.30 = (bf16[16,5,128]{2,0,1:T(8,128)(2,1)S(1)}, bf16[16,5,128]{2,0,1:T(8,128)(2,1)S(1)}, bf16[16,5,128]{2,0,1:T(8,128)(2,1)S(1)}) fusion(pred[8,5]{0,1:T(8,128)(4,1)S(1)} %iota_compare_fusion.1, bf16[1,128,640]{2,1,0:T(8,128)(2,1)} %param.8, bf16[1,128,640]{2,1,0:T(8,128)(2,1)} %param.7, bf16[1,128,640]{2,1,0:T(8,128)(2,1)} %param.6), kind=kLoop, calls=%fused_computation.76 | loop fusion | flops 460800 | bytes 553000 | tf_op jit(solution)/shard_map/reduce_sum | solution.py:158
  3.4 0.6 pad_maximum_fusion.refs_0_
  4.0 0.3 copy-done.5
  4.6 0.8 copy-done
  5.6 0.7 copy-done.1
  6.5 0.7 copy-done.2
  8.0 0.3 select_reduce_fusion.2
  8.3 0.6 reshape.373.refs_1_
  9.0 0.3 fusion.68
  9.3 31.2 %shard_map.101 = (bf16[4,16,1920]{2,1,0:T(8,128)(2,1)}, bf16[8,8,30,128]{3,2,1,0:T(8,128)(2,1)}) custom-call(bf16[16,1920]{1,0:T(8,128)(2,1)} %pad_maximum_fusion.refs_0_, bf16[30,128]{1,0:T(8,128)(2,1)} %reshape.373.refs_1_), custom_call_target="tpu_custom_call" | custom-call | tf_op jit(solution)/shard_map/pallas_call | solution.py:137
  40.5 1.0 %slice_bitcast_fusion.1 = (bf16[8,5,8,128]{3,2,1,0:T(8,128)(2,1)S(1)}, bf16[8,5,8,128]{3,2,1,0:T(8,128)(2,1)S(1)}, bf16[8,5,8,128]{3,2,1,0:T(8,128)(2,1)S(1)}) fusion(bf16[64,1920]{1,0:T(8,128)(2,1)} %bitcast.264), kind=kLoop, calls=%fused_computation.92 | loop fusion | bytes 491520
  42.2 0.5 copy-done.3
  42.8 0.5 reshape.377
  43.9 0.3 fusion.66
  45.3 0.5 multiply_reduce_fusion.3
  45.8 0.7 copy-done.7
  46.5 0.8 multiply_reduce_fusion
  47.9 0.4 fusion.17
  49.0 0.6 pad_bitcast_fusion.refs_1_
  49.9 0.7 maximum_maximum_fusion.refs_0_
  50.8 0.8 copy.230
  51.6 16.4 %shard_map.102 = (bf16[4,16,768]{2,1,0:T(8,128)(2,1)}, bf16[8,8,11,128]{3,2,1,0:T(8,128)(2,1)}, f32[8,5,128]{2,1,0:T(8,128)}) custom-call(bf16[16,768]{1,0:T(8,128)(2,1)} %maximum_maximum_fusion.refs_0_, bf16[11,128]{1,0:T(8,128)(2,1)} %pad_bitcast_fusion.refs_1_, f32[5,128]{1,0:T(8,128)} %get-tuple-element.30.refs_2_), custom_call_target="tpu_custom_call" | custom-call | tf_op jit(solution)/shard_map/pallas_call | solution.py:137
  68.0 1.1 %convolution_bitcast_fusion.6 = f32[16,5,128]{2,0,1:T(8,128)S(1)} fusion(bf16[5,64,64]{1,2,0:T(8,128)(2,1)S(1)} %fusion.31, bf16[64,768]{1,0:T(8,128)(2,1)} %bitcast.273), kind=kOutput, calls=%fused_computation.33 | convolution fusion | flops 1310720 | bytes 143360 | tf_op jit(solution)/shard_map/hqk,qhe->khe/dot_general | solution.py:199
  69.1 8.6 %psum.7 = f32[640]{0:T(1024)} all-reduce(f32[640]{0:T(1024)S(1)} %bitcast.272), channel_id=1, replica_groups=mesh['dp'=2,'ctx'=64,'head'=4] {'dp'}, use_global_device_ids=true, to_apply=%region_23.24 | all-reduce | flops 640 | bytes 5120 | tf_op jit(solution)/shard_map/psum | solution.py:331
  78.5 0.6 copy-done.4
  79.6 0.3 fusion.16
  81.1 0.8 copy.232
  81.9 0.3 fusion.15
  82.2 0.3 fusion.13
  82.7 0.8 copy.231
  83.7 0.8 copy.233
  (104 shorter events, 8.9 us)
Async XLA Ops:
  0.6 0.7 copy-start.9
  3.4 0.9 %copy-start.5 = (bf16[1,128,640]{2,1,0:T(8,128)(2,1)S(1)}, bf16[1,128,640]{2,1,0:T(8,128)(2,1)}, u32[]{:S(2)}) copy-start(bf16[1,128,640]{2,1,0:T(8,128)(2,1)} %param.9) | copy-start | bytes 491524
  4.5 0.9 %copy-start = (bf16[1,128,640]{2,1,0:T(8,128)(2,1)S(1)}, bf16[1,128,640]{2,1,0:T(8,128)(2,1)}, u32[]{:S(2)}) copy-start(bf16[1,128,640]{2,1,0:T(8,128)(2,1)} %param.6) | copy-start | bytes 491524
  5.4 0.9 %copy-start.1 = (bf16[1,128,640]{2,1,0:T(8,128)(2,1)S(1)}, bf16[1,128,640]{2,1,0:T(8,128)(2,1)}, u32[]{:S(2)}) copy-start(bf16[1,128,640]{2,1,0:T(8,128)(2,1)} %param.7) | copy-start | bytes 491524
  6.3 0.9 %copy-start.2 = (bf16[1,128,640]{2,1,0:T(8,128)(2,1)S(1)}, bf16[1,128,640]{2,1,0:T(8,128)(2,1)}, u32[]{:S(2)}) copy-start(bf16[1,128,640]{2,1,0:T(8,128)(2,1)} %param.8) | copy-start | bytes 491524
  41.7 1.0 %copy-start.3 = (bf16[8,8,30,128]{3,2,1,0:T(8,128)(2,1)S(1)}, bf16[8,8,30,128]{3,2,1,0:T(8,128)(2,1)}, u32[]{:S(2)}) copy-start(bf16[8,8,30,128]{3,2,1,0:T(8,128)(2,1)} %get-tuple-element.11) | copy-start | bytes 1474564
  45.8 0.7 copy-start.7
  68.0 1.1 %copy-start.6 = (f32[8,5,128]{2,1,0:T(8,128)S(1)}, f32[8,5,128]{2,1,0:T(8,128)}, u32[]{:S(2)}) copy-start(f32[8,5,128]{2,1,0:T(8,128)} %get-tuple-element.14) | copy-start | bytes 61444
  68.0 9.8 %copy-start.8 = (bf16[4,16,768]{2,1,0:T(8,128)(2,1)S(1)}, bf16[4,16,768]{2,1,0:T(8,128)(2,1)}, u32[]{:S(2)}) copy-start(bf16[4,16,768]{2,1,0:T(8,128)(2,1)} %get-tuple-element.12) | copy-start | bytes 294916
  78.1 1.0 %copy-start.4 = (bf16[8,8,11,128]{3,2,1,0:T(8,128)(2,1)S(1)}, bf16[8,8,11,128]{3,2,1,0:T(8,128)(2,1)}, u32[]{:S(2)}) copy-start(bf16[8,8,11,128]{3,2,1,0:T(8,128)(2,1)} %get-tuple-element.13) | copy-start | bytes 540676

commit v12 on v11

--- a/solution.py
+++ b/solution.py
@@ -19,12 +19,14 @@
 
 def gather_kernel(group, inner, has_sum, *refs):
     if has_sum:
-        (mid_x, top_x, sum_x, mid_out, top_out, sum_out, stage, sum_stage, row_sum,
-         send_mid, recv_mid, send_a, recv_a, send_b, recv_b, local_sem,
-         send_sa, recv_sa, send_sb, recv_sb) = refs
+        (mid_x, top_y, top_z, sum_x, mid_out, out_y, out_z, sum_out,
+         stage_y, stage_z, sum_stage, row_sum, *sems) = refs
     else:
-        (mid_x, top_x, mid_out, top_out, stage,
-         send_mid, recv_mid, send_a, recv_a, send_b, recv_b, local_sem) = refs
+        (mid_x, top_y, top_z, mid_out, out_y, out_z, stage_y, stage_z, *sems) = refs
+    (send_mid, recv_mid, send_ay, recv_ay, send_by, recv_by,
+     send_az, recv_az, send_bz, recv_bz, local_sem) = sems[:11]
+    if has_sum:
+        send_sa, recv_sa, send_sb, recv_sb = sems[11:]
     count = lax.axis_size("ctx")
     outer = count // inner
     me = lax.axis_index("ctx")
@@ -57,11 +59,17 @@
         peer = base + lax.rem(me % group + j, group)
         return remote(mid_x, mid_out.at[j], send_mid.at[j], recv_mid.at[j], peer)
 
-    def copy_a(j):
-        return remote(top_x, stage.at[j], send_a.at[j], recv_a.at[j], inner_peer(j))
-
-    def copy_b(j):
-        return remote(stage, top_out.at[j], send_b.at[j], recv_b.at[j], outer_peer(j))
+    def copy_ay(j):
+        return remote(top_y, stage_y.at[j], send_ay.at[j], recv_ay.at[j], inner_peer(j))
+
+    def copy_by(j):
+        return remote(stage_y, out_y.at[j], send_by.at[j], recv_by.at[j], outer_peer(j))
+
+    def copy_az(j):
+        return remote(top_z, stage_z.at[j], send_az.at[j], recv_az.at[j], outer_peer(j))
+
+    def copy_bz(j):
+        return remote(stage_z, out_z.at[j], send_bz.at[j], recv_bz.at[j], inner_peer(j))
 
     def sum_a(j):
         return remote(sum_x, sum_stage.at[j], send_sa.at[j], recv_sa.at[j], inner_peer(j))
@@ -70,19 +78,29 @@
         return remote(row_sum, sum_out.at[j], send_sb.at[j], recv_sb.at[j], outer_peer(j))
 
     for j in range(1, inner):
-        copy_a(j).start()
-        if has_sum:
+        copy_ay(j).start()
+    for j in range(1, outer):
+        copy_az(j).start()
+    if has_sum:
+        for j in range(1, inner):
             sum_a(j).start()
     for j in range(1, group):
         mid_copy(j).start()
-    own = pltpu.make_async_copy(top_x, stage.at[0], local_sem)
-    own.start()
+    own_y = pltpu.make_async_copy(top_y, stage_y.at[0], local_sem.at[0])
+    own_z = pltpu.make_async_copy(top_z, stage_z.at[0], local_sem.at[1])
+    own_y.start()
+    own_z.start()
     mid_out[0] = mid_x[...]
-    own.wait()
+    own_y.wait()
+    own_z.wait()
     for j in range(1, inner):
-        copy_a(j).wait()
+        copy_ay(j).wait()
     for j in range(1, outer):
-        copy_b(j).start()
+        copy_by(j).start()
+    for j in range(1, outer):
+        copy_az(j).wait()
+    for j in range(1, inner):
+        copy_bz(j).start()
     if has_sum:
         total = sum_x[...]
         for j in range(1, inner):
@@ -92,49 +110,49 @@
         for j in range(1, outer):
             sum_b(j).start()
         sum_out[0] = total
-    top_out[0] = stage[...]
+    out_y[0] = stage_y[...]
+    out_z[0] = stage_z[...]
     for j in range(1, group):
         mid_copy(j).wait()
     for j in range(1, outer):
-        copy_b(j).wait()
+        copy_by(j).wait()
         if has_sum:
             sum_b(j).wait()
+    for j in range(1, inner):
+        copy_bz(j).wait()
 
 
 def ctx_gather(mid_x, top_x, group, tag, sum_x=None):
     count = lax.axis_size("ctx")
     inner = RING
     outer = count // inner
+    half = (top_x.shape[0] + 1) // 2
+    top_y = top_x[:half]
+    top_z = top_x[half:]
     has_sum = sum_x is not None
-    operands = (mid_x, top_x) + ((sum_x,) if has_sum else ())
+    operands = (mid_x, top_y, top_z) + ((sum_x,) if has_sum else ())
     out_shape = (
         jax.ShapeDtypeStruct((group,) + mid_x.shape, mid_x.dtype),
-        jax.ShapeDtypeStruct((outer, inner) + top_x.shape, top_x.dtype),
-    )
-    scratch = [pltpu.VMEM((inner,) + top_x.shape, top_x.dtype)]
+        jax.ShapeDtypeStruct((outer, inner) + top_y.shape, top_x.dtype),
+        jax.ShapeDtypeStruct((inner, outer) + top_z.shape, top_x.dtype),
+    )
+    scratch = [
+        pltpu.VMEM((inner,) + top_y.shape, top_x.dtype),
+        pltpu.VMEM((outer,) + top_z.shape, top_x.dtype),
+    ]
     if has_sum:
         out_shape += (jax.ShapeDtypeStruct((outer,) + sum_x.shape, sum_x.dtype),)
         scratch += [
             pltpu.VMEM((inner,) + sum_x.shape, sum_x.dtype),
             pltpu.VMEM(sum_x.shape, sum_x.dtype),
         ]
-    scratch += [
-        pltpu.SemaphoreType.DMA((group,)),
-        pltpu.SemaphoreType.DMA((group,)),
-        pltpu.SemaphoreType.DMA((inner,)),
-        pltpu.SemaphoreType.DMA((inner,)),
-        pltpu.SemaphoreType.DMA((outer,)),
-        pltpu.SemaphoreType.DMA((outer,)),
-        pltpu.SemaphoreType.DMA,
-    ]
-    if has_sum:
-        scratch += [
-            pltpu.SemaphoreType.DMA((inner,)),
-            pltpu.SemaphoreType.DMA((inner,)),
-            pltpu.SemaphoreType.DMA((outer,)),
-            pltpu.SemaphoreType.DMA((outer,)),
-        ]
-    return pl.pallas_call(
+    for size in (group, inner, outer, outer, inner):
+        scratch += [pltpu.SemaphoreType.DMA((size,)), pltpu.SemaphoreType.DMA((size,))]
+    scratch.append(pltpu.SemaphoreType.DMA((2,)))
+    if has_sum:
+        for size in (inner, outer):
+            scratch += [pltpu.SemaphoreType.DMA((size,)), pltpu.SemaphoreType.DMA((size,))]
+    outs = pl.pallas_call(
         functools.partial(gather_kernel, group, inner, has_sum),
         out_shape=out_shape,
         in_specs=[pl.BlockSpec(memory_space=pltpu.VMEM)] * len(operands),
@@ -142,6 +160,8 @@
         scratch_shapes=scratch,
         compiler_params=pltpu.CompilerParams(collective_id=tag, has_side_effects=True),
     )(*operands)
+    top_all = jnp.concatenate([outs[1], jnp.transpose(outs[2], (1, 0, 2, 3))], 2)
+    return (outs[0], top_all) + tuple(outs[3:])
 
 
 def lane_dense(block):

time: 85.1 us -> 80.7 us (0.948)
  Pallas kernels: 47.6 us -> 44.1 us
  blocking collectives: 8.64 us -> 6.35 us
  other arithmetic: 6.05 us -> 6.95 us
    pallas_call x2, Pallas kernels: 47.6 us -> 44.1 us  [ctx_gather(): pl.pallas_call(functools.partial(gather_kernel, group, inner, has_sum), o...]
    psum x1, blocking collectives: 8.64 us -> 6.35 us  [shards(): lax.psum(jnp.sum(gain_rows_sum, axis=0).reshape(flat_width), 'dp')]
    slice x0 -> x2, local copies, waits for them, and re-layouts: none -> 1.23 us  [ctx_gather(): top_z = top_x[half:]]
    reshape x3 -> x0, local copies, waits for them, and re-layouts: 1.23 us -> none  [the longest x2 1.22 us: lane_dense(): return block.reshape(-1, HEAD_DIM)]
    unnamed x31 -> x36, local copies, waits for them, and re-layouts: 10 us -> 10.4 us
where the time goes in v12:
time: 80.7 us; the launch traced here: 80.1 us
  Pallas kernels  44.1 us (55%)
  local copies, waits for them, and re-layouts  16.2 us (20%)
  other arithmetic  6.95 us (9%)
  blocking collectives  6.35 us (8%)
  matrix products  5.38 us (7%)
  between operations  1.11 us (1%)
    pallas_call x2, Pallas kernels, ctx_gather(): pl.pallas_call(functools.partial(gather_kernel, group, inner, has_sum), o...  44.1 us
    unnamed x36, local copies, waits for them, and re-layouts  10.4 us
    psum x1, blocking collectives, shards(): lax.psum(jnp.sum(gain_rows_sum, axis=0).reshape(flat_width), 'dp')  6.35 us
    reduce_sum x6, other arithmetic, pick_rows(): return jnp.sum(chosen, axis=1, dtype=source_rows.dtype)  2.46 us

profile of v12, /device:TPU:1, one launch (start us, length us, event | category | flops | bytes accessed | tf_op | source)
XLA Modules:
  0.0 80.1 jit_solution(11804919681781327756)
XLA Ops:
  0.6 0.7 copy-done.11
  1.9 1.5 %fusion.30 = (bf16[16,5,128]{2,0,1:T(8,128)(2,1)S(1)}, bf16[16,5,128]{2,0,1:T(8,128)(2,1)S(1)}, bf16[16,5,128]{2,0,1:T(8,128)(2,1)S(1)}) fusion(pred[8,5]{0,1:T(8,128)(4,1)S(1)} %iota_compare_fusion.1, bf16[1,128,640]{2,1,0:T(8,128)(2,1)} %param.8, bf16[1,128,640]{2,1,0:T(8,128)(2,1)} %param.7, bf16[1,128,640]{2,1,0:T(8,128)(2,1)} %param.6), kind=kLoop, calls=%fused_computation.78 | loop fusion | flops 460800 | bytes 553000 | tf_op jit(solution)/shard_map/reduce_sum | solution.py:178
  3.4 0.6 pad_maximum_fusion.1.refs_0_
  4.0 0.3 copy-done.5
  4.6 0.8 copy-done
  5.6 0.7 copy-done.1
  6.5 0.7 copy-done.2
  8.0 0.3 select_reduce_fusion
  8.3 0.6 slice_reduce_fusion
  9.3 29.1 %shard_map.101 = (bf16[4,16,1920]{2,1,0:T(8,128)(2,1)}, bf16[8,8,15,128]{3,2,1,0:T(8,128)(2,1)}, bf16[8,8,15,128]{3,2,1,0:T(8,128)(2,1)}) custom-call(bf16[16,1920]{1,0:T(8,128)(2,1)} %pad_maximum_fusion.1.refs_0_, bf16[15,128]{1,0:T(8,128)(2,1)} %bitcast.283, bf16[15,128]{1,0:T(8,128)(2,1)} %bitcast.282), custom_call_target="tpu_custom_call" | custom-call | tf_op jit(solution)/shard_map/pallas_call | solution.py:155
  38.5 1.0 %slice_bitcast_fusion.1 = (bf16[8,5,8,128]{3,2,1,0:T(8,128)(2,1)S(1)}, bf16[8,5,8,128]{3,2,1,0:T(8,128)(2,1)S(1)}, bf16[8,5,8,128]{3,2,1,0:T(8,128)(2,1)S(1)}) fusion(bf16[64,1920]{1,0:T(8,128)(2,1)} %bitcast.273), kind=kLoop, calls=%fused_computation.94 | loop fusion | bytes 491520
  40.2 0.7 copy-done.4
  41.1 0.5 reshape.388
  42.3 0.3 fusion.69
  43.6 0.5 multiply_reduce_fusion.3
  44.2 0.7 copy-done.9
  44.8 0.8 multiply_reduce_fusion
  46.3 0.4 fusion.17
  47.3 0.7 fusion.59.refs_1_
  48.1 0.6 fusion.62.refs_2_
  49.0 0.7 maximum_maximum_fusion.refs_0_
  49.9 0.8 %copy.243 = bf16[1,128,640]{2,1,0:T(8,128)(2,1)} copy(bf16[1,128,640]{1,2,0:T(8,128)(2,1)S(1)} %bitcast.266) | data formatting | bytes 327680
  50.7 15.0 %shard_map.102 = (bf16[4,16,768]{2,1,0:T(8,128)(2,1)}, bf16[8,8,6,128]{3,2,1,0:T(8,128)(2,1)}, bf16[8,8,5,128]{3,2,1,0:T(8,128)(2,1)}, f32[8,5,128]{2,1,0:T(8,128)}) custom-call(bf16[16,768]{1,0:T(8,128)(2,1)} %maximum_maximum_fusion.refs_0_, bf16[6,128]{1,0:T(8,128)(2,1)} %fusion.59.refs_1_, bf16[5,128]{1,0:T(8,128)(2,1)} %fusion.62.refs_2_, ...), custom_call_target="tpu_custom_call" | custom-call | tf_op jit(solution)/shard_map/pallas_call | solution.py:155
  65.7 1.1 %convolution_bitcast_fusion.6 = f32[16,5,128]{2,0,1:T(8,128)S(1)} fusion(bf16[5,64,64]{1,2,0:T(8,128)(2,1)S(1)} %fusion.31, bf16[64,768]{1,0:T(8,128)(2,1)} %bitcast.284), kind=kOutput, calls=%fused_computation.33 | convolution fusion | flops 1310720 | bytes 143360 | tf_op jit(solution)/shard_map/hqk,qhe->khe/dot_general | solution.py:219
  66.8 6.3 %psum.7 = f32[640]{0:T(1024)} all-reduce(f32[640]{0:T(1024)S(1)} %bitcast.281), channel_id=1, replica_groups=mesh['dp'=2,'ctx'=64,'head'=4] {'dp'}, use_global_device_ids=true, to_apply=%region_23.24 | all-reduce | flops 640 | bytes 5120 | tf_op jit(solution)/shard_map/psum | solution.py:351
  73.9 0.6 copy-done.7
  75.2 0.3 fusion.16
  76.7 0.8 %copy.245 = bf16[1,128,640]{2,1,0:T(8,128)(2,1)} copy(bf16[1,128,640]{1,2,0:T(8,128)(2,1)S(1)} %bitcast.267) | data formatting | bytes 327680
  77.5 0.3 fusion.15
  77.9 0.3 fusion.13
  78.3 0.8 %copy.244 = bf16[1,128,640]{2,1,0:T(8,128)(2,1)} copy(bf16[1,128,640]{1,2,0:T(8,128)(2,1)S(1)} %bitcast.268) | data formatting | bytes 327680
  79.3 0.8 %copy.246 = bf16[1,128,640]{2,1,0:T(8,128)(2,1)} copy(bf16[1,128,640]{1,2,0:T(8,128)(2,1)S(1)} %bitcast.269) | data formatting | bytes 327680
  (113 shorter events, 9.8 us)
Async XLA Ops:
  0.6 0.7 copy-start.11
  3.4 0.9 %copy-start.5 = (bf16[1,128,640]{2,1,0:T(8,128)(2,1)S(1)}, bf16[1,128,640]{2,1,0:T(8,128)(2,1)}, u32[]{:S(2)}) copy-start(bf16[1,128,640]{2,1,0:T(8,128)(2,1)} %param.9) | copy-start | bytes 491524
  4.5 0.9 %copy-start = (bf16[1,128,640]{2,1,0:T(8,128)(2,1)S(1)}, bf16[1,128,640]{2,1,0:T(8,128)(2,1)}, u32[]{:S(2)}) copy-start(bf16[1,128,640]{2,1,0:T(8,128)(2,1)} %param.6) | copy-start | bytes 491524
  5.4 0.9 %copy-start.1 = (bf16[1,128,640]{2,1,0:T(8,128)(2,1)S(1)}, bf16[1,128,640]{2,1,0:T(8,128)(2,1)}, u32[]{:S(2)}) copy-start(bf16[1,128,640]{2,1,0:T(8,128)(2,1)} %param.7) | copy-start | bytes 491524
  6.3 0.9 %copy-start.2 = (bf16[1,128,640]{2,1,0:T(8,128)(2,1)S(1)}, bf16[1,128,640]{2,1,0:T(8,128)(2,1)}, u32[]{:S(2)}) copy-start(bf16[1,128,640]{2,1,0:T(8,128)(2,1)} %param.8) | copy-start | bytes 491524
  39.9 1.0 %copy-start.4 = (bf16[8,8,15,128]{3,2,1,0:T(8,128)(2,1)S(1)}, bf16[8,8,15,128]{3,2,1,0:T(8,128)(2,1)}, u32[]{:S(2)}) copy-start(bf16[8,8,15,128]{3,2,1,0:T(8,128)(2,1)} %get-tuple-element.14) | copy-start | bytes 737284
  39.9 1.0 %copy-start.3 = (bf16[8,8,15,128]{3,2,1,0:T(8,128)(2,1)S(1)}, bf16[8,8,15,128]{3,2,1,0:T(8,128)(2,1)}, u32[]{:S(2)}) copy-start(bf16[8,8,15,128]{3,2,1,0:T(8,128)(2,1)} %get-tuple-element.13) | copy-start | bytes 737284
  44.1 0.7 copy-start.9
  65.7 1.1 %copy-start.8 = (f32[8,5,128]{2,1,0:T(8,128)S(1)}, f32[8,5,128]{2,1,0:T(8,128)}, u32[]{:S(2)}) copy-start(f32[8,5,128]{2,1,0:T(8,128)} %get-tuple-element.18) | copy-start | bytes 61444
  65.7 7.5 %copy-start.10 = (bf16[4,16,768]{2,1,0:T(8,128)(2,1)S(1)}, bf16[4,16,768]{2,1,0:T(8,128)(2,1)}, u32[]{:S(2)}) copy-start(bf16[4,16,768]{2,1,0:T(8,128)(2,1)} %get-tuple-element.15) | copy-start | bytes 294916
  73.5 0.9 %copy-start.7 = (bf16[8,8,5,128]{3,2,1,0:T(8,128)(2,1)S(1)}, bf16[8,8,5,128]{3,2,1,0:T(8,128)(2,1)}, u32[]{:S(2)}) copy-start(bf16[8,8,5,128]{3,2,1,0:T(8,128)(2,1)} %get-tuple-element.17) | copy-start | bytes 245764
  73.7 0.9 %copy-start.6 = (bf16[8,8,6,128]{3,2,1,0:T(8,128)(2,1)S(1)}, bf16[8,8,6,128]{3,2,1,0:T(8,128)(2,1)}, u32[]{:S(2)}) copy-start(bf16[8,8,6,128]{3,2,1,0:T(8,128)(2,1)} %get-tuple-element.16) | copy-start | bytes 294916

commit v13 on v12

--- a/solution.py
+++ b/solution.py
@@ -126,7 +126,8 @@
     count = lax.axis_size("ctx")
     inner = RING
     outer = count // inner
-    half = (top_x.shape[0] + 1) // 2
+    rows = top_x.shape[0]
+    half = max(1, min(rows - 1, 8 * round(0.75 * rows / 8)))
     top_y = top_x[:half]
     top_z = top_x[half:]
     has_sum = sum_x is not None

time: 80.7 us -> 82.6 us (1.024)
  blocking collectives: 6.35 us -> 7.67 us
    psum x1, blocking collectives: 6.35 us -> 7.67 us  [shards(): lax.psum(jnp.sum(gain_rows_sum, axis=0).reshape(flat_width), 'dp')]
    unnamed x36 -> x35, local copies, waits for them, and re-layouts: 10.4 us -> 10.3 us
where the time goes in v13:
time: 82.6 us; the launch traced here: 82 us
  Pallas kernels  44.4 us (54%)
  local copies, waits for them, and re-layouts  16.6 us (20%)
  blocking collectives  7.67 us (9%)
  other arithmetic  6.82 us (8%)
  matrix products  5.38 us (7%)
  between operations  1.11 us (1%)
    pallas_call x2, Pallas kernels, ctx_gather(): pl.pallas_call(functools.partial(gather_kernel, group, inner, has_sum), o...  44.4 us
    unnamed x35, local copies, waits for them, and re-layouts  10.3 us
    psum x1, blocking collectives, shards(): lax.psum(jnp.sum(gain_rows_sum, axis=0).reshape(flat_width), 'dp')  7.67 us
    reduce_sum x6, other arithmetic, pick_rows(): return jnp.sum(chosen, axis=1, dtype=source_rows.dtype)  2.47 us

profile of v13, /device:TPU:1, one launch (start us, length us, event | category | flops | bytes accessed | tf_op | source)
XLA Modules:
  0.0 82.0 jit_solution(1660533590383779779)
XLA Ops:
  0.6 0.7 copy-done.11
  1.9 1.5 %fusion.30 = (bf16[16,5,128]{2,0,1:T(8,128)(2,1)S(1)}, bf16[16,5,128]{2,0,1:T(8,128)(2,1)S(1)}, bf16[16,5,128]{2,0,1:T(8,128)(2,1)S(1)}) fusion(pred[8,5]{0,1:T(8,128)(4,1)S(1)} %iota_compare_fusion.1, bf16[1,128,640]{2,1,0:T(8,128)(2,1)} %param.8, bf16[1,128,640]{2,1,0:T(8,128)(2,1)} %param.7, bf16[1,128,640]{2,1,0:T(8,128)(2,1)} %param.6), kind=kLoop, calls=%fused_computation.78 | loop fusion | flops 460800 | bytes 553000 | tf_op jit(solution)/shard_map/reduce_sum | solution.py:179
  3.4 0.6 pad_maximum_fusion.1.refs_0_
  4.0 0.3 copy-done.4
  4.6 0.8 copy-done
  5.6 0.7 copy-done.1
  6.5 0.7 copy-done.2
  8.0 0.3 select_reduce_fusion.2
  8.4 0.6 slice.131.refs_2_
  8.9 0.6 slice.130.refs_1_
  9.9 28.0 %shard_map.101 = (bf16[4,16,1920]{2,1,0:T(8,128)(2,1)}, bf16[8,8,24,128]{3,2,1,0:T(8,128)(2,1)}, bf16[8,8,6,128]{3,2,1,0:T(8,128)(2,1)}) custom-call(bf16[16,1920]{1,0:T(8,128)(2,1)} %pad_maximum_fusion.1.refs_0_, bf16[24,128]{1,0:T(8,128)(2,1)} %slice.130.refs_1_, bf16[6,128]{1,0:T(8,128)(2,1)} %slice.131.refs_2_), custom_call_target="tpu_custom_call" | custom-call | tf_op jit(solution)/shard_map/pallas_call | solution.py:156
  37.9 1.0 %slice_bitcast_fusion.1 = (bf16[8,5,8,128]{3,2,1,0:T(8,128)(2,1)S(1)}, bf16[8,5,8,128]{3,2,1,0:T(8,128)(2,1)S(1)}, bf16[8,5,8,128]{3,2,1,0:T(8,128)(2,1)S(1)}) fusion(bf16[64,1920]{1,0:T(8,128)(2,1)} %bitcast.274), kind=kLoop, calls=%fused_computation.94 | loop fusion | bytes 491520
  39.6 0.5 copy-done.3
  40.4 0.5 reshape.389
  41.5 0.3 fusion.69
  42.9 0.5 multiply_reduce_fusion.3
  43.4 0.7 copy-done.9
  44.1 0.8 multiply_reduce_fusion
  45.6 0.4 fusion.17
  46.6 0.7 fusion.59.refs_1_
  47.3 0.6 fusion.65.refs_2_
  48.3 0.7 maximum_maximum_fusion.refs_0_
  49.1 0.8 %copy.240 = bf16[1,128,640]{2,1,0:T(8,128)(2,1)} copy(bf16[1,128,640]{1,2,0:T(8,128)(2,1)S(1)} %bitcast.268) | data formatting | bytes 327680
  49.9 16.4 %shard_map.102 = (bf16[4,16,768]{2,1,0:T(8,128)(2,1)}, bf16[8,8,8,128]{3,2,1,0:T(8,128)(2,1)}, bf16[8,8,3,128]{3,2,1,0:T(4,128)(2,1)}, f32[8,5,128]{2,1,0:T(8,128)}) custom-call(bf16[16,768]{1,0:T(8,128)(2,1)} %maximum_maximum_fusion.refs_0_, bf16[8,128]{1,0:T(8,128)(2,1)} %fusion.59.refs_1_, bf16[3,128]{1,0:T(4,128)(2,1)} %fusion.65.refs_2_, ...), custom_call_target="tpu_custom_call" | custom-call | tf_op jit(solution)/shard_map/pallas_call | solution.py:156
  66.4 1.1 %convolution_bitcast_fusion.6 = f32[16,5,128]{2,0,1:T(8,128)S(1)} fusion(bf16[5,64,64]{1,2,0:T(8,128)(2,1)S(1)} %fusion.31, bf16[64,768]{1,0:T(8,128)(2,1)} %bitcast.283), kind=kOutput, calls=%fused_computation.33 | convolution fusion | flops 1310720 | bytes 143360 | tf_op jit(solution)/shard_map/hqk,qhe->khe/dot_general | solution.py:220
  67.5 7.7 %psum.7 = f32[640]{0:T(1024)} all-reduce(f32[640]{0:T(1024)S(1)} %bitcast.282), channel_id=1, replica_groups=mesh['dp'=2,'ctx'=64,'head'=4] {'dp'}, use_global_device_ids=true, to_apply=%region_23.24 | all-reduce | flops 640 | bytes 5120 | tf_op jit(solution)/shard_map/psum | solution.py:352
  75.8 0.7 copy-done.5
  78.6 0.8 %copy.242 = bf16[1,128,640]{2,1,0:T(8,128)(2,1)} copy(bf16[1,128,640]{1,2,0:T(8,128)(2,1)S(1)} %bitcast.269) | data formatting | bytes 327680
  79.5 0.3 fusion.15
  79.8 0.3 fusion.13
  80.2 0.8 %copy.241 = bf16[1,128,640]{2,1,0:T(8,128)(2,1)} copy(bf16[1,128,640]{1,2,0:T(8,128)(2,1)S(1)} %bitcast.270) | data formatting | bytes 327680
  81.2 0.8 %copy.243 = bf16[1,128,640]{2,1,0:T(8,128)(2,1)} copy(bf16[1,128,640]{1,2,0:T(8,128)(2,1)S(1)} %bitcast.271) | data formatting | bytes 327680
  (114 shorter events, 9.8 us)
Async XLA Ops:
  0.6 0.7 copy-start.11
  3.4 0.9 %copy-start.4 = (bf16[1,128,640]{2,1,0:T(8,128)(2,1)S(1)}, bf16[1,128,640]{2,1,0:T(8,128)(2,1)}, u32[]{:S(2)}) copy-start(bf16[1,128,640]{2,1,0:T(8,128)(2,1)} %param.9) | copy-start | bytes 491524
  4.5 0.9 %copy-start = (bf16[1,128,640]{2,1,0:T(8,128)(2,1)S(1)}, bf16[1,128,640]{2,1,0:T(8,128)(2,1)}, u32[]{:S(2)}) copy-start(bf16[1,128,640]{2,1,0:T(8,128)(2,1)} %param.6) | copy-start | bytes 491524
  5.4 0.9 %copy-start.1 = (bf16[1,128,640]{2,1,0:T(8,128)(2,1)S(1)}, bf16[1,128,640]{2,1,0:T(8,128)(2,1)}, u32[]{:S(2)}) copy-start(bf16[1,128,640]{2,1,0:T(8,128)(2,1)} %param.7) | copy-start | bytes 491524
  6.3 0.9 %copy-start.2 = (bf16[1,128,640]{2,1,0:T(8,128)(2,1)S(1)}, bf16[1,128,640]{2,1,0:T(8,128)(2,1)}, u32[]{:S(2)}) copy-start(bf16[1,128,640]{2,1,0:T(8,128)(2,1)} %param.8) | copy-start | bytes 491524
  39.2 1.0 %copy-start.3 = (bf16[8,8,24,128]{3,2,1,0:T(8,128)(2,1)S(1)}, bf16[8,8,24,128]{3,2,1,0:T(8,128)(2,1)}, u32[]{:S(2)}) copy-start(bf16[8,8,24,128]{3,2,1,0:T(8,128)(2,1)} %get-tuple-element.13) | copy-start | bytes 1179652
  39.4 0.9 %copy-start.6 = (bf16[8,8,6,128]{3,2,1,0:T(8,128)(2,1)S(1)}, bf16[8,8,6,128]{3,2,1,0:T(8,128)(2,1)}, u32[]{:S(2)}) copy-start(bf16[8,8,6,128]{3,2,1,0:T(8,128)(2,1)} %get-tuple-element.14) | copy-start | bytes 294916
  43.4 0.7 copy-start.9
  66.3 1.1 %copy-start.8 = (f32[8,5,128]{2,1,0:T(8,128)S(1)}, f32[8,5,128]{2,1,0:T(8,128)}, u32[]{:S(2)}) copy-start(f32[8,5,128]{2,1,0:T(8,128)} %get-tuple-element.18) | copy-start | bytes 61444
  66.4 8.8 %copy-start.10 = (bf16[4,16,768]{2,1,0:T(8,128)(2,1)S(1)}, bf16[4,16,768]{2,1,0:T(8,128)(2,1)}, u32[]{:S(2)}) copy-start(bf16[4,16,768]{2,1,0:T(8,128)(2,1)} %get-tuple-element.15) | copy-start | bytes 294916
  75.6 0.9 %copy-start.5 = (bf16[8,8,8,128]{3,2,1,0:T(8,128)(2,1)S(1)}, bf16[8,8,8,128]{3,2,1,0:T(8,128)(2,1)}, u32[]{:S(2)}) copy-start(bf16[8,8,8,128]{3,2,1,0:T(8,128)(2,1)} %get-tuple-element.16) | copy-start | bytes 393220
  75.6 0.9 %copy-start.7 = (bf16[8,8,3,128]{3,2,1,0:T(4,128)(2,1)S(1)}, bf16[8,8,3,128]{3,2,1,0:T(4,128)(2,1)}, u32[]{:S(2)}) copy-start(bf16[8,8,3,128]{3,2,1,0:T(4,128)(2,1)} %get-tuple-element.17) | copy-start | bytes 147460

commit v14 on v13

--- a/solution.py
+++ b/solution.py
@@ -127,7 +127,7 @@
     inner = RING
     outer = count // inner
     rows = top_x.shape[0]
-    half = max(1, min(rows - 1, 8 * round(0.75 * rows / 8)))
+    half = max(1, min(rows - 1, 8 * round(0.25 * rows / 8)))
     top_y = top_x[:half]
     top_z = top_x[half:]
     has_sum = sum_x is not None

time: 82.6 us -> 84.8 us (1.027)
  Pallas kernels: 44.4 us -> 49.6 us
  blocking collectives: 7.67 us -> 4.88 us
    pallas_call x2, Pallas kernels: 44.4 us -> 49.6 us  [ctx_gather(): pl.pallas_call(functools.partial(gather_kernel, group, inner, has_sum), o...]
    psum x1, blocking collectives: 7.67 us -> 4.88 us  [shards(): lax.psum(jnp.sum(gain_rows_sum, axis=0).reshape(flat_width), 'dp')]
    unnamed x35 -> x34, local copies, waits for them, and re-layouts: 10.3 us -> 10.1 us
where the time goes in v14:
time: 84.8 us; the launch traced here: 84.3 us
  Pallas kernels  49.6 us (58%)
  local copies, waits for them, and re-layouts  17.1 us (20%)
  other arithmetic  6.23 us (7%)
  matrix products  5.39 us (6%)
  blocking collectives  4.88 us (6%)
  between operations  1.12 us (1%)
    pallas_call x2, Pallas kernels, ctx_gather(): pl.pallas_call(functools.partial(gather_kernel, group, inner, has_sum), o...  49.6 us
    unnamed x34, local copies, waits for them, and re-layouts  10.1 us
    psum x1, blocking collectives, shards(): lax.psum(jnp.sum(gain_rows_sum, axis=0).reshape(flat_width), 'dp')  4.88 us
    reduce_sum x6, other arithmetic, pick_rows(): return jnp.sum(chosen, axis=1, dtype=source_rows.dtype)  2.46 us

profile of v14, /device:TPU:1, one launch (start us, length us, event | category | flops | bytes accessed | tf_op | source)
XLA Modules:
  0.0 84.3 jit_solution(11204607570193647591)
XLA Ops:
  0.6 0.7 copy-done.11
  1.9 1.5 %fusion.30 = (bf16[16,5,128]{2,0,1:T(8,128)(2,1)S(1)}, bf16[16,5,128]{2,0,1:T(8,128)(2,1)S(1)}, bf16[16,5,128]{2,0,1:T(8,128)(2,1)S(1)}) fusion(pred[8,5]{0,1:T(8,128)(4,1)S(1)} %iota_compare_fusion.1, bf16[1,128,640]{2,1,0:T(8,128)(2,1)} %param.8, bf16[1,128,640]{2,1,0:T(8,128)(2,1)} %param.7, bf16[1,128,640]{2,1,0:T(8,128)(2,1)} %param.6), kind=kLoop, calls=%fused_computation.78 | loop fusion | flops 460800 | bytes 553000 | tf_op jit(solution)/shard_map/reduce_sum | solution.py:179
  3.4 0.6 pad_maximum_fusion.2.refs_0_
  4.0 0.3 copy-done.5
  4.6 0.8 copy-done
  5.6 0.7 copy-done.1
  6.5 0.7 copy-done.2
  8.0 0.3 select_reduce_fusion.2
  8.4 0.6 slice.130.refs_1_
  8.9 0.6 slice.131.refs_2_
  9.9 30.5 %shard_map.101 = (bf16[4,16,1920]{2,1,0:T(8,128)(2,1)}, bf16[8,8,8,128]{3,2,1,0:T(8,128)(2,1)}, bf16[8,8,22,128]{3,2,1,0:T(8,128)(2,1)}) custom-call(bf16[16,1920]{1,0:T(8,128)(2,1)} %pad_maximum_fusion.2.refs_0_, bf16[8,128]{1,0:T(8,128)(2,1)} %slice.130.refs_1_, bf16[22,128]{1,0:T(8,128)(2,1)} %slice.131.refs_2_), custom_call_target="tpu_custom_call" | custom-call | tf_op jit(solution)/shard_map/pallas_call | solution.py:156
  40.4 1.0 %slice_bitcast_fusion.1 = (bf16[8,5,8,128]{3,2,1,0:T(8,128)(2,1)S(1)}, bf16[8,5,8,128]{3,2,1,0:T(8,128)(2,1)S(1)}, bf16[8,5,8,128]{3,2,1,0:T(8,128)(2,1)S(1)}) fusion(bf16[64,1920]{1,0:T(8,128)(2,1)} %bitcast.268), kind=kLoop, calls=%fused_computation.94 | loop fusion | bytes 491520
  42.1 0.5 copy-done.3
  42.9 0.5 reshape.385
  44.0 0.3 fusion.66
  45.4 0.5 multiply_reduce_fusion.3
  45.9 0.7 copy-done.9
  46.6 0.8 multiply_reduce_fusion
  48.1 0.4 fusion.17
  49.0 0.5 slice_bitcast_fusion.5.refs_1_
  49.6 0.6 slice_bitcast_fusion.4.refs_2_
  50.6 0.7 maximum_maximum_fusion.refs_0_
  51.4 0.8 copy.243
  52.3 19.1 %shard_map.102 = (bf16[4,16,768]{2,1,0:T(8,128)(2,1)}, bf16[8,8,1,128]{3,2,1,0:T(2,128)(2,1)}, bf16[8,8,10,128]{3,2,1,0:T(8,128)(2,1)}, f32[8,5,128]{2,1,0:T(8,128)}) custom-call(bf16[16,768]{1,0:T(8,128)(2,1)} %maximum_maximum_fusion.refs_0_, bf16[1,128]{1,0:T(2,128)(2,1)} %slice_bitcast_fusion.5.refs_1_, bf16[10,128]{1,0:T(8,128)(2,1)} %slice_bitcast_fusion.4.refs_2_, ...), custom_call_target="tpu_custom_call" | custom-call | tf_op jit(solution)/shard_map/pallas_call | solution.py:156
  71.4 1.1 %convolution_bitcast_fusion.6 = f32[16,5,128]{2,0,1:T(8,128)S(1)} fusion(bf16[5,64,64]{1,2,0:T(8,128)(2,1)S(1)} %fusion.31, bf16[64,768]{1,0:T(8,128)(2,1)} %bitcast.277), kind=kOutput, calls=%fused_computation.33 | convolution fusion | flops 1310720 | bytes 143360 | tf_op jit(solution)/shard_map/hqk,qhe->khe/dot_general | solution.py:220
  72.5 4.9 %psum.7 = f32[640]{0:T(1024)} all-reduce(f32[640]{0:T(1024)S(1)} %bitcast.276), channel_id=1, replica_groups=mesh['dp'=2,'ctx'=64,'head'=4] {'dp'}, use_global_device_ids=true, to_apply=%region_23.24 | all-reduce | flops 640 | bytes 5120 | tf_op jit(solution)/shard_map/psum | solution.py:352
  78.1 0.6 copy-done.4
  80.9 0.8 copy.245
  81.7 0.3 fusion.15
  82.0 0.3 fusion.13
  82.5 0.8 copy.244
  83.5 0.8 copy.246
  (114 shorter events, 9.9 us)
Async XLA Ops:
  0.6 0.7 copy-start.11
  3.4 0.9 %copy-start.5 = (bf16[1,128,640]{2,1,0:T(8,128)(2,1)S(1)}, bf16[1,128,640]{2,1,0:T(8,128)(2,1)}, u32[]{:S(2)}) copy-start(bf16[1,128,640]{2,1,0:T(8,128)(2,1)} %param.9) | copy-start | bytes 491524
  4.5 0.9 %copy-start = (bf16[1,128,640]{2,1,0:T(8,128)(2,1)S(1)}, bf16[1,128,640]{2,1,0:T(8,128)(2,1)}, u32[]{:S(2)}) copy-start(bf16[1,128,640]{2,1,0:T(8,128)(2,1)} %param.6) | copy-start | bytes 491524
  5.4 0.9 %copy-start.1 = (bf16[1,128,640]{2,1,0:T(8,128)(2,1)S(1)}, bf16[1,128,640]{2,1,0:T(8,128)(2,1)}, u32[]{:S(2)}) copy-start(bf16[1,128,640]{2,1,0:T(8,128)(2,1)} %param.7) | copy-start | bytes 491524
  6.3 0.9 %copy-start.2 = (bf16[1,128,640]{2,1,0:T(8,128)(2,1)S(1)}, bf16[1,128,640]{2,1,0:T(8,128)(2,1)}, u32[]{:S(2)}) copy-start(bf16[1,128,640]{2,1,0:T(8,128)(2,1)} %param.8) | copy-start | bytes 491524
  41.6 1.0 %copy-start.3 = (bf16[8,8,22,128]{3,2,1,0:T(8,128)(2,1)S(1)}, bf16[8,8,22,128]{3,2,1,0:T(8,128)(2,1)}, u32[]{:S(2)}) copy-start(bf16[8,8,22,128]{3,2,1,0:T(8,128)(2,1)} %get-tuple-element.14) | copy-start | bytes 1081348
  41.8 0.9 %copy-start.6 = (bf16[8,8,8,128]{3,2,1,0:T(8,128)(2,1)S(1)}, bf16[8,8,8,128]{3,2,1,0:T(8,128)(2,1)}, u32[]{:S(2)}) copy-start(bf16[8,8,8,128]{3,2,1,0:T(8,128)(2,1)} %get-tuple-element.13) | copy-start | bytes 393220
  45.9 0.7 copy-start.9
  71.3 1.1 %copy-start.8 = (f32[8,5,128]{2,1,0:T(8,128)S(1)}, f32[8,5,128]{2,1,0:T(8,128)}, u32[]{:S(2)}) copy-start(f32[8,5,128]{2,1,0:T(8,128)} %get-tuple-element.18) | copy-start | bytes 61444
  71.3 6.0 %copy-start.10 = (bf16[4,16,768]{2,1,0:T(8,128)(2,1)S(1)}, bf16[4,16,768]{2,1,0:T(8,128)(2,1)}, u32[]{:S(2)}) copy-start(bf16[4,16,768]{2,1,0:T(8,128)(2,1)} %get-tuple-element.15) | copy-start | bytes 294916
  77.7 1.0 %copy-start.4 = (bf16[8,8,10,128]{3,2,1,0:T(8,128)(2,1)S(1)}, bf16[8,8,10,128]{3,2,1,0:T(8,128)(2,1)}, u32[]{:S(2)}) copy-start(bf16[8,8,10,128]{3,2,1,0:T(8,128)(2,1)} %get-tuple-element.17) | copy-start | bytes 491524
  77.8 0.8 copy-start.7

commit v15 on v12

--- a/solution.py
+++ b/solution.py
@@ -48,11 +48,17 @@
         pl.semaphore_signal(barrier, 1, device_id=(row, inner_peer(j), col), device_id_type=mesh_ids)
     for j in range(1, outer):
         pl.semaphore_signal(barrier, 1, device_id=(row, outer_peer(j), col), device_id_type=mesh_ids)
-    pl.semaphore_wait(barrier, inner + outer - 2)
-
-    def remote(src, dst, send, recv, peer):
+    if has_sum:
+        for j in range(outer):
+            pl.semaphore_signal(
+                barrier, 1, device_id=(1 - row, outer_peer(j), col), device_id_type=mesh_ids
+            )
+    pl.semaphore_wait(barrier, inner + outer - 2 + (outer if has_sum else 0))
+
+    def remote(src, dst, send, recv, peer, core=None):
         return pltpu.make_async_remote_copy(
-            src, dst, send, recv, device_id=(row, peer, col), device_id_type=mesh_ids
+            src, dst, send, recv, device_id=(row if core is None else core, peer, col),
+            device_id_type=mesh_ids,
         )
 
     def mid_copy(j):
@@ -74,8 +80,14 @@
     def sum_a(j):
         return remote(sum_x, sum_stage.at[j], send_sa.at[j], recv_sa.at[j], inner_peer(j))
 
-    def sum_b(j):
-        return remote(row_sum, sum_out.at[j], send_sb.at[j], recv_sb.at[j], outer_peer(j))
+    def sum_b(c, j):
+        slot = c * outer + j
+        return remote(
+            row_sum, sum_out.at[c, j], send_sb.at[slot], recv_sb.at[slot], outer_peer(j),
+            core=(1 - row) if c else row,
+        )
+
+    sum_peers = [(0, j) for j in range(1, outer)] + [(1, j) for j in range(outer)]
 
     for j in range(1, inner):
         copy_ay(j).start()
@@ -107,17 +119,18 @@
             sum_a(j).wait()
             total = total + sum_stage[j]
         row_sum[...] = total
-        for j in range(1, outer):
-            sum_b(j).start()
-        sum_out[0] = total
+        for c, j in sum_peers:
+            sum_b(c, j).start()
+        sum_out[0, 0] = total
     out_y[0] = stage_y[...]
     out_z[0] = stage_z[...]
     for j in range(1, group):
         mid_copy(j).wait()
     for j in range(1, outer):
         copy_by(j).wait()
-        if has_sum:
-            sum_b(j).wait()
+    if has_sum:
+        for c, j in sum_peers:
+            sum_b(c, j).wait()
     for j in range(1, inner):
         copy_bz(j).wait()
 
@@ -141,7 +154,7 @@
         pltpu.VMEM((outer,) + top_z.shape, top_x.dtype),
     ]
     if has_sum:
-        out_shape += (jax.ShapeDtypeStruct((outer,) + sum_x.shape, sum_x.dtype),)
+        out_shape += (jax.ShapeDtypeStruct((2, outer) + sum_x.shape, sum_x.dtype),)
         scratch += [
             pltpu.VMEM((inner,) + sum_x.shape, sum_x.dtype),
             pltpu.VMEM(sum_x.shape, sum_x.dtype),
@@ -150,7 +163,7 @@
         scratch += [pltpu.SemaphoreType.DMA((size,)), pltpu.SemaphoreType.DMA((size,))]
     scratch.append(pltpu.SemaphoreType.DMA((2,)))
     if has_sum:
-        for size in (inner, outer):
+        for size in (inner, 2 * outer):
             scratch += [pltpu.SemaphoreType.DMA((size,)), pltpu.SemaphoreType.DMA((size,))]
     outs = pl.pallas_call(
         functools.partial(gather_kernel, group, inner, has_sum),
@@ -348,7 +361,7 @@
     gathered = gathered.reshape(ctx_size, -1)
     grad_width = top_rows * flat_width
     top_low_all = gathered[:, :grad_width].reshape(-1, head_count, HEAD_DIM)
-    gain_grad = lax.psum(jnp.sum(gain_rows_sum, axis=0).reshape(flat_width), "dp")
+    gain_grad = jnp.sum(gain_rows_sum, axis=(0, 1)).reshape(flat_width)
     shift_count = top_rows * head_count
     top_shift_all = join_wide(
         gathered[:, grad_width : grad_width + shift_count],

time: 80.7 us -> 78.7 us (0.975)
  blocking collectives: 6.35 us -> 0 us
  Pallas kernels: 44.1 us -> 47.9 us
    psum x1 -> x0, blocking collectives: 6.35 us -> none  [shards(): lax.psum(jnp.sum(gain_rows_sum, axis=0).reshape(flat_width), 'dp')]
    pallas_call x2, Pallas kernels: 44.1 us -> 47.9 us  [ctx_gather(): pl.pallas_call(functools.partial(gather_kernel, group, inner, has_sum), o...]
where the time goes in v15:
time: 78.7 us; the launch traced here: 78.2 us
  Pallas kernels  47.9 us (61%)
  local copies, waits for them, and re-layouts  16.2 us (21%)
  other arithmetic  7.56 us (10%)
  matrix products  5.39 us (7%)
  between operations  1.1 us (1%)
    pallas_call x2, Pallas kernels, ctx_gather(): pl.pallas_call(functools.partial(gather_kernel, group, inner, has_sum), o...  47.9 us
    unnamed x36, local copies, waits for them, and re-layouts  10.4 us
    reduce_sum x6, other arithmetic, pick_rows(): return jnp.sum(chosen, axis=1, dtype=source_rows.dtype)  2.46 us

profile of v15, /device:TPU:1, one launch (start us, length us, event | category | flops | bytes accessed | tf_op | source)
XLA Modules:
  0.0 78.2 jit_solution(4003400545391464556)
XLA Ops:
  0.6 0.7 copy-done.11
  1.9 1.5 %fusion.30 = (bf16[16,5,128]{2,0,1:T(8,128)(2,1)S(1)}, bf16[16,5,128]{2,0,1:T(8,128)(2,1)S(1)}, bf16[16,5,128]{2,0,1:T(8,128)(2,1)S(1)}) fusion(pred[8,5]{0,1:T(8,128)(4,1)S(1)} %iota_compare_fusion.1, bf16[1,128,640]{2,1,0:T(8,128)(2,1)} %param.8, bf16[1,128,640]{2,1,0:T(8,128)(2,1)} %param.7, bf16[1,128,640]{2,1,0:T(8,128)(2,1)} %param.6), kind=kLoop, calls=%fused_computation.78 | loop fusion | flops 460800 | bytes 553000 | tf_op jit(solution)/shard_map/reduce_sum | solution.py:191
  3.4 0.6 pad_maximum_fusion.1.refs_0_
  4.0 0.3 copy-done.5
  4.6 0.8 copy-done
  5.6 0.7 copy-done.1
  6.5 0.7 copy-done.2
  8.0 0.3 select_reduce_fusion
  8.3 0.6 slice_reduce_fusion
  9.3 29.1 %shard_map.101 = (bf16[4,16,1920]{2,1,0:T(8,128)(2,1)}, bf16[8,8,15,128]{3,2,1,0:T(8,128)(2,1)}, bf16[8,8,15,128]{3,2,1,0:T(8,128)(2,1)}) custom-call(bf16[16,1920]{1,0:T(8,128)(2,1)} %pad_maximum_fusion.1.refs_0_, bf16[15,128]{1,0:T(8,128)(2,1)} %bitcast.282, bf16[15,128]{1,0:T(8,128)(2,1)} %bitcast.281), custom_call_target="tpu_custom_call" | custom-call | tf_op jit(solution)/shard_map/pallas_call | solution.py:168
  38.5 1.0 %slice_bitcast_fusion.1 = (bf16[8,5,8,128]{3,2,1,0:T(8,128)(2,1)S(1)}, bf16[8,5,8,128]{3,2,1,0:T(8,128)(2,1)S(1)}, bf16[8,5,8,128]{3,2,1,0:T(8,128)(2,1)S(1)}) fusion(bf16[64,1920]{1,0:T(8,128)(2,1)} %bitcast.273), kind=kLoop, calls=%fused_computation.94 | loop fusion | bytes 491520
  40.2 0.7 copy-done.4
  41.1 0.5 reshape.388
  42.3 0.3 fusion.69
  43.6 0.5 multiply_reduce_fusion.3
  44.2 0.7 copy-done.9
  44.8 0.8 multiply_reduce_fusion
  46.3 0.4 fusion.17
  47.3 0.7 fusion.59.refs_1_
  48.1 0.6 fusion.62.refs_2_
  49.0 0.7 maximum_maximum_fusion.refs_0_
  49.9 0.8 %copy.243 = bf16[1,128,640]{2,1,0:T(8,128)(2,1)} copy(bf16[1,128,640]{1,2,0:T(8,128)(2,1)S(1)} %bitcast.266) | data formatting | bytes 327680
  50.7 18.8 %shard_map.102 = (bf16[4,16,768]{2,1,0:T(8,128)(2,1)}, bf16[8,8,6,128]{3,2,1,0:T(8,128)(2,1)}, bf16[8,8,5,128]{3,2,1,0:T(8,128)(2,1)}, f32[2,8,5,128]{3,2,1,0:T(8,128)}) custom-call(bf16[16,768]{1,0:T(8,128)(2,1)} %maximum_maximum_fusion.refs_0_, bf16[6,128]{1,0:T(8,128)(2,1)} %fusion.59.refs_1_, bf16[5,128]{1,0:T(8,128)(2,1)} %fusion.62.refs_2_, ...), custom_call_target="tpu_custom_call" | custom-call | tf_op jit(solution)/shard_map/pallas_call | solution.py:168
  69.5 1.1 %convolution_bitcast_fusion.6 = f32[16,5,128]{2,0,1:T(8,128)S(1)} fusion(bf16[5,64,64]{1,2,0:T(8,128)(2,1)S(1)} %fusion.31, bf16[64,768]{1,0:T(8,128)(2,1)} %bitcast.283), kind=kOutput, calls=%fused_computation.33 | convolution fusion | flops 1310720 | bytes 143360 | tf_op jit(solution)/shard_map/hqk,qhe->khe/dot_general | solution.py:232
  70.6 0.6 reduce_sum.202
  71.9 0.5 copy-done.7
  73.2 0.3 fusion.16
  74.8 0.8 %copy.245 = bf16[1,128,640]{2,1,0:T(8,128)(2,1)} copy(bf16[1,128,640]{1,2,0:T(8,128)(2,1)S(1)} %bitcast.267) | data formatting | bytes 327680
  75.6 0.3 fusion.15
  75.9 0.3 fusion.13
  76.3 0.8 %copy.244 = bf16[1,128,640]{2,1,0:T(8,128)(2,1)} copy(bf16[1,128,640]{1,2,0:T(8,128)(2,1)S(1)} %bitcast.268) | data formatting | bytes 327680
  77.3 0.8 %copy.246 = bf16[1,128,640]{2,1,0:T(8,128)(2,1)} copy(bf16[1,128,640]{1,2,0:T(8,128)(2,1)S(1)} %bitcast.269) | data formatting | bytes 327680
  (112 shorter events, 9.8 us)
Async XLA Ops:
  0.6 0.7 copy-start.11
  3.4 0.9 %copy-start.5 = (bf16[1,128,640]{2,1,0:T(8,128)(2,1)S(1)}, bf16[1,128,640]{2,1,0:T(8,128)(2,1)}, u32[]{:S(2)}) copy-start(bf16[1,128,640]{2,1,0:T(8,128)(2,1)} %param.9) | copy-start | bytes 491524
  4.5 0.9 %copy-start = (bf16[1,128,640]{2,1,0:T(8,128)(2,1)S(1)}, bf16[1,128,640]{2,1,0:T(8,128)(2,1)}, u32[]{:S(2)}) copy-start(bf16[1,128,640]{2,1,0:T(8,128)(2,1)} %param.6) | copy-start | bytes 491524
  5.4 0.9 %copy-start.1 = (bf16[1,128,640]{2,1,0:T(8,128)(2,1)S(1)}, bf16[1,128,640]{2,1,0:T(8,128)(2,1)}, u32[]{:S(2)}) copy-start(bf16[1,128,640]{2,1,0:T(8,128)(2,1)} %param.7) | copy-start | bytes 491524
  6.3 0.9 %copy-start.2 = (bf16[1,128,640]{2,1,0:T(8,128)(2,1)S(1)}, bf16[1,128,640]{2,1,0:T(8,128)(2,1)}, u32[]{:S(2)}) copy-start(bf16[1,128,640]{2,1,0:T(8,128)(2,1)} %param.8) | copy-start | bytes 491524
  39.9 1.0 %copy-start.4 = (bf16[8,8,15,128]{3,2,1,0:T(8,128)(2,1)S(1)}, bf16[8,8,15,128]{3,2,1,0:T(8,128)(2,1)}, u32[]{:S(2)}) copy-start(bf16[8,8,15,128]{3,2,1,0:T(8,128)(2,1)} %get-tuple-element.14) | copy-start | bytes 737284
  39.9 1.0 %copy-start.3 = (bf16[8,8,15,128]{3,2,1,0:T(8,128)(2,1)S(1)}, bf16[8,8,15,128]{3,2,1,0:T(8,128)(2,1)}, u32[]{:S(2)}) copy-start(bf16[8,8,15,128]{3,2,1,0:T(8,128)(2,1)} %get-tuple-element.13) | copy-start | bytes 737284
  44.1 0.7 copy-start.9
  69.5 1.1 %copy-start.8 = (f32[2,8,5,128]{3,2,1,0:T(8,128)S(1)}, f32[2,8,5,128]{3,2,1,0:T(8,128)}, u32[]{:S(2)}) copy-start(f32[2,8,5,128]{3,2,1,0:T(8,128)} %get-tuple-element.18) | copy-start | bytes 122884
  69.5 1.7 %copy-start.10 = (bf16[4,16,768]{2,1,0:T(8,128)(2,1)S(1)}, bf16[4,16,768]{2,1,0:T(8,128)(2,1)}, u32[]{:S(2)}) copy-start(bf16[4,16,768]{2,1,0:T(8,128)(2,1)} %get-tuple-element.15) | copy-start | bytes 294916
  71.5 0.9 %copy-start.7 = (bf16[8,8,5,128]{3,2,1,0:T(8,128)(2,1)S(1)}, bf16[8,8,5,128]{3,2,1,0:T(8,128)(2,1)}, u32[]{:S(2)}) copy-start(bf16[8,8,5,128]{3,2,1,0:T(8,128)(2,1)} %get-tuple-element.17) | copy-start | bytes 245764
  71.7 0.9 %copy-start.6 = (bf16[8,8,6,128]{3,2,1,0:T(8,128)(2,1)S(1)}, bf16[8,8,6,128]{3,2,1,0:T(8,128)(2,1)}, u32[]{:S(2)}) copy-start(bf16[8,8,6,128]{3,2,1,0:T(8,128)(2,1)} %get-tuple-element.16) | copy-start | bytes 294916

commit v16 on v15

--- a/solution.py
+++ b/solution.py
@@ -107,23 +107,24 @@
     own_z.wait()
     for j in range(1, inner):
         copy_ay(j).wait()
+    if has_sum:
+        total = sum_x[...]
+        for j in range(1, inner):
+            sum_a(j).wait()
+            total = total + sum_stage[j]
+        row_sum[...] = total
     for j in range(1, outer):
         copy_by(j).start()
     for j in range(1, outer):
         copy_az(j).wait()
     for j in range(1, inner):
         copy_bz(j).start()
-    if has_sum:
-        total = sum_x[...]
-        for j in range(1, inner):
-            sum_a(j).wait()
-            total = total + sum_stage[j]
-        row_sum[...] = total
+    out_y[0] = stage_y[...]
+    out_z[0] = stage_z[...]
+    if has_sum:
+        sum_out[0, 0] = total
         for c, j in sum_peers:
             sum_b(c, j).start()
-        sum_out[0, 0] = total
-    out_y[0] = stage_y[...]
-    out_z[0] = stage_z[...]
     for j in range(1, group):
         mid_copy(j).wait()
     for j in range(1, outer):

time: 78.7 us -> 78.9 us (level)
  no operation moved by 1% of the time
where the time goes in v16:
time: 78.9 us; the launch traced here: 78.4 us
  Pallas kernels  48.1 us (61%)
  local copies, waits for them, and re-layouts  16.2 us (21%)
  other arithmetic  7.56 us (10%)
  matrix products  5.39 us (7%)
  between operations  1.1 us (1%)
    pallas_call x2, Pallas kernels, ctx_gather(): pl.pallas_call(functools.partial(gather_kernel, group, inner, has_sum), o...  48.1 us
    unnamed x36, local copies, waits for them, and re-layouts  10.4 us
    reduce_sum x6, other arithmetic, pick_rows(): return jnp.sum(chosen, axis=1, dtype=source_rows.dtype)  2.46 us

profile of v16, /device:TPU:1, one launch (start us, length us, event | category | flops | bytes accessed | tf_op | source)
XLA Modules:
  0.0 78.4 jit_solution(414052176118329465)
XLA Ops:
  0.6 0.7 copy-done.11
  1.9 1.5 %fusion.30 = (bf16[16,5,128]{2,0,1:T(8,128)(2,1)S(1)}, bf16[16,5,128]{2,0,1:T(8,128)(2,1)S(1)}, bf16[16,5,128]{2,0,1:T(8,128)(2,1)S(1)}) fusion(pred[8,5]{0,1:T(8,128)(4,1)S(1)} %iota_compare_fusion.1, bf16[1,128,640]{2,1,0:T(8,128)(2,1)} %param.8, bf16[1,128,640]{2,1,0:T(8,128)(2,1)} %param.7, bf16[1,128,640]{2,1,0:T(8,128)(2,1)} %param.6), kind=kLoop, calls=%fused_computation.78 | loop fusion | flops 460800 | bytes 553000 | tf_op jit(solution)/shard_map/reduce_sum | solution.py:192
  3.4 0.6 pad_maximum_fusion.1.refs_0_
  4.0 0.3 copy-done.5
  4.6 0.8 copy-done
  5.6 0.7 copy-done.1
  6.5 0.7 copy-done.2
  8.0 0.3 select_reduce_fusion
  8.3 0.6 slice_reduce_fusion
  9.3 29.1 %shard_map.101 = (bf16[4,16,1920]{2,1,0:T(8,128)(2,1)}, bf16[8,8,15,128]{3,2,1,0:T(8,128)(2,1)}, bf16[8,8,15,128]{3,2,1,0:T(8,128)(2,1)}) custom-call(bf16[16,1920]{1,0:T(8,128)(2,1)} %pad_maximum_fusion.1.refs_0_, bf16[15,128]{1,0:T(8,128)(2,1)} %bitcast.282, bf16[15,128]{1,0:T(8,128)(2,1)} %bitcast.281), custom_call_target="tpu_custom_call" | custom-call | tf_op jit(solution)/shard_map/pallas_call | solution.py:169
  38.5 1.0 %slice_bitcast_fusion.1 = (bf16[8,5,8,128]{3,2,1,0:T(8,128)(2,1)S(1)}, bf16[8,5,8,128]{3,2,1,0:T(8,128)(2,1)S(1)}, bf16[8,5,8,128]{3,2,1,0:T(8,128)(2,1)S(1)}) fusion(bf16[64,1920]{1,0:T(8,128)(2,1)} %bitcast.273), kind=kLoop, calls=%fused_computation.94 | loop fusion | bytes 491520
  40.2 0.7 copy-done.4
  41.1 0.5 reshape.388
  42.3 0.3 fusion.69
  43.6 0.5 multiply_reduce_fusion.3
  44.2 0.7 copy-done.9
  44.8 0.8 multiply_reduce_fusion
  46.3 0.4 fusion.17
  47.3 0.7 fusion.59.refs_1_
  48.1 0.6 fusion.62.refs_2_
  49.0 0.7 maximum_maximum_fusion.refs_0_
  49.9 0.8 %copy.243 = bf16[1,128,640]{2,1,0:T(8,128)(2,1)} copy(bf16[1,128,640]{1,2,0:T(8,128)(2,1)S(1)} %bitcast.266) | data formatting | bytes 327680
  50.7 19.0 %shard_map.102 = (bf16[4,16,768]{2,1,0:T(8,128)(2,1)}, bf16[8,8,6,128]{3,2,1,0:T(8,128)(2,1)}, bf16[8,8,5,128]{3,2,1,0:T(8,128)(2,1)}, f32[2,8,5,128]{3,2,1,0:T(8,128)}) custom-call(bf16[16,768]{1,0:T(8,128)(2,1)} %maximum_maximum_fusion.refs_0_, bf16[6,128]{1,0:T(8,128)(2,1)} %fusion.59.refs_1_, bf16[5,128]{1,0:T(8,128)(2,1)} %fusion.62.refs_2_, ...), custom_call_target="tpu_custom_call" | custom-call | tf_op jit(solution)/shard_map/pallas_call | solution.py:169
  69.7 1.1 %convolution_bitcast_fusion.6 = f32[16,5,128]{2,0,1:T(8,128)S(1)} fusion(bf16[5,64,64]{1,2,0:T(8,128)(2,1)S(1)} %fusion.31, bf16[64,768]{1,0:T(8,128)(2,1)} %bitcast.283), kind=kOutput, calls=%fused_computation.33 | convolution fusion | flops 1310720 | bytes 143360 | tf_op jit(solution)/shard_map/hqk,qhe->khe/dot_general | solution.py:233
  70.8 0.6 reduce_sum.202
  72.1 0.5 copy-done.7
  73.5 0.3 fusion.16
  75.0 0.8 %copy.245 = bf16[1,128,640]{2,1,0:T(8,128)(2,1)} copy(bf16[1,128,640]{1,2,0:T(8,128)(2,1)S(1)} %bitcast.267) | data formatting | bytes 327680
  75.8 0.3 fusion.15
  76.1 0.3 fusion.13
  76.6 0.8 %copy.244 = bf16[1,128,640]{2,1,0:T(8,128)(2,1)} copy(bf16[1,128,640]{1,2,0:T(8,128)(2,1)S(1)} %bitcast.268) | data formatting | bytes 327680
  77.6 0.8 %copy.246 = bf16[1,128,640]{2,1,0:T(8,128)(2,1)} copy(bf16[1,128,640]{1,2,0:T(8,128)(2,1)S(1)} %bitcast.269) | data formatting | bytes 327680
  (112 shorter events, 9.8 us)
Async XLA Ops:
  0.6 0.7 copy-start.11
  3.4 0.9 %copy-start.5 = (bf16[1,128,640]{2,1,0:T(8,128)(2,1)S(1)}, bf16[1,128,640]{2,1,0:T(8,128)(2,1)}, u32[]{:S(2)}) copy-start(bf16[1,128,640]{2,1,0:T(8,128)(2,1)} %param.9) | copy-start | bytes 491524
  4.5 0.9 %copy-start = (bf16[1,128,640]{2,1,0:T(8,128)(2,1)S(1)}, bf16[1,128,640]{2,1,0:T(8,128)(2,1)}, u32[]{:S(2)}) copy-start(bf16[1,128,640]{2,1,0:T(8,128)(2,1)} %param.6) | copy-start | bytes 491524
  5.4 0.9 %copy-start.1 = (bf16[1,128,640]{2,1,0:T(8,128)(2,1)S(1)}, bf16[1,128,640]{2,1,0:T(8,128)(2,1)}, u32[]{:S(2)}) copy-start(bf16[1,128,640]{2,1,0:T(8,128)(2,1)} %param.7) | copy-start | bytes 491524
  6.3 0.9 %copy-start.2 = (bf16[1,128,640]{2,1,0:T(8,128)(2,1)S(1)}, bf16[1,128,640]{2,1,0:T(8,128)(2,1)}, u32[]{:S(2)}) copy-start(bf16[1,128,640]{2,1,0:T(8,128)(2,1)} %param.8) | copy-start | bytes 491524
  39.9 1.0 %copy-start.4 = (bf16[8,8,15,128]{3,2,1,0:T(8,128)(2,1)S(1)}, bf16[8,8,15,128]{3,2,1,0:T(8,128)(2,1)}, u32[]{:S(2)}) copy-start(bf16[8,8,15,128]{3,2,1,0:T(8,128)(2,1)} %get-tuple-element.14) | copy-start | bytes 737284
  39.9 1.0 %copy-start.3 = (bf16[8,8,15,128]{3,2,1,0:T(8,128)(2,1)S(1)}, bf16[8,8,15,128]{3,2,1,0:T(8,128)(2,1)}, u32[]{:S(2)}) copy-start(bf16[8,8,15,128]{3,2,1,0:T(8,128)(2,1)} %get-tuple-element.13) | copy-start | bytes 737284
  44.1 0.7 copy-start.9
  69.7 1.1 %copy-start.8 = (f32[2,8,5,128]{3,2,1,0:T(8,128)S(1)}, f32[2,8,5,128]{3,2,1,0:T(8,128)}, u32[]{:S(2)}) copy-start(f32[2,8,5,128]{3,2,1,0:T(8,128)} %get-tuple-element.18) | copy-start | bytes 122884
  69.7 1.7 %copy-start.10 = (bf16[4,16,768]{2,1,0:T(8,128)(2,1)S(1)}, bf16[4,16,768]{2,1,0:T(8,128)(2,1)}, u32[]{:S(2)}) copy-start(bf16[4,16,768]{2,1,0:T(8,128)(2,1)} %get-tuple-element.15) | copy-start | bytes 294916
  71.8 0.9 %copy-start.7 = (bf16[8,8,5,128]{3,2,1,0:T(8,128)(2,1)S(1)}, bf16[8,8,5,128]{3,2,1,0:T(8,128)(2,1)}, u32[]{:S(2)}) copy-start(bf16[8,8,5,128]{3,2,1,0:T(8,128)(2,1)} %get-tuple-element.17) | copy-start | bytes 245764
  71.9 0.9 %copy-start.6 = (bf16[8,8,6,128]{3,2,1,0:T(8,128)(2,1)S(1)}, bf16[8,8,6,128]{3,2,1,0:T(8,128)(2,1)}, u32[]{:S(2)}) copy-start(bf16[8,8,6,128]{3,2,1,0:T(8,128)(2,1)} %get-tuple-element.16) | copy-start | bytes 294916

commit v17 on v16

--- a/solution.py
+++ b/solution.py
@@ -176,6 +176,11 @@
     )(*operands)
     top_all = jnp.concatenate([outs[1], jnp.transpose(outs[2], (1, 0, 2, 3))], 2)
     return (outs[0], top_all) + tuple(outs[3:])
+
+
+def token_major(rows):
+    parts = [rows[:, h, :] for h in range(rows.shape[1])]
+    return jnp.concatenate(parts, axis=1).astype(jnp.bfloat16)[None]
 
 
 def lane_dense(block):
@@ -325,7 +330,7 @@
     inv_rms = lax.rsqrt(jnp.mean(attn * attn, axis=-1, keepdims=True) + EPS)
     normed = attn * inv_rms
     gain_rows = out_gain.reshape(head_count, HEAD_DIM)
-    attended = (normed * gain_rows).astype(jnp.bfloat16).reshape(1, tokens, flat_width)
+    attended = token_major(normed * gain_rows)
     grad_full = grad_y[0].reshape(row_shape).astype(jnp.float32)
     gain_part = jnp.sum(grad_full * normed, axis=0).reshape(flat_width)
     grad_norm = grad_full * gain_rows
@@ -390,12 +395,11 @@
     value_grad = (
         base_dv + place_rows(mid_dv, R1, mid_shift) + place_rows(top_dv, ctx_size, top_shift)
     )
-    out_shape = (1, tokens, flat_width)
     return (
         attended,
-        query_grad.astype(jnp.bfloat16).reshape(out_shape),
-        key_grad.astype(jnp.bfloat16).reshape(out_shape),
-        value_grad.astype(jnp.bfloat16).reshape(out_shape),
+        token_major(query_grad),
+        token_major(key_grad),
+        token_major(value_grad),
         gain_grad,
     )
 

time: 78.9 us -> 77.1 us (0.977)
  local copies, waits for them, and re-layouts: 16.2 us -> 14.3 us
    unnamed x36 -> x56, local copies, waits for them, and re-layouts: 10.4 us -> 9.11 us
where the time goes in v17:
time: 77.1 us; the launch traced here: 76.6 us
  Pallas kernels  48.1 us (62%)
  local copies, waits for them, and re-layouts  14.3 us (19%)
  other arithmetic  7.55 us (10%)
  matrix products  5.39 us (7%)
  between operations  1.21 us (2%)
    pallas_call x2, Pallas kernels, ctx_gather(): pl.pallas_call(functools.partial(gather_kernel, group, inner, has_sum), o...  48.1 us
    unnamed x56, local copies, waits for them, and re-layouts  9.11 us
    reduce_sum x6, other arithmetic, pick_rows(): return jnp.sum(chosen, axis=1, dtype=source_rows.dtype)  2.46 us

profile of v17, /device:TPU:1, one launch (start us, length us, event | category | flops | bytes accessed | tf_op | source)
XLA Modules:
  0.0 76.6 jit_solution(16592011106819461271)
XLA Ops:
  0.6 0.7 copy-done.15
  1.9 1.5 %fusion.30 = (bf16[16,5,128]{2,0,1:T(8,128)(2,1)S(1)}, bf16[16,5,128]{2,0,1:T(8,128)(2,1)S(1)}, bf16[16,5,128]{2,0,1:T(8,128)(2,1)S(1)}) fusion(pred[8,5]{0,1:T(8,128)(4,1)S(1)} %iota_compare_fusion.1, bf16[1,128,640]{2,1,0:T(8,128)(2,1)} %param.8, bf16[1,128,640]{2,1,0:T(8,128)(2,1)} %param.7, bf16[1,128,640]{2,1,0:T(8,128)(2,1)} %param.6), kind=kLoop, calls=%fused_computation.78 | loop fusion | flops 460800 | bytes 553000 | tf_op jit(solution)/shard_map/reduce_sum | solution.py:197
  3.4 0.6 pad_maximum_fusion.1.refs_0_
  4.0 0.3 copy-done.5
  4.6 0.8 %copy-done = bf16[1,128,640]{2,1,0:T(8,128)(2,1)S(1)} copy-done((bf16[1,128,640]{2,1,0:T(8,128)(2,1)S(1)}, bf16[1,128,640]{2,1,0:T(8,128)(2,1)}, u32[]{:S(2)}) %copy-start) | copy-done | bytes 163864
  5.6 0.7 copy-done.1
  6.5 0.7 copy-done.2
  8.0 0.3 select_reduce_fusion
  8.3 0.6 slice_reduce_fusion
  9.0 0.3 fusion.71
  9.3 29.1 %shard_map.101 = (bf16[4,16,1920]{2,1,0:T(8,128)(2,1)}, bf16[8,8,15,128]{3,2,1,0:T(8,128)(2,1)}, bf16[8,8,15,128]{3,2,1,0:T(8,128)(2,1)}) custom-call(bf16[16,1920]{1,0:T(8,128)(2,1)} %pad_maximum_fusion.1.refs_0_, bf16[15,128]{1,0:T(8,128)(2,1)} %bitcast.354, bf16[15,128]{1,0:T(8,128)(2,1)} %bitcast.353), custom_call_target="tpu_custom_call" | custom-call | tf_op jit(solution)/shard_map/pallas_call | solution.py:169
  38.5 1.0 %slice_bitcast_fusion.1 = (bf16[8,5,8,128]{3,2,1,0:T(8,128)(2,1)S(1)}, bf16[8,5,8,128]{3,2,1,0:T(8,128)(2,1)S(1)}, bf16[8,5,8,128]{3,2,1,0:T(8,128)(2,1)S(1)}) fusion(bf16[64,1920]{1,0:T(8,128)(2,1)} %bitcast.345), kind=kLoop, calls=%fused_computation.94 | loop fusion | bytes 491520
  40.2 0.7 copy-done.4
  41.1 0.5 reshape.688
  42.3 0.3 fusion.69
  43.6 0.5 multiply_reduce_fusion.3
  44.2 0.7 copy-done.9
  44.8 0.8 %multiply_reduce_fusion = (f32[5,128]{1,0:T(8,128)}, f32[128,5]{0,1:T(8,128)S(1)}, bf16[128,5,128]{2,0,1:T(8,128)(2,1)S(1)}) fusion(f32[128,5,128]{2,0,1:T(8,128)S(1)} %copy.189, f32[128,5,128]{2,0,1:T(8,128)S(1)} %get-tuple-element.65, f32[128,5]{0,1:T(8,128)S(1)} %add_rsqrt_fusion, f32[5,128]{1,0:T(8,128)S(1)} %bitcast.348), kind=kLoop, calls=%fused_computation.54 | loop fusion | flops 654080 | bytes 829440 | tf_op jit(solution)/shard_map/reduce_sum | solution.py:335
  46.3 0.4 fusion.17
  47.3 0.7 fusion.59.refs_1_
  48.1 0.6 fusion.62.refs_2_
  49.0 0.7 maximum_maximum_fusion.refs_0_
  49.8 19.0 %shard_map.102 = (bf16[4,16,768]{2,1,0:T(8,128)(2,1)}, bf16[8,8,6,128]{3,2,1,0:T(8,128)(2,1)}, bf16[8,8,5,128]{3,2,1,0:T(8,128)(2,1)}, f32[2,8,5,128]{3,2,1,0:T(8,128)}) custom-call(bf16[16,768]{1,0:T(8,128)(2,1)} %maximum_maximum_fusion.refs_0_, bf16[6,128]{1,0:T(8,128)(2,1)} %fusion.59.refs_1_, bf16[5,128]{1,0:T(8,128)(2,1)} %fusion.62.refs_2_, ...), custom_call_target="tpu_custom_call" | custom-call | tf_op jit(solution)/shard_map/pallas_call | solution.py:169
  68.8 1.1 %convolution_bitcast_fusion.6 = f32[16,5,128]{2,0,1:T(8,128)S(1)} fusion(bf16[5,64,64]{1,2,0:T(8,128)(2,1)S(1)} %fusion.31, bf16[64,768]{1,0:T(8,128)(2,1)} %bitcast.355), kind=kOutput, calls=%fused_computation.33 | convolution fusion | flops 1310720 | bytes 143360 | tf_op jit(solution)/shard_map/hqk,qhe->khe/dot_general | solution.py:238
  69.9 0.6 reduce_sum.202
  71.2 0.5 copy-done.7
  72.6 0.3 fusion.16
  73.9 0.3 fusion.15
  74.2 0.3 fusion.13
  74.7 0.6 copy-done.12
  75.4 0.6 copy-done.13
  75.9 0.7 copy-done.14
  (132 shorter events, 9.1 us)
Async XLA Ops:
  0.6 0.7 copy-start.15
  3.4 0.9 %copy-start.5 = (bf16[1,128,640]{2,1,0:T(8,128)(2,1)S(1)}, bf16[1,128,640]{2,1,0:T(8,128)(2,1)}, u32[]{:S(2)}) copy-start(bf16[1,128,640]{2,1,0:T(8,128)(2,1)} %param.9) | copy-start | bytes 491524
  4.5 0.9 %copy-start = (bf16[1,128,640]{2,1,0:T(8,128)(2,1)S(1)}, bf16[1,128,640]{2,1,0:T(8,128)(2,1)}, u32[]{:S(2)}) copy-start(bf16[1,128,640]{2,1,0:T(8,128)(2,1)} %param.6) | copy-start | bytes 491524
  5.4 0.9 %copy-start.1 = (bf16[1,128,640]{2,1,0:T(8,128)(2,1)S(1)}, bf16[1,128,640]{2,1,0:T(8,128)(2,1)}, u32[]{:S(2)}) copy-start(bf16[1,128,640]{2,1,0:T(8,128)(2,1)} %param.7) | copy-start | bytes 491524
  6.3 0.9 %copy-start.2 = (bf16[1,128,640]{2,1,0:T(8,128)(2,1)S(1)}, bf16[1,128,640]{2,1,0:T(8,128)(2,1)}, u32[]{:S(2)}) copy-start(bf16[1,128,640]{2,1,0:T(8,128)(2,1)} %param.8) | copy-start | bytes 491524
  39.9 1.0 %copy-start.4 = (bf16[8,8,15,128]{3,2,1,0:T(8,128)(2,1)S(1)}, bf16[8,8,15,128]{3,2,1,0:T(8,128)(2,1)}, u32[]{:S(2)}) copy-start(bf16[8,8,15,128]{3,2,1,0:T(8,128)(2,1)} %get-tuple-element.14) | copy-start | bytes 737284
  39.9 1.0 %copy-start.3 = (bf16[8,8,15,128]{3,2,1,0:T(8,128)(2,1)S(1)}, bf16[8,8,15,128]{3,2,1,0:T(8,128)(2,1)}, u32[]{:S(2)}) copy-start(bf16[8,8,15,128]{3,2,1,0:T(8,128)(2,1)} %get-tuple-element.13) | copy-start | bytes 737284
  44.1 0.7 copy-start.9
  49.8 20.8 %copy-start.11 = (bf16[1,128,640]{2,1,0:T(8,128)(2,1)}, bf16[1,128,640]{2,1,0:T(8,128)(2,1)S(1)}, u32[]{:S(2)}) copy-start(bf16[1,128,640]{2,1,0:T(8,128)(2,1)S(1)} %constant_dynamic-update-slice_fusion.3) | copy-start | bytes 491524
  68.8 1.1 %copy-start.8 = (f32[2,8,5,128]{3,2,1,0:T(8,128)S(1)}, f32[2,8,5,128]{3,2,1,0:T(8,128)}, u32[]{:S(2)}) copy-start(f32[2,8,5,128]{3,2,1,0:T(8,128)} %get-tuple-element.18) | copy-start | bytes 122884
  68.8 1.7 %copy-start.10 = (bf16[4,16,768]{2,1,0:T(8,128)(2,1)S(1)}, bf16[4,16,768]{2,1,0:T(8,128)(2,1)}, u32[]{:S(2)}) copy-start(bf16[4,16,768]{2,1,0:T(8,128)(2,1)} %get-tuple-element.15) | copy-start | bytes 294916
  70.9 0.9 %copy-start.7 = (bf16[8,8,5,128]{3,2,1,0:T(8,128)(2,1)S(1)}, bf16[8,8,5,128]{3,2,1,0:T(8,128)(2,1)}, u32[]{:S(2)}) copy-start(bf16[8,8,5,128]{3,2,1,0:T(8,128)(2,1)} %get-tuple-element.17) | copy-start | bytes 245764
  71.0 0.9 %copy-start.6 = (bf16[8,8,6,128]{3,2,1,0:T(8,128)(2,1)S(1)}, bf16[8,8,6,128]{3,2,1,0:T(8,128)(2,1)}, u32[]{:S(2)}) copy-start(bf16[8,8,6,128]{3,2,1,0:T(8,128)(2,1)} %get-tuple-element.16) | copy-start | bytes 294916
  74.6 0.7 copy-start.12
  75.3 0.7 copy-start.13
  75.9 0.7 copy-start.14

commit v18 on v17

--- a/solution.py
+++ b/solution.py
@@ -213,11 +213,13 @@
     )
 
 
-def attend(q_rows, k_rows, v_rows):
+def attend(q_rows, k_rows, v_rows, own_rows=None):
     scores = level_scores(q_rows, k_rows)
     row_max = jnp.max(scores, axis=-1, keepdims=True)
     log_total = row_max[..., 0] + jnp.log(jnp.sum(jnp.exp(scores - row_max), axis=-1))
-    soft_rows = jnp.exp(scores - log_total[..., None]).astype(jnp.bfloat16)
+    if own_rows is not None:
+        scores = scores[:, :own_rows]
+    soft_rows = jnp.exp(scores - log_total[:, : scores.shape[1], None]).astype(jnp.bfloat16)
     level_out = jnp.einsum("hqk,khe->qhe", soft_rows, v_rows, preferred_element_type=jnp.float32)
     return (level_out, log_total.T)
 
@@ -305,8 +307,8 @@
     mid_q, mid_k, mid_v = split_qkv(mid_all, head_count)
     top_q, top_k, top_v = split_qkv(top_all, head_count)
     base_out, base_total = attend(q_own, k_own, v_own)
-    mid_out_all, mid_total_all = attend(mid_q, mid_k, mid_v)
-    top_out_all, top_total_all = attend(top_q, top_k, top_v)
+    mid_out_all, mid_total_all = attend(mid_q, mid_k, mid_v, mid_rows)
+    top_out_all, top_total_all = attend(top_q, top_k, top_v, top_rows)
     mid_out = mid_out_all[:mid_rows]
     mid_total = mid_total_all[:mid_rows]
     top_out = top_out_all[:top_rows]

time: 77.1 us -> 78.9 us (1.023)
  other arithmetic: 7.55 us -> 10.1 us
    reduce_sum x1, other arithmetic: 0.62 us -> 1.49 us  [shards(): gain_grad = jnp.sum(gain_rows_sum, axis=(0, 1)).reshape(flat_width)]
    transpose x2, other arithmetic: 0.08 us -> 0.87 us  [score_grads(): row_shift.T[..., None]]
    unnamed x56 -> x54, local copies, waits for them, and re-layouts: 9.11 us -> 8.87 us
where the time goes in v18:
time: 78.9 us; the launch traced here: 78.3 us
  Pallas kernels  48.1 us (61%)
  local copies, waits for them, and re-layouts  14.1 us (18%)
  other arithmetic  10.1 us (13%)
  matrix products  4.9 us (6%)
  between operations  1.15 us (1%)
    pallas_call x2, Pallas kernels, ctx_gather(): pl.pallas_call(functools.partial(gather_kernel, group, inner, has_sum), o...  48.1 us
    unnamed x54, local copies, waits for them, and re-layouts  8.87 us
    reduce_sum x6, other arithmetic, pick_rows(): return jnp.sum(chosen, axis=1, dtype=source_rows.dtype)  2.47 us

profile of v18, /device:TPU:1, one launch (start us, length us, event | category | flops | bytes accessed | tf_op | source)
XLA Modules:
  0.0 78.3 jit_solution(18256903900804982842)
XLA Ops:
  0.6 0.7 copy-done.14
  1.9 1.5 %fusion.29 = (bf16[16,5,128]{2,0,1:T(8,128)(2,1)S(1)}, bf16[16,5,128]{2,0,1:T(8,128)(2,1)S(1)}, bf16[16,5,128]{2,0,1:T(8,128)(2,1)S(1)}) fusion(pred[8,5]{0,1:T(8,128)(4,1)S(1)} %iota_compare_fusion.1, bf16[1,128,640]{2,1,0:T(8,128)(2,1)} %param.8, bf16[1,128,640]{2,1,0:T(8,128)(2,1)} %param.7, bf16[1,128,640]{2,1,0:T(8,128)(2,1)} %param.6), kind=kLoop, calls=%fused_computation.79 | loop fusion | flops 460800 | bytes 553000 | tf_op jit(solution)/shard_map/reduce_sum | solution.py:197
  3.4 0.6 pad_maximum_fusion.1.refs_0_
  4.0 0.3 copy-done.6
  4.6 0.8 copy-done
  5.6 0.7 copy-done.1
  6.5 0.7 copy-done.2
  8.0 0.3 select_reduce_fusion
  8.3 0.6 slice_reduce_fusion
  9.0 0.4 fusion.75
  9.3 0.3 exponential_reduce_fusion.1
  9.7 29.1 %shard_map.101 = (bf16[4,16,1920]{2,1,0:T(8,128)(2,1)}, bf16[8,8,15,128]{3,2,1,0:T(8,128)(2,1)}, bf16[8,8,15,128]{3,2,1,0:T(8,128)(2,1)}) custom-call(bf16[16,1920]{1,0:T(8,128)(2,1)} %pad_maximum_fusion.1.refs_0_, bf16[15,128]{1,0:T(8,128)(2,1)} %bitcast.359, bf16[15,128]{1,0:T(8,128)(2,1)} %bitcast.358), custom_call_target="tpu_custom_call" | custom-call | tf_op jit(solution)/shard_map/pallas_call | solution.py:169
  38.8 1.0 %slice_bitcast_fusion.1 = (bf16[8,5,8,128]{3,2,1,0:T(8,128)(2,1)S(1)}, bf16[8,5,8,128]{3,2,1,0:T(8,128)(2,1)S(1)}, bf16[8,5,8,128]{3,2,1,0:T(8,128)(2,1)S(1)}) fusion(bf16[64,1920]{1,0:T(8,128)(2,1)} %bitcast.348), kind=kLoop, calls=%fused_computation.94 | loop fusion | bytes 491520
  40.8 0.5 copy-done.4
  41.6 0.5 reshape.690
  42.7 0.4 fusion.73
  43.1 0.3 exponential_reduce_fusion
  44.5 0.5 multiply_reduce_fusion.3
  45.1 0.7 copy-done.9
  45.7 0.8 multiply_reduce_fusion
  47.2 0.3 fusion.17
  48.2 0.7 fusion.62.refs_1_
  48.9 0.6 fusion.66.refs_2_
  49.9 0.7 maximum_maximum_fusion.refs_0_
  50.7 19.0 %shard_map.102 = (bf16[4,16,768]{2,1,0:T(8,128)(2,1)}, bf16[8,8,6,128]{3,2,1,0:T(8,128)(2,1)}, bf16[8,8,5,128]{3,2,1,0:T(8,128)(2,1)}, f32[2,8,5,128]{3,2,1,0:T(8,128)}) custom-call(bf16[16,768]{1,0:T(8,128)(2,1)} %maximum_maximum_fusion.refs_0_, bf16[6,128]{1,0:T(8,128)(2,1)} %fusion.62.refs_1_, bf16[5,128]{1,0:T(8,128)(2,1)} %fusion.66.refs_2_, ...), custom_call_target="tpu_custom_call" | custom-call | tf_op jit(solution)/shard_map/pallas_call | solution.py:169
  69.7 1.5 %reduce_sum.202 = f32[5,128]{1,0:T(8,128)} reduce(f32[2,8,5,128]{3,2,1,0:T(8,128)} %get-tuple-element.18, f32[]{:T(128)} %constant.37.clone.1), dimensions={0,1}, to_apply=%region_22.23 | reduce | flops 9600 | bytes 43524 | tf_op jit(solution)/shard_map/reduce_sum | solution.py:372
  71.2 0.9 %add_bitcast_fusion = f32[5,64]{0,1:T(8,128)S(1)} fusion(bf16[64,768]{1,0:T(8,128)(2,1)} %bitcast.343), kind=kLoop, calls=%fused_computation.156 | loop fusion | flops 960 | bytes 2560 | tf_op jit(solution)/shard_map/transpose | solution.py:232
  72.8 0.6 copy-done.7
  75.4 0.5 fusion.15
  76.4 0.6 copy-done.11
  77.1 0.6 copy-done.12
  77.7 0.7 copy-done.13
  (128 shorter events, 9.9 us)
Async XLA Ops:
  0.6 0.7 copy-start.14
  3.4 0.9 %copy-start.6 = (bf16[1,128,640]{2,1,0:T(8,128)(2,1)S(1)}, bf16[1,128,640]{2,1,0:T(8,128)(2,1)}, u32[]{:S(2)}) copy-start(bf16[1,128,640]{2,1,0:T(8,128)(2,1)} %param.9) | copy-start | bytes 491524
  4.5 0.9 %copy-start = (bf16[1,128,640]{2,1,0:T(8,128)(2,1)S(1)}, bf16[1,128,640]{2,1,0:T(8,128)(2,1)}, u32[]{:S(2)}) copy-start(bf16[1,128,640]{2,1,0:T(8,128)(2,1)} %param.6) | copy-start | bytes 491524
  5.4 0.9 %copy-start.1 = (bf16[1,128,640]{2,1,0:T(8,128)(2,1)S(1)}, bf16[1,128,640]{2,1,0:T(8,128)(2,1)}, u32[]{:S(2)}) copy-start(bf16[1,128,640]{2,1,0:T(8,128)(2,1)} %param.7) | copy-start | bytes 491524
  6.3 0.9 %copy-start.2 = (bf16[1,128,640]{2,1,0:T(8,128)(2,1)S(1)}, bf16[1,128,640]{2,1,0:T(8,128)(2,1)}, u32[]{:S(2)}) copy-start(bf16[1,128,640]{2,1,0:T(8,128)(2,1)} %param.8) | copy-start | bytes 491524
  40.3 1.0 %copy-start.4 = (bf16[8,8,15,128]{3,2,1,0:T(8,128)(2,1)S(1)}, bf16[8,8,15,128]{3,2,1,0:T(8,128)(2,1)}, u32[]{:S(2)}) copy-start(bf16[8,8,15,128]{3,2,1,0:T(8,128)(2,1)} %get-tuple-element.13) | copy-start | bytes 737284
  40.3 1.0 %copy-start.5 = (bf16[8,8,15,128]{3,2,1,0:T(8,128)(2,1)S(1)}, bf16[8,8,15,128]{3,2,1,0:T(8,128)(2,1)}, u32[]{:S(2)}) copy-start(bf16[8,8,15,128]{3,2,1,0:T(8,128)(2,1)} %get-tuple-element.14) | copy-start | bytes 737284
  45.0 0.7 copy-start.9
  50.6 21.7 %copy-start.10 = (bf16[1,128,640]{2,1,0:T(8,128)(2,1)}, bf16[1,128,640]{2,1,0:T(8,128)(2,1)S(1)}, u32[]{:S(2)}) copy-start(bf16[1,128,640]{2,1,0:T(8,128)(2,1)S(1)} %constant_dynamic-update-slice_fusion.3) | copy-start | bytes 491524
  69.7 2.4 %copy-start.3 = (bf16[4,16,768]{2,1,0:T(8,128)(2,1)S(1)}, bf16[4,16,768]{2,1,0:T(8,128)(2,1)}, u32[]{:S(2)}) copy-start(bf16[4,16,768]{2,1,0:T(8,128)(2,1)} %get-tuple-element.15) | copy-start | bytes 294916
  72.5 0.9 %copy-start.7 = (bf16[8,8,6,128]{3,2,1,0:T(8,128)(2,1)S(1)}, bf16[8,8,6,128]{3,2,1,0:T(8,128)(2,1)}, u32[]{:S(2)}) copy-start(bf16[8,8,6,128]{3,2,1,0:T(8,128)(2,1)} %get-tuple-element.16) | copy-start | bytes 294916
  72.5 1.0 %copy-start.8 = (bf16[8,8,5,128]{3,2,1,0:T(8,128)(2,1)S(1)}, bf16[8,8,5,128]{3,2,1,0:T(8,128)(2,1)}, u32[]{:S(2)}) copy-start(bf16[8,8,5,128]{3,2,1,0:T(8,128)(2,1)} %get-tuple-element.17) | copy-start | bytes 245764
  76.3 0.7 copy-start.11
  77.0 0.7 copy-start.12
  77.7 0.7 copy-start.13

commit v19 on v17

--- a/solution.py
+++ b/solution.py
@@ -190,11 +190,11 @@
 def pick_rows(source_rows, dilation, shifts):
     row_count, head_count, head_width = source_rows.shape
     grouped = source_rows.reshape(row_count // dilation, dilation, head_count, head_width)
-    hit_mask = jnp.arange(dilation, dtype=jnp.int32).reshape(1, dilation, 1, 1) == shifts.reshape(
-        1, 1, head_count, 1
-    )
-    chosen = jnp.where(hit_mask, grouped, jnp.zeros((), source_rows.dtype))
-    return jnp.sum(chosen, axis=1, dtype=source_rows.dtype)
+    index = jnp.broadcast_to(
+        shifts.astype(jnp.int32).reshape(1, 1, head_count, 1),
+        (row_count // dilation, 1, head_count, head_width),
+    )
+    return jnp.take_along_axis(grouped, index, axis=1)[:, 0]
 
 
 def place_rows(row_values, dilation, shifts):

time: 77.1 us -> 521 us (6.76)
  local copies, waits for them, and re-layouts: 14.3 us -> 453 us
    gather x0 -> x30, local copies, waits for them, and re-layouts: none -> 443 us  [pick_rows(): return jnp.take_along_axis(grouped, index, axis=1)[:, 0]]
where the time goes in v19:
time: 521 us; the launch traced here: 520 us
  local copies, waits for them, and re-layouts  453 us (87%)
  Pallas kernels  48.2 us (9%)
  other arithmetic  10.6 us (2%)
  matrix products  6.25 us (1%)
    gather x30, local copies, waits for them, and re-layouts, pick_rows(): return jnp.take_along_axis(grouped, index, axis=1)[:, 0]  443 us
    pallas_call x2, Pallas kernels, ctx_gather(): pl.pallas_call(functools.partial(gather_kernel, group, inner, has_sum), o...  48.2 us

profile of v19, /device:TPU:1, one launch (start us, length us, event | category | flops | bytes accessed | tf_op | source)
XLA Modules:
  0.0 519.9 jit_solution(7404922322485294972)
XLA Ops:
  0.6 0.7 compare_bitcast_fusion
  1.4 0.8 broadcast_add_fusion
  2.3 0.8 broadcast_compare_fusion
  3.2 0.8 add_bitcast_fusion.6
  5.8 0.5 copy-done
  7.1 102.5 %gather_fusion.4 = bf16[10240]{0:T(1024)(128)(2,1)S(1)} fusion(bf16[16,8,5,128]{3,1,2,0:T(8,128)(2,1)S(1)} %bitcast.404, s32[10240]{0:T(1024)S(1)} %reshape.835), kind=kCustom, calls=%fused_computation.5.clone | custom fusion | bytes 204800 | tf_op jit(solution)/shard_map/jit(take_along_axis)/gather | solution.py:197
  109.6 102.5 %gather_fusion.3 = bf16[10240]{0:T(1024)(128)(2,1)S(1)} fusion(bf16[16,8,5,128]{3,1,2,0:T(8,128)(2,1)S(1)} %bitcast.403, s32[10240]{0:T(1024)S(1)} %reshape.835), kind=kCustom, calls=%fused_computation.4.clone | custom fusion | bytes 204800 | tf_op jit(solution)/shard_map/jit(take_along_axis)/gather | solution.py:197
  212.1 102.5 %gather_fusion.2 = bf16[10240]{0:T(1024)(128)(2,1)S(1)} fusion(bf16[16,8,5,128]{3,1,2,0:T(8,128)(2,1)S(1)} %bitcast.402, s32[10240]{0:T(1024)S(1)} %reshape.835), kind=kCustom, calls=%fused_computation.clone | custom fusion | bytes 204800 | tf_op jit(solution)/shard_map/jit(take_along_axis)/gather | solution.py:197
  314.8 0.6 pad_maximum_fusion.1.refs_0_
  315.7 13.3 %gather_fusion.5 = bf16[1280]{0:T(1024)(128)(2,1)S(1)} fusion(bf16[2,64,5,128]{3,2,1,0:T(8,128)(2,1)S(1)} %reshape_reshape_squeeze.21, s32[1280]{0:T(1024)S(1)} %reshape.853), kind=kCustom, calls=%fused_computation.1.clone | custom fusion | bytes 25600 | tf_op jit(solution)/shard_map/jit(take_along_axis)/gather | solution.py:197
  329.2 13.3 %gather_fusion.6 = bf16[1280]{0:T(1024)(128)(2,1)S(1)} fusion(bf16[2,64,5,128]{3,2,1,0:T(8,128)(2,1)S(1)} %reshape_reshape_squeeze.22, s32[1280]{0:T(1024)S(1)} %reshape.853), kind=kCustom, calls=%fused_computation.6.clone | custom fusion | bytes 25600 | tf_op jit(solution)/shard_map/jit(take_along_axis)/gather | solution.py:197
  342.7 13.3 %gather_fusion.7 = bf16[1280]{0:T(1024)(128)(2,1)S(1)} fusion(bf16[2,64,5,128]{3,2,1,0:T(8,128)(2,1)S(1)} %reshape_reshape_squeeze.23, s32[1280]{0:T(1024)S(1)} %reshape.853), kind=kCustom, calls=%fused_computation.7.clone | custom fusion | bytes 25600 | tf_op jit(solution)/shard_map/jit(take_along_axis)/gather | solution.py:197
  356.1 0.6 slice_reduce_fusion
  357.1 29.2 %shard_map.101 = (bf16[4,16,1920]{2,1,0:T(8,128)(2,1)}, bf16[8,8,15,128]{3,2,1,0:T(8,128)(2,1)}, bf16[8,8,15,128]{3,2,1,0:T(8,128)(2,1)}) custom-call(bf16[16,1920]{1,0:T(8,128)(2,1)} %pad_maximum_fusion.1.refs_0_, bf16[15,128]{1,0:T(8,128)(2,1)} %bitcast.438, bf16[15,128]{1,0:T(8,128)(2,1)} %bitcast.437), custom_call_target="tpu_custom_call" | custom-call | tf_op jit(solution)/shard_map/pallas_call | solution.py:169
  386.3 1.0 slice_bitcast_fusion.1
  388.7 0.5 reshape.692
  390.5 0.8 gather_fusion.10
  391.5 2.0 gather_fusion.8
  395.1 0.8 multiply_reduce_fusion
  396.3 12.7 %gather_fusion.1 = f32[1280]{0:T(1024)S(1)} fusion(f32[2,64,5,128]{3,1,0,2:T(8,128)S(1)} %bitcast.400, s32[1280]{0:T(1024)S(1)} %reshape.808), kind=kCustom, calls=%fused_computation.11 | custom fusion | bytes 30720 | tf_op jit(solution)/shard_map/jit(take_along_axis)/gather | solution.py:197
  409.0 76.4 %gather_fusion = f32[10240]{0:T(1024)S(1)} fusion(f32[16,8,5,128]{3,1,0,2:T(8,128)S(1)} %bitcast.401, s32[10240]{0:T(1024)S(1)} %reshape.800), kind=kCustom, calls=%fused_computation.10 | custom fusion | bytes 245760 | tf_op jit(solution)/shard_map/jit(take_along_axis)/gather | solution.py:197
  485.9 0.8 gather_fusion.11
  486.9 0.7 fusion.87.refs_1_
  487.7 0.6 fusion.96.refs_2_
  488.4 2.2 gather_fusion.9
  491.1 0.7 maximum_maximum_fusion.refs_0_
  491.9 19.0 %shard_map.102 = (bf16[4,16,768]{2,1,0:T(8,128)(2,1)}, bf16[8,8,6,128]{3,2,1,0:T(8,128)(2,1)}, bf16[8,8,5,128]{3,2,1,0:T(8,128)(2,1)}, f32[2,8,5,128]{3,2,1,0:T(8,128)}) custom-call(bf16[16,768]{1,0:T(8,128)(2,1)} %maximum_maximum_fusion.refs_0_, bf16[6,128]{1,0:T(8,128)(2,1)} %fusion.87.refs_1_, bf16[5,128]{1,0:T(8,128)(2,1)} %fusion.96.refs_2_, ...), custom_call_target="tpu_custom_call" | custom-call | tf_op jit(solution)/shard_map/pallas_call | solution.py:169
  510.9 1.0 convolution_bitcast_fusion.6
  511.9 1.5 reduce_sum.79
  513.4 0.9 add_bitcast_fusion.4
  514.4 1.1 fusion.20
  519.2 0.7 copy-done.13
  (197 shorter events, 13.8 us)
Async XLA Ops:
  0.6 4.8 copy-start.6
  5.4 0.9 copy-start
  5.5 1.0 copy-start.1
  5.6 1.0 copy-start.2
  387.4 1.0 copy-start.3
  387.5 1.0 copy-start.4
  388.0 0.7 copy-start.5
  393.7 0.8 slice-start
  394.4 0.7 copy-start.9
  491.8 19.0 %copy-start.10 = (bf16[1,128,640]{2,1,0:T(8,128)(2,1)}, bf16[1,128,640]{2,1,0:T(8,128)(2,1)S(1)}, u32[]{:S(2)}) copy-start(bf16[1,128,640]{2,1,0:T(8,128)(2,1)S(1)} %constant_dynamic-update-slice_fusion.3) | copy-start | bytes 491524
  511.9 3.9 copy-start.7
  511.9 3.9 copy-start.8
  518.4 0.7 copy-start.11
  518.5 0.7 copy-start.12
  519.2 0.7 copy-start.13

commit v20 on v17

--- a/solution.py
+++ b/solution.py
@@ -19,7 +19,8 @@
 
 def gather_kernel(group, inner, has_sum, *refs):
     if has_sum:
-        (mid_x, top_y, top_z, sum_x, mid_out, out_y, out_z, sum_out,
+        (mid_x, top_y, top_z, sum_x, q_ref, k_ref, v_ref, lse_ref, grad_ref, shift_ref,
+         mid_out, out_y, out_z, sum_out, dq_ref, dk_ref, dv_ref,
          stage_y, stage_z, sum_stage, row_sum, *sems) = refs
     else:
         (mid_x, top_y, top_z, mid_out, out_y, out_z, stage_y, stage_z, *sems) = refs
@@ -125,6 +126,8 @@
         sum_out[0, 0] = total
         for c, j in sum_peers:
             sum_b(c, j).start()
+    if has_sum:
+        base_backward(q_ref, k_ref, v_ref, lse_ref, grad_ref, shift_ref, dq_ref, dk_ref, dv_ref)
     for j in range(1, group):
         mid_copy(j).wait()
     for j in range(1, outer):
@@ -136,7 +139,34 @@
         copy_bz(j).wait()
 
 
-def ctx_gather(mid_x, top_x, group, tag, sum_x=None):
+def base_backward(q_ref, k_ref, v_ref, lse_ref, grad_ref, shift_ref, dq_ref, dk_ref, dv_ref):
+    score_scale = 1.0 / math.sqrt(HEAD_DIM)
+    lse = lse_ref[...]
+    shift = shift_ref[...]
+    rows_by_rows = (((1,), (1,)), ((), ()))
+    cols_by_cols = (((0,), (0,)), ((), ()))
+    for h in range(lse.shape[1]):
+        cols = pl.ds(h * HEAD_DIM, HEAD_DIM)
+        q_h = q_ref[:, cols]
+        k_h = k_ref[:, cols]
+        v_h = v_ref[:, cols]
+        g_h = grad_ref[:, cols]
+        scores = lax.dot_general(q_h, k_h, rows_by_rows, preferred_element_type=jnp.float32)
+        exact_soft = jnp.exp(scores * score_scale - lse[:, h : h + 1])
+        prob_grad = lax.dot_general(g_h, v_h, rows_by_rows, preferred_element_type=jnp.float32)
+        score_grad = (exact_soft * (prob_grad + shift[:, h : h + 1]) * score_scale).astype(
+            jnp.bfloat16
+        )
+        dq_ref[:, cols] = jnp.dot(score_grad, k_h, preferred_element_type=jnp.float32)
+        dk_ref[:, cols] = lax.dot_general(
+            score_grad, q_h, cols_by_cols, preferred_element_type=jnp.float32
+        )
+        dv_ref[:, cols] = lax.dot_general(
+            exact_soft.astype(jnp.bfloat16), g_h, cols_by_cols, preferred_element_type=jnp.float32
+        )
+
+
+def ctx_gather(mid_x, top_x, group, tag, sum_x=None, base=None):
     count = lax.axis_size("ctx")
     inner = RING
     outer = count // inner
@@ -144,7 +174,7 @@
     top_y = top_x[:half]
     top_z = top_x[half:]
     has_sum = sum_x is not None
-    operands = (mid_x, top_y, top_z) + ((sum_x,) if has_sum else ())
+    operands = (mid_x, top_y, top_z) + ((sum_x,) + tuple(base) if has_sum else ())
     out_shape = (
         jax.ShapeDtypeStruct((group,) + mid_x.shape, mid_x.dtype),
         jax.ShapeDtypeStruct((outer, inner) + top_y.shape, top_x.dtype),
@@ -156,6 +186,7 @@
     ]
     if has_sum:
         out_shape += (jax.ShapeDtypeStruct((2, outer) + sum_x.shape, sum_x.dtype),)
+        out_shape += (jax.ShapeDtypeStruct(base[0].shape, jnp.float32),) * 3
         scratch += [
             pltpu.VMEM((inner,) + sum_x.shape, sum_x.dtype),
             pltpu.VMEM(sum_x.shape, sum_x.dtype),
@@ -340,9 +371,6 @@
     inner = jnp.sum(grad_attn * attn, axis=-1)
     base_low = (base_share[..., None] * grad_attn).astype(jnp.bfloat16)
     base_shift = -(base_share * inner)
-    base_grad, base_soft = score_grads(q_own, k_own, v_own, base_total, base_low, base_shift)
-    base_dq = query_part(base_grad, k_own)
-    base_dk, base_dv = key_parts(base_grad, base_soft, q_own, base_low)
 
     mid_sel = pick_rows(mid_share[..., None], R1, mid_shift)[..., 0]
     mid_low = (mid_sel[..., None] * pick_rows(grad_attn, R1, mid_shift)).astype(jnp.bfloat16)
@@ -354,13 +382,18 @@
     shift_high, shift_low = split_wide(top_row_shift.reshape(-1))
     top_flat = jnp.concatenate([top_low.reshape(-1), shift_high, shift_low])
     top_flat = jnp.pad(top_flat, (0, -top_flat.shape[0] % HEAD_DIM))
-    mid_gathered, gathered, gain_rows_sum = ctx_gather(
+    base_inputs = (
+        queries[0], keys[0], values[0], base_total, base_low.reshape(tokens, flat_width), base_shift
+    )
+    mid_gathered, gathered, gain_rows_sum, base_dq, base_dk, base_dv = ctx_gather(
         pack_grads(mid_low, mid_row_shift, flat_width + HEAD_DIM),
         lane_dense(top_flat),
         SPAN,
         1,
         sum_x=lane_dense(gain_part),
-    )
+        base=base_inputs,
+    )
+    base_dq, base_dk, base_dv = (x.reshape(row_shape) for x in (base_dq, base_dk, base_dv))
     mid_low_all, mid_shift_all = unpack_grads(
         mid_gathered.reshape(-1, mid_gathered.shape[-1]), head_count
     )

time: 77.1 us -> 82.5 us (1.070)
  local copies, waits for them, and re-layouts: 14.3 us -> 19.1 us
  matrix products: 5.39 us -> 4.15 us
  Pallas kernels: 48.1 us -> 49 us
  other arithmetic: 7.55 us -> 8.39 us
    unnamed x56 -> x62, local copies, waits for them, and re-layouts: 9.11 us -> 10.9 us
    pallas_call x0 -> x3, local copies, waits for them, and re-layouts: none -> 1.47 us  [ctx_gather(): pl.pallas_call(functools.partial(gather_kernel, group, inner, has_sum), o...]
    reshape x0 -> x4, local copies, waits for them, and re-layouts: none -> 1.31 us  [the longest x1 0.82 us: shards(): base_low.reshape(tokens, flat_width)]
where the time goes in v20:
time: 82.5 us; the launch traced here: 81.8 us
  Pallas kernels  49 us (59%)
  local copies, waits for them, and re-layouts  19.1 us (23%)
  other arithmetic  8.39 us (10%)
  matrix products  4.15 us (5%)
  between operations  1.23 us (1%)
    pallas_call x2, Pallas kernels, ctx_gather(): pl.pallas_call(functools.partial(gather_kernel, group, inner, has_sum), o...  49 us
    unnamed x62, local copies, waits for them, and re-layouts  10.9 us
    reduce_sum x6, other arithmetic, pick_rows(): return jnp.sum(chosen, axis=1, dtype=source_rows.dtype)  2.32 us

profile of v20, /device:TPU:1, one launch (start us, length us, event | category | flops | bytes accessed | tf_op | source)
XLA Modules:
  0.0 81.8 jit_solution(11155981972370248677)
XLA Ops:
  0.6 0.7 copy-done.18
  1.8 1.5 %fusion.26 = (bf16[16,5,128]{2,0,1:T(8,128)(2,1)S(1)}, bf16[16,5,128]{2,0,1:T(8,128)(2,1)S(1)}, bf16[16,5,128]{2,0,1:T(8,128)(2,1)S(1)}) fusion(pred[8,5]{0,1:T(8,128)(4,1)S(1)} %iota_compare_fusion.1, bf16[1,128,640]{2,1,0:T(8,128)(2,1)} %param.8, bf16[1,128,640]{2,1,0:T(8,128)(2,1)} %param.7, bf16[1,128,640]{2,1,0:T(8,128)(2,1)} %param.6), kind=kLoop, calls=%fused_computation.70 | loop fusion | flops 460800 | bytes 553000 | tf_op jit(solution)/shard_map/reduce_sum | solution.py:228
  3.3 0.6 pad_maximum_fusion.1.refs_0_
  4.5 0.8 copy-done.2
  5.5 0.7 copy-done.1
  6.9 0.7 copy-done
  8.7 0.6 slice_reduce_fusion
  9.4 29.1 %shard_map.101 = (bf16[4,16,1920]{2,1,0:T(8,128)(2,1)}, bf16[8,8,15,128]{3,2,1,0:T(8,128)(2,1)}, bf16[8,8,15,128]{3,2,1,0:T(8,128)(2,1)}) custom-call(bf16[16,1920]{1,0:T(8,128)(2,1)} %pad_maximum_fusion.1.refs_0_, bf16[15,128]{1,0:T(8,128)(2,1)} %bitcast.452, bf16[15,128]{1,0:T(8,128)(2,1)} %bitcast.451), custom_call_target="tpu_custom_call" | custom-call | tf_op jit(solution)/shard_map/pallas_call | solution.py:200
  38.5 1.0 %slice_bitcast_fusion.1 = (bf16[8,5,8,128]{3,2,1,0:T(8,128)(2,1)S(1)}, bf16[8,5,8,128]{3,2,1,0:T(8,128)(2,1)S(1)}, bf16[8,5,8,128]{3,2,1,0:T(8,128)(2,1)S(1)}) fusion(bf16[64,1920]{1,0:T(8,128)(2,1)} %bitcast.444), kind=kLoop, calls=%fused_computation.91 | loop fusion | bytes 491520
  40.1 0.7 copy-done.7
  41.1 0.5 reshape.699
  43.3 0.3 convolution_bitcast_fusion
  43.8 0.5 multiply_reduce_fusion.3
  44.4 0.7 copy-done.12
  45.0 0.8 multiply_reduce_fusion
  45.8 0.3 multiply_convert_fusion
  46.5 0.8 %copy.368.refs_8_ = bf16[128,640]{1,0:T(8,128)(2,1)} copy(bf16[128,640]{0,1:T(8,128)(2,1)S(1)} %bitcast.435) | data formatting | bytes 327680 | tf_op jit(solution)/shard_map/reshape | solution.py:386
  48.1 0.7 maximum_maximum_fusion.refs_0_
  48.9 0.6 multiply_negate_fusion.refs_9_
  49.8 0.6 fusion.57.refs_1_
  50.5 0.6 fusion.60.refs_2_
  51.2 19.8 %shard_map.102 = (bf16[4,16,768]{2,1,0:T(8,128)(2,1)}, bf16[8,8,6,128]{3,2,1,0:T(8,128)(2,1)}, bf16[8,8,5,128]{3,2,1,0:T(8,128)(2,1)}, f32[2,8,5,128]{3,2,1,0:T(...) custom-call(bf16[16,768]{1,0:T(8,128)(2,1)} %maximum_maximum_fusion.refs_0_, ...), custom_call_target="tpu_custom_call" | custom-call | tf_op jit(solution)/shard_map/pallas_call | solution.py:200
  71.0 1.0 %convolution_bitcast_fusion.3 = f32[16,5,128]{2,0,1:T(8,128)S(1)} fusion(bf16[5,64,64]{1,2,0:T(8,128)(2,1)S(1)} %fusion.28, bf16[64,768]{1,0:T(8,128)(2,1)} %bitcast.455), kind=kOutput, calls=%fused_computation.17 | convolution fusion | flops 1310720 | bytes 143360 | tf_op jit(solution)/shard_map/hqk,qhe->khe/dot_general | solution.py:269
  72.1 1.1 %copy.369 = f32[128,640]{0,1:T(8,128)S(1)} copy(f32[128,640]{1,0:T(8,128)} %get-tuple-element.18) | data formatting | bytes 655360 | tf_op jit(solution)/shard_map/pallas_call | solution.py:200
  73.4 0.7 copy-done.11
  74.1 0.6 reduce_sum.202
  75.4 0.6 copy-done.10
  77.6 0.4 copy-done.5
  78.3 0.8 copy-done.4
  79.9 0.6 copy-done.15
  80.6 0.6 copy-done.16
  81.1 0.7 copy-done.17
  (142 shorter events, 10.9 us)
Async XLA Ops:
  0.6 0.7 copy-start.18
  3.3 0.9 %copy-start.8 = (bf16[1,128,640]{2,1,0:T(8,128)(2,1)S(1)}, bf16[1,128,640]{2,1,0:T(8,128)(2,1)}, u32[]{:S(2)}) copy-start(bf16[1,128,640]{2,1,0:T(8,128)(2,1)} %param.9) | copy-start | bytes 491524
  4.4 0.9 %copy-start.2 = (bf16[1,128,640]{2,1,0:T(8,128)(2,1)S(1)}, bf16[1,128,640]{2,1,0:T(8,128)(2,1)}, u32[]{:S(2)}) copy-start(bf16[1,128,640]{2,1,0:T(8,128)(2,1)} %param.6) | copy-start | bytes 491524
  5.3 0.9 %copy-start.1 = (bf16[1,128,640]{2,1,0:T(8,128)(2,1)S(1)}, bf16[1,128,640]{2,1,0:T(8,128)(2,1)}, u32[]{:S(2)}) copy-start(bf16[1,128,640]{2,1,0:T(8,128)(2,1)} %param.7) | copy-start | bytes 491524
  6.7 0.9 %copy-start = (bf16[1,128,640]{2,1,0:T(8,128)(2,1)S(1)}, bf16[1,128,640]{2,1,0:T(8,128)(2,1)}, u32[]{:S(2)}) copy-start(bf16[1,128,640]{2,1,0:T(8,128)(2,1)} %param.8) | copy-start | bytes 491524
  6.9 35.8 %copy-start.3 = (f32[5,128]{0,1:T(8,128)}, f32[5,128]{0,1:T(8,128)S(1)}, u32[]{:S(2)}) copy-start(f32[5,128]{0,1:T(8,128)S(1)} %copy.327) | copy-start | bytes 7684
  39.8 1.0 %copy-start.7 = (bf16[8,8,15,128]{3,2,1,0:T(8,128)(2,1)S(1)}, bf16[8,8,15,128]{3,2,1,0:T(8,128)(2,1)}, u32[]{:S(2)}) copy-start(bf16[8,8,15,128]{3,2,1,0:T(8,128)(2,1)} %get-tuple-element.17) | copy-start | bytes 737284
  39.9 1.0 %copy-start.6 = (bf16[8,8,15,128]{3,2,1,0:T(8,128)(2,1)S(1)}, bf16[8,8,15,128]{3,2,1,0:T(8,128)(2,1)}, u32[]{:S(2)}) copy-start(bf16[8,8,15,128]{3,2,1,0:T(8,128)(2,1)} %get-tuple-element.16) | copy-start | bytes 737284
  44.3 0.7 copy-start.12
  51.2 19.8 %copy-start.14 = (bf16[1,128,640]{2,1,0:T(8,128)(2,1)}, bf16[1,128,640]{2,1,0:T(8,128)(2,1)S(1)}, u32[]{:S(2)}) copy-start(bf16[1,128,640]{2,1,0:T(8,128)(2,1)S(1)} %constant_dynamic-update-slice_fusion.3) | copy-start | bytes 491524
  73.2 0.8 %copy-start.11 = (f32[2,8,5,128]{3,2,1,0:T(8,128)S(1)}, f32[2,8,5,128]{3,2,1,0:T(8,128)}, u32[]{:S(2)}) copy-start(f32[2,8,5,128]{3,2,1,0:T(8,128)} %get-tuple-element.24) | copy-start | bytes 122884
  73.2 1.4 %copy-start.13 = (bf16[4,16,768]{2,1,0:T(8,128)(2,1)S(1)}, bf16[4,16,768]{2,1,0:T(8,128)(2,1)}, u32[]{:S(2)}) copy-start(bf16[4,16,768]{2,1,0:T(8,128)(2,1)} %get-tuple-element.19) | copy-start | bytes 294916
  75.0 0.9 %copy-start.10 = (bf16[8,8,5,128]{3,2,1,0:T(8,128)(2,1)S(1)}, bf16[8,8,5,128]{3,2,1,0:T(8,128)(2,1)}, u32[]{:S(2)}) copy-start(bf16[8,8,5,128]{3,2,1,0:T(8,128)(2,1)} %get-tuple-element.21) | copy-start | bytes 245764
  75.2 0.9 %copy-start.9 = (bf16[8,8,6,128]{3,2,1,0:T(8,128)(2,1)S(1)}, bf16[8,8,6,128]{3,2,1,0:T(8,128)(2,1)}, u32[]{:S(2)}) copy-start(bf16[8,8,6,128]{3,2,1,0:T(8,128)(2,1)} %get-tuple-element.20) | copy-start | bytes 294916
  77.0 1.0 %copy-start.5 = (f32[128,640]{1,0:T(8,128)S(1)}, f32[128,640]{1,0:T(8,128)}, u32[]{:S(2)}) copy-start(f32[128,640]{1,0:T(8,128)} %get-tuple-element.22) | copy-start | bytes 983044
  78.1 1.0 %copy-start.4 = (f32[128,640]{1,0:T(8,128)S(1)}, f32[128,640]{1,0:T(8,128)}, u32[]{:S(2)}) copy-start(f32[128,640]{1,0:T(8,128)} %get-tuple-element.23) | copy-start | bytes 983044
  79.8 0.7 copy-start.15
  80.5 0.7 copy-start.16
  81.1 0.7 copy-start.17

commit v21 on v17

--- a/solution.py
+++ b/solution.py
@@ -243,10 +243,17 @@
     return jnp.einsum("hqk,khe->qhe", score_grad, k_rows, preferred_element_type=jnp.float32)
 
 
-def split_qkv(packed, head_count):
+def split_qkv(packed, head_count, parts=3):
     width = head_count * HEAD_DIM
     shape = (packed.shape[0], head_count, HEAD_DIM)
-    return tuple(packed[:, i * width : (i + 1) * width].reshape(shape) for i in range(3))
+    return tuple(packed[:, i * width : (i + 1) * width].reshape(shape) for i in range(parts))
+
+
+def log_totals(q_rows, k_rows):
+    scores = level_scores(q_rows, k_rows)
+    row_max = jnp.max(scores, axis=-1, keepdims=True)
+    log_total = row_max[..., 0] + jnp.log(jnp.sum(jnp.exp(scores - row_max), axis=-1))
+    return log_total.T
 
 
 def split_wide(values):
@@ -293,9 +300,9 @@
     mid_pack = jnp.concatenate(
         [pick_rows(x, R1, mid_shift).reshape(-1, flat_width) for x in (q_own, k_own, v_own)], 1
     )
+    top_q_own = pick_rows(q_own, ctx_size, top_shift)
     top_pack = jnp.concatenate(
-        [pick_rows(x, ctx_size, top_shift).reshape(-1, flat_width) for x in (q_own, k_own, v_own)],
-        1,
+        [pick_rows(x, ctx_size, top_shift).reshape(-1, flat_width) for x in (k_own, v_own)], 1
     )
     mid_rows = mid_pack.shape[0]
     top_rows = top_pack.shape[0]
@@ -303,14 +310,12 @@
     mid_all = mid_all.reshape(-1, mid_pack.shape[1])
     top_all = top_all.reshape(-1, top_pack.shape[1])
     mid_q, mid_k, mid_v = split_qkv(mid_all, head_count)
-    top_q, top_k, top_v = split_qkv(top_all, head_count)
+    top_k, top_v = split_qkv(top_all, head_count, 2)
     base_out, base_total = attend(q_own, k_own, v_own)
     mid_out_all, mid_total_all = attend(mid_q, mid_k, mid_v)
-    top_out_all, top_total_all = attend(top_q, top_k, top_v)
+    top_out, top_total = attend(top_q_own, top_k, top_v)
     mid_out = mid_out_all[:mid_rows]
     mid_total = mid_total_all[:mid_rows]
-    top_out = top_out_all[:top_rows]
-    top_total = top_total_all[:top_rows]
     mid_full = place_rows(mid_total[..., None], R1, mid_shift)[..., 0]
     top_full = place_rows(top_total[..., None], ctx_size, top_shift)[..., 0]
     row_max = jnp.maximum(base_total, jnp.where(mid_hit, mid_full, base_total))
@@ -352,7 +357,9 @@
     top_row_shift = -(top_sel * pick_rows(inner[..., None], ctx_size, top_shift)[..., 0])
 
     shift_high, shift_low = split_wide(top_row_shift.reshape(-1))
-    top_flat = jnp.concatenate([top_low.reshape(-1), shift_high, shift_low])
+    top_flat = jnp.concatenate(
+        [top_q_own.reshape(-1), top_low.reshape(-1), shift_high, shift_low]
+    )
     top_flat = jnp.pad(top_flat, (0, -top_flat.shape[0] % HEAD_DIM))
     mid_gathered, gathered, gain_rows_sum = ctx_gather(
         pack_grads(mid_low, mid_row_shift, flat_width + HEAD_DIM),
@@ -365,8 +372,11 @@
         mid_gathered.reshape(-1, mid_gathered.shape[-1]), head_count
     )
     gathered = gathered.reshape(ctx_size, -1)
-    grad_width = top_rows * flat_width
-    top_low_all = gathered[:, :grad_width].reshape(-1, head_count, HEAD_DIM)
+    q_width = top_rows * flat_width
+    top_q = gathered[:, :q_width].reshape(-1, head_count, HEAD_DIM)
+    grad_width = 2 * q_width
+    top_low_all = gathered[:, q_width:grad_width].reshape(-1, head_count, HEAD_DIM)
+    top_total_all = log_totals(top_q, top_k)
     gain_grad = jnp.sum(gain_rows_sum, axis=(0, 1)).reshape(flat_width)
     shift_count = top_rows * head_count
     top_shift_all = join_wide(

time: 77.1 us -> 80.4 us (1.043)
  Pallas kernels: 48.1 us -> 51.2 us
    pallas_call x2, Pallas kernels: 48.1 us -> 51.2 us  [ctx_gather(): pl.pallas_call(functools.partial(gather_kernel, group, inner, has_sum), o...]
    unnamed x56 -> x55, local copies, waits for them, and re-layouts: 9.11 us -> 8.99 us
where the time goes in v21:
time: 80.4 us; the launch traced here: 79.9 us
  Pallas kernels  51.2 us (64%)
  local copies, waits for them, and re-layouts  14.1 us (18%)
  other arithmetic  7.79 us (10%)
  matrix products  5.56 us (7%)
  between operations  1.2 us (1%)
    pallas_call x2, Pallas kernels, ctx_gather(): pl.pallas_call(functools.partial(gather_kernel, group, inner, has_sum), o...  51.2 us
    unnamed x55, local copies, waits for them, and re-layouts  8.99 us
    reduce_sum x6, other arithmetic, pick_rows(): return jnp.sum(chosen, axis=1, dtype=source_rows.dtype)  2.47 us

profile of v21, /device:TPU:1, one launch (start us, length us, event | category | flops | bytes accessed | tf_op | source)
XLA Modules:
  0.0 79.9 jit_solution(3096642704927799441)
XLA Ops:
  0.6 0.7 copy-done.15
  1.9 1.5 %fusion.29 = (bf16[16,5,128]{2,0,1:T(8,128)(2,1)S(1)}, bf16[16,5,128]{2,0,1:T(8,128)(2,1)S(1)}, bf16[16,5,128]{2,0,1:T(8,128)(2,1)S(1)}) fusion(pred[8,5]{0,1:T(8,128)(4,1)S(1)} %iota_compare_fusion.1, bf16[1,128,640]{2,1,0:T(8,128)(2,1)} %param.8, bf16[1,128,640]{2,1,0:T(8,128)(2,1)} %param.7, bf16[1,128,640]{2,1,0:T(8,128)(2,1)} %param.6), kind=kLoop, calls=%fused_computation.78 | loop fusion | flops 460800 | bytes 553000 | tf_op jit(solution)/shard_map/reduce_sum | solution.py:197
  3.4 0.6 pad_maximum_fusion.1.refs_0_
  4.0 0.3 copy-done.7
  4.6 0.8 copy-done
  5.6 0.7 copy-done.1
  6.5 0.7 copy-done.2
  8.0 0.3 select_reduce_fusion
  8.3 0.6 slice_reduce_fusion
  9.0 0.3 fusion.73
  9.3 29.1 %shard_map.101 = (bf16[4,16,1920]{2,1,0:T(8,128)(2,1)}, bf16[8,8,10,128]{3,2,1,0:T(8,128)(2,1)}, bf16[8,8,10,128]{3,2,1,0:T(8,128)(2,1)}) custom-call(bf16[16,1920]{1,0:T(8,128)(2,1)} %pad_maximum_fusion.1.refs_0_, bf16[10,128]{1,0:T(8,128)(2,1)} %bitcast.344, bf16[10,128]{1,0:T(8,128)(2,1)} %bitcast.343), custom_call_target="tpu_custom_call" | custom-call | tf_op jit(solution)/shard_map/pallas_call | solution.py:169
  38.5 1.0 %slice_bitcast_fusion.1 = (bf16[8,5,8,128]{3,2,1,0:T(8,128)(2,1)S(1)}, bf16[8,5,8,128]{3,2,1,0:T(8,128)(2,1)S(1)}, bf16[8,5,8,128]{3,2,1,0:T(8,128)(2,1)S(1)}) fusion(bf16[64,1920]{1,0:T(8,128)(2,1)} %bitcast.336), kind=kLoop, calls=%fused_computation.96 | loop fusion | bytes 491520
  40.2 0.7 copy-done.4
  41.1 0.4 reshape.697
  43.2 0.5 multiply_reduce_fusion.3
  43.8 0.7 copy-done.9
  44.4 0.8 multiply_reduce_fusion
  45.9 0.4 fusion.17
  47.0 0.6 pad_maximum_fusion.2.refs_1_
  47.7 0.6 fusion.60.refs_2_
  48.7 0.7 maximum_maximum_fusion.refs_0_
  49.5 22.1 %shard_map.102 = (bf16[4,16,768]{2,1,0:T(8,128)(2,1)}, bf16[8,8,11,128]{3,2,1,0:T(8,128)(2,1)}, bf16[8,8,10,128]{3,2,1,0:T(8,128)(2,1)}, f32[2,8,5,128]{3,2,1,0:T(8,128)}) custom-call(bf16[16,768]{1,0:T(8,128)(2,1)} %maximum_maximum_fusion.refs_0_, bf16[11,128]{1,0:T(8,128)(2,1)} %pad_maximum_fusion.2.refs_1_, bf16[10,128]{1,0:T(8,128)(2,1)} %fusion.60.refs_2_, ...), custom_call_target="tpu_custom_call" | custom-call | tf_op jit(solution)/shard_map/pallas_call | solution.py:169
  71.6 1.1 %convolution_bitcast_fusion.5 = f32[16,5,128]{2,0,1:T(8,128)S(1)} fusion(bf16[5,64,64]{1,2,0:T(8,128)(2,1)S(1)} %fusion.30, bf16[64,768]{1,0:T(8,128)(2,1)} %bitcast.345), kind=kOutput, calls=%fused_computation.32 | convolution fusion | flops 1310720 | bytes 143360 | tf_op jit(solution)/shard_map/hqk,qhe->khe/dot_general | solution.py:238
  72.7 0.6 reduce_sum.212
  74.0 0.4 copy-done.6
  75.5 0.3 fusion.74
  75.9 0.3 fusion.16
  77.2 0.3 fusion.15
  77.5 0.3 fusion.13
  78.0 0.6 copy-done.12
  78.6 0.6 copy-done.13
  79.2 0.7 copy-done.14
  (136 shorter events, 9.6 us)
Async XLA Ops:
  0.6 0.7 copy-start.15
  3.4 0.9 %copy-start.7 = (bf16[1,128,640]{2,1,0:T(8,128)(2,1)S(1)}, bf16[1,128,640]{2,1,0:T(8,128)(2,1)}, u32[]{:S(2)}) copy-start(bf16[1,128,640]{2,1,0:T(8,128)(2,1)} %param.9) | copy-start | bytes 491524
  4.5 0.9 %copy-start = (bf16[1,128,640]{2,1,0:T(8,128)(2,1)S(1)}, bf16[1,128,640]{2,1,0:T(8,128)(2,1)}, u32[]{:S(2)}) copy-start(bf16[1,128,640]{2,1,0:T(8,128)(2,1)} %param.6) | copy-start | bytes 491524
  5.4 0.9 %copy-start.1 = (bf16[1,128,640]{2,1,0:T(8,128)(2,1)S(1)}, bf16[1,128,640]{2,1,0:T(8,128)(2,1)}, u32[]{:S(2)}) copy-start(bf16[1,128,640]{2,1,0:T(8,128)(2,1)} %param.7) | copy-start | bytes 491524
  6.3 0.9 %copy-start.2 = (bf16[1,128,640]{2,1,0:T(8,128)(2,1)S(1)}, bf16[1,128,640]{2,1,0:T(8,128)(2,1)}, u32[]{:S(2)}) copy-start(bf16[1,128,640]{2,1,0:T(8,128)(2,1)} %param.8) | copy-start | bytes 491524
  39.9 1.0 %copy-start.4 = (bf16[8,8,10,128]{3,2,1,0:T(8,128)(2,1)S(1)}, bf16[8,8,10,128]{3,2,1,0:T(8,128)(2,1)}, u32[]{:S(2)}) copy-start(bf16[8,8,10,128]{3,2,1,0:T(8,128)(2,1)} %get-tuple-element.14) | copy-start | bytes 491524
  39.9 1.0 %copy-start.3 = (bf16[8,8,10,128]{3,2,1,0:T(8,128)(2,1)S(1)}, bf16[8,8,10,128]{3,2,1,0:T(8,128)(2,1)}, u32[]{:S(2)}) copy-start(bf16[8,8,10,128]{3,2,1,0:T(8,128)(2,1)} %get-tuple-element.13) | copy-start | bytes 491524
  43.8 0.7 copy-start.9
  49.4 23.9 %copy-start.11 = (bf16[1,128,640]{2,1,0:T(8,128)(2,1)}, bf16[1,128,640]{2,1,0:T(8,128)(2,1)S(1)}, u32[]{:S(2)}) copy-start(bf16[1,128,640]{2,1,0:T(8,128)(2,1)S(1)} %constant_dynamic-update-slice_fusion.2) | copy-start | bytes 491524
  71.6 1.1 %copy-start.8 = (f32[2,8,5,128]{3,2,1,0:T(8,128)S(1)}, f32[2,8,5,128]{3,2,1,0:T(8,128)}, u32[]{:S(2)}) copy-start(f32[2,8,5,128]{3,2,1,0:T(8,128)} %get-tuple-element.18) | copy-start | bytes 122884
  71.6 1.7 %copy-start.10 = (bf16[4,16,768]{2,1,0:T(8,128)(2,1)S(1)}, bf16[4,16,768]{2,1,0:T(8,128)(2,1)}, u32[]{:S(2)}) copy-start(bf16[4,16,768]{2,1,0:T(8,128)(2,1)} %get-tuple-element.15) | copy-start | bytes 294916
  73.4 1.0 %copy-start.6 = (bf16[8,8,10,128]{3,2,1,0:T(8,128)(2,1)S(1)}, bf16[8,8,10,128]{3,2,1,0:T(8,128)(2,1)}, u32[]{:S(2)}) copy-start(bf16[8,8,10,128]{3,2,1,0:T(8,128)(2,1)} %get-tuple-element.17) | copy-start | bytes 491524
  73.6 1.0 %copy-start.5 = (bf16[8,8,11,128]{3,2,1,0:T(8,128)(2,1)S(1)}, bf16[8,8,11,128]{3,2,1,0:T(8,128)(2,1)}, u32[]{:S(2)}) copy-start(bf16[8,8,11,128]{3,2,1,0:T(8,128)(2,1)} %get-tuple-element.16) | copy-start | bytes 540676
  77.9 0.7 copy-start.12
  78.5 0.7 copy-start.13
  79.2 0.7 copy-start.14

commit v22 on v17

--- a/solution.py
+++ b/solution.py
@@ -19,8 +19,8 @@
 
 def gather_kernel(group, inner, has_sum, *refs):
     if has_sum:
-        (mid_x, top_y, top_z, sum_x, mid_out, out_y, out_z, sum_out,
-         stage_y, stage_z, sum_stage, row_sum, *sems) = refs
+        (mid_x, top_y, top_z, sum_x, mid_out, out_y, out_z, sum_total,
+         stage_y, stage_z, sum_stage, row_sum, sum_out, *sems) = refs
     else:
         (mid_x, top_y, top_z, mid_out, out_y, out_z, stage_y, stage_z, *sems) = refs
     (send_mid, recv_mid, send_ay, recv_ay, send_by, recv_by,
@@ -134,6 +134,11 @@
             sum_b(c, j).wait()
     for j in range(1, inner):
         copy_bz(j).wait()
+    if has_sum:
+        total = sum_out[0, 0]
+        for c, j in sum_peers:
+            total = total + sum_out[c, j]
+        sum_total[...] = total
 
 
 def ctx_gather(mid_x, top_x, group, tag, sum_x=None):
@@ -155,10 +160,11 @@
         pltpu.VMEM((outer,) + top_z.shape, top_x.dtype),
     ]
     if has_sum:
-        out_shape += (jax.ShapeDtypeStruct((2, outer) + sum_x.shape, sum_x.dtype),)
+        out_shape += (jax.ShapeDtypeStruct(sum_x.shape, sum_x.dtype),)
         scratch += [
             pltpu.VMEM((inner,) + sum_x.shape, sum_x.dtype),
             pltpu.VMEM(sum_x.shape, sum_x.dtype),
+            pltpu.VMEM((2, outer) + sum_x.shape, sum_x.dtype),
         ]
     for size in (group, inner, outer, outer, inner):
         scratch += [pltpu.SemaphoreType.DMA((size,)), pltpu.SemaphoreType.DMA((size,))]
@@ -367,7 +373,7 @@
     gathered = gathered.reshape(ctx_size, -1)
     grad_width = top_rows * flat_width
     top_low_all = gathered[:, :grad_width].reshape(-1, head_count, HEAD_DIM)
-    gain_grad = jnp.sum(gain_rows_sum, axis=(0, 1)).reshape(flat_width)
+    gain_grad = gain_rows_sum.reshape(flat_width)
     shift_count = top_rows * head_count
     top_shift_all = join_wide(
         gathered[:, grad_width : grad_width + shift_count],

time: 77.1 us -> 76.7 us (level)
    unnamed x56 -> x57, local copies, waits for them, and re-layouts: 9.11 us -> 9.18 us
where the time goes in v22:
time: 76.7 us; the launch traced here: 76.1 us
  Pallas kernels  48.1 us (63%)
  local copies, waits for them, and re-layouts  14.4 us (19%)
  other arithmetic  6.94 us (9%)
  matrix products  5.4 us (7%)
  between operations  1.22 us (2%)
    pallas_call x2, Pallas kernels, ctx_gather(): pl.pallas_call(functools.partial(gather_kernel, group, inner, has_sum), o...  48.1 us
    unnamed x57, local copies, waits for them, and re-layouts  9.18 us
    reduce_sum x6, other arithmetic, pick_rows(): return jnp.sum(chosen, axis=1, dtype=source_rows.dtype)  2.46 us
    dot_general x3, matrix products, key_parts(): jnp.einsum('hqk,qhe->khe', soft_low, grad_low, preferred_element_type=jnp...  1.54 us

profile of v22, /device:TPU:1, one launch (start us, length us, event | category | flops | bytes accessed | tf_op | source)
XLA Modules:
  0.0 76.1 jit_solution(1233027645802149918)
XLA Ops:
  0.6 0.7 copy-done.15
  1.9 1.5 %fusion.30 = (bf16[16,5,128]{2,0,1:T(8,128)(2,1)S(1)}, bf16[16,5,128]{2,0,1:T(8,128)(2,1)S(1)}, bf16[16,5,128]{2,0,1:T(8,128)(2,1)S(1)}) fusion(pred[8,5]{0,1:T(8,128)(4,1)S(1)} %iota_compare_fusion.1, bf16[1,128,640]{2,1,0:T(8,128)(2,1)} %param.8, bf16[1,128,640]{2,1,0:T(8,128)(2,1)} %param.7, bf16[1,128,640]{2,1,0:T(8,128)(2,1)} %param.6), kind=kLoop, calls=%fused_computation.78 | loop fusion | flops 460800 | bytes 553000 | tf_op jit(solution)/shard_map/reduce_sum | solution.py:203
  3.4 0.6 pad_maximum_fusion.1.refs_0_
  4.0 0.3 copy-done.5
  4.6 0.8 %copy-done = bf16[1,128,640]{2,1,0:T(8,128)(2,1)S(1)} copy-done((bf16[1,128,640]{2,1,0:T(8,128)(2,1)S(1)}, bf16[1,128,640]{2,1,0:T(8,128)(2,1)}, u32[]{:S(2)}) %copy-start) | copy-done | bytes 163864
  5.6 0.7 copy-done.1
  6.5 0.7 copy-done.2
  8.0 0.3 select_reduce_fusion
  8.3 0.6 slice_reduce_fusion
  9.0 0.3 fusion.71
  9.3 29.1 %shard_map.101 = (bf16[4,16,1920]{2,1,0:T(8,128)(2,1)}, bf16[8,8,15,128]{3,2,1,0:T(8,128)(2,1)}, bf16[8,8,15,128]{3,2,1,0:T(8,128)(2,1)}) custom-call(bf16[16,1920]{1,0:T(8,128)(2,1)} %pad_maximum_fusion.1.refs_0_, bf16[15,128]{1,0:T(8,128)(2,1)} %bitcast.354, bf16[15,128]{1,0:T(8,128)(2,1)} %bitcast.353), custom_call_target="tpu_custom_call" | custom-call | tf_op jit(solution)/shard_map/pallas_call | solution.py:175
  38.5 1.0 %slice_bitcast_fusion.1 = (bf16[8,5,8,128]{3,2,1,0:T(8,128)(2,1)S(1)}, bf16[8,5,8,128]{3,2,1,0:T(8,128)(2,1)S(1)}, bf16[8,5,8,128]{3,2,1,0:T(8,128)(2,1)S(1)}) fusion(bf16[64,1920]{1,0:T(8,128)(2,1)} %bitcast.345), kind=kLoop, calls=%fused_computation.94 | loop fusion | bytes 491520
  40.2 0.7 copy-done.4
  41.1 0.5 reshape.688
  42.3 0.3 fusion.69
  43.1 0.3 convolution_bitcast_fusion.3
  43.6 0.5 multiply_reduce_fusion.3
  44.2 0.7 copy-done.8
  44.8 0.8 %multiply_reduce_fusion = (f32[5,128]{1,0:T(8,128)}, f32[128,5]{0,1:T(8,128)S(1)}, bf16[128,5,128]{2,0,1:T(8,128)(2,1)S(1)}) fusion(f32[128,5,128]{2,0,1:T(8,128)S(1)} %copy.189, f32[128,5,128]{2,0,1:T(8,128)S(1)} %get-tuple-element.65, f32[128,5]{0,1:T(8,128)S(1)} %add_rsqrt_fusion, f32[5,128]{1,0:T(8,128)S(1)} %bitcast.348), kind=kLoop, calls=%fused_computation.54 | loop fusion | flops 654080 | bytes 829440 | tf_op jit(solution)/shard_map/reduce_sum | solution.py:341
  46.3 0.4 fusion.17
  47.3 0.7 fusion.59.refs_1_
  48.1 0.6 fusion.62.refs_2_
  49.0 0.7 maximum_maximum_fusion.refs_0_
  49.8 19.0 %shard_map.102 = (bf16[4,16,768]{2,1,0:T(8,128)(2,1)}, bf16[8,8,6,128]{3,2,1,0:T(8,128)(2,1)}, bf16[8,8,5,128]{3,2,1,0:T(8,128)(2,1)}, f32[5,128]{1,0:T(8,128)}) custom-call(bf16[16,768]{1,0:T(8,128)(2,1)} %maximum_maximum_fusion.refs_0_, bf16[6,128]{1,0:T(8,128)(2,1)} %fusion.59.refs_1_, bf16[5,128]{1,0:T(8,128)(2,1)} %fusion.62.refs_2_, ...), custom_call_target="tpu_custom_call" | custom-call | tf_op jit(solution)/shard_map/pallas_call | solution.py:175
  68.8 1.1 %convolution_bitcast_fusion.6 = f32[16,5,128]{2,0,1:T(8,128)S(1)} fusion(bf16[5,64,64]{1,2,0:T(8,128)(2,1)S(1)} %fusion.31, bf16[64,768]{1,0:T(8,128)(2,1)} %bitcast.355), kind=kOutput, calls=%fused_computation.33 | convolution fusion | flops 1310720 | bytes 143360 | tf_op jit(solution)/shard_map/hqk,qhe->khe/dot_general | solution.py:244
  70.6 0.5 copy-done.7
  72.0 0.3 fusion.16
  73.3 0.3 fusion.15
  73.6 0.3 fusion.13
  74.1 0.6 copy-done.11
  74.8 0.6 copy-done.12
  75.4 0.6 copy.344
  (132 shorter events, 9.0 us)
Async XLA Ops:
  0.6 0.7 copy-start.15
  3.4 0.9 %copy-start.5 = (bf16[1,128,640]{2,1,0:T(8,128)(2,1)S(1)}, bf16[1,128,640]{2,1,0:T(8,128)(2,1)}, u32[]{:S(2)}) copy-start(bf16[1,128,640]{2,1,0:T(8,128)(2,1)} %param.9) | copy-start | bytes 491524
  4.5 0.9 %copy-start = (bf16[1,128,640]{2,1,0:T(8,128)(2,1)S(1)}, bf16[1,128,640]{2,1,0:T(8,128)(2,1)}, u32[]{:S(2)}) copy-start(bf16[1,128,640]{2,1,0:T(8,128)(2,1)} %param.6) | copy-start | bytes 491524
  5.4 0.9 %copy-start.1 = (bf16[1,128,640]{2,1,0:T(8,128)(2,1)S(1)}, bf16[1,128,640]{2,1,0:T(8,128)(2,1)}, u32[]{:S(2)}) copy-start(bf16[1,128,640]{2,1,0:T(8,128)(2,1)} %param.7) | copy-start | bytes 491524
  6.3 0.9 %copy-start.2 = (bf16[1,128,640]{2,1,0:T(8,128)(2,1)S(1)}, bf16[1,128,640]{2,1,0:T(8,128)(2,1)}, u32[]{:S(2)}) copy-start(bf16[1,128,640]{2,1,0:T(8,128)(2,1)} %param.8) | copy-start | bytes 491524
  39.9 1.0 %copy-start.4 = (bf16[8,8,15,128]{3,2,1,0:T(8,128)(2,1)S(1)}, bf16[8,8,15,128]{3,2,1,0:T(8,128)(2,1)}, u32[]{:S(2)}) copy-start(bf16[8,8,15,128]{3,2,1,0:T(8,128)(2,1)} %get-tuple-element.14) | copy-start | bytes 737284
  39.9 1.0 %copy-start.3 = (bf16[8,8,15,128]{3,2,1,0:T(8,128)(2,1)S(1)}, bf16[8,8,15,128]{3,2,1,0:T(8,128)(2,1)}, u32[]{:S(2)}) copy-start(bf16[8,8,15,128]{3,2,1,0:T(8,128)(2,1)} %get-tuple-element.13) | copy-start | bytes 737284
  44.1 0.7 copy-start.8
  49.8 20.5 %copy-start.10 = (bf16[1,128,640]{2,1,0:T(8,128)(2,1)}, bf16[1,128,640]{2,1,0:T(8,128)(2,1)S(1)}, u32[]{:S(2)}) copy-start(bf16[1,128,640]{2,1,0:T(8,128)(2,1)S(1)} %constant_dynamic-update-slice_fusion.3) | copy-start | bytes 491524
  68.8 1.1 %copy-start.9 = (bf16[4,16,768]{2,1,0:T(8,128)(2,1)S(1)}, bf16[4,16,768]{2,1,0:T(8,128)(2,1)}, u32[]{:S(2)}) copy-start(bf16[4,16,768]{2,1,0:T(8,128)(2,1)} %get-tuple-element.15) | copy-start | bytes 294916
  70.3 0.9 %copy-start.7 = (bf16[8,8,5,128]{3,2,1,0:T(8,128)(2,1)S(1)}, bf16[8,8,5,128]{3,2,1,0:T(8,128)(2,1)}, u32[]{:S(2)}) copy-start(bf16[8,8,5,128]{3,2,1,0:T(8,128)(2,1)} %get-tuple-element.17) | copy-start | bytes 245764
  70.4 0.9 %copy-start.6 = (bf16[8,8,6,128]{3,2,1,0:T(8,128)(2,1)S(1)}, bf16[8,8,6,128]{3,2,1,0:T(8,128)(2,1)}, u32[]{:S(2)}) copy-start(bf16[8,8,6,128]{3,2,1,0:T(8,128)(2,1)} %get-tuple-element.16) | copy-start | bytes 294916
  74.0 0.7 copy-start.11
  74.7 0.7 copy-start.12
  74.7 0.7 copy-start.14
  75.4 0.7 copy-start.13

commit v23 on v22

--- a/solution.py
+++ b/solution.py
@@ -141,7 +141,7 @@
         sum_total[...] = total
 
 
-def ctx_gather(mid_x, top_x, group, tag, sum_x=None):
+def ctx_gather(mid_x, top_x, group, tag, sum_x=None, raw=False):
     count = lax.axis_size("ctx")
     inner = RING
     outer = count // inner
@@ -180,6 +180,8 @@
         scratch_shapes=scratch,
         compiler_params=pltpu.CompilerParams(collective_id=tag, has_side_effects=True),
     )(*operands)
+    if raw:
+        return outs
     top_all = jnp.concatenate([outs[1], jnp.transpose(outs[2], (1, 0, 2, 3))], 2)
     return (outs[0], top_all) + tuple(outs[3:])
 
@@ -299,17 +301,24 @@
     mid_pack = jnp.concatenate(
         [pick_rows(x, R1, mid_shift).reshape(-1, flat_width) for x in (q_own, k_own, v_own)], 1
     )
-    top_pack = jnp.concatenate(
-        [pick_rows(x, ctx_size, top_shift).reshape(-1, flat_width) for x in (q_own, k_own, v_own)],
-        1,
-    )
+    top_blocks = jnp.concatenate(
+        [pick_rows(x, ctx_size, top_shift) for x in (q_own, k_own, v_own)], 1
+    )
+    top_pack = jnp.pad(top_blocks, ((0, 0), (0, 16 - top_blocks.shape[1]), (0, 0)))
     mid_rows = mid_pack.shape[0]
     top_rows = top_pack.shape[0]
-    mid_all, top_all = ctx_gather(mid_pack, lane_dense(top_pack), SPAN, 0)
+    mid_all, rows_y, rows_z = ctx_gather(mid_pack, lane_dense(top_pack), SPAN, 0, raw=True)
     mid_all = mid_all.reshape(-1, mid_pack.shape[1])
-    top_all = top_all.reshape(-1, top_pack.shape[1])
     mid_q, mid_k, mid_v = split_qkv(mid_all, head_count)
-    top_q, top_k, top_v = split_qkv(top_all, head_count)
+    rows_y = rows_y.reshape((ctx_size,) + rows_y.shape[2:])
+    rows_z = jnp.transpose(rows_z, (1, 0, 2, 3)).reshape((ctx_size,) + rows_z.shape[2:])
+    top_q, top_k, top_v = (
+        jnp.stack(
+            [rows_y[:, p * head_count : (p + 1) * head_count],
+             rows_z[:, p * head_count : (p + 1) * head_count]], 1
+        ).reshape(-1, head_count, HEAD_DIM)
+        for p in range(3)
+    )
     base_out, base_total = attend(q_own, k_own, v_own)
     mid_out_all, mid_total_all = attend(mid_q, mid_k, mid_v)
     top_out_all, top_total_all = attend(top_q, top_k, top_v)

time: 76.7 us -> 76.1 us (level)
    unnamed x57 -> x55, local copies, waits for them, and re-layouts: 9.18 us -> 9.19 us
where the time goes in v23:
time: 76.1 us; the launch traced here: 75.6 us
  Pallas kernels  48.1 us (63%)
  local copies, waits for them, and re-layouts  14 us (18%)
  other arithmetic  6.95 us (9%)
  matrix products  5.28 us (7%)
  between operations  1.23 us (2%)
    pallas_call x2, Pallas kernels, ctx_gather(): pl.pallas_call(functools.partial(gather_kernel, group, inner, has_sum), o...  48.1 us
    unnamed x55, local copies, waits for them, and re-layouts  9.19 us
    reduce_sum x6, other arithmetic, pick_rows(): return jnp.sum(chosen, axis=1, dtype=source_rows.dtype)  2.47 us
    dot_general x3, matrix products, key_parts(): jnp.einsum('hqk,qhe->khe', soft_low, grad_low, preferred_element_type=jnp...  1.54 us

profile of v23, /device:TPU:1, one launch (start us, length us, event | category | flops | bytes accessed | tf_op | source)
XLA Modules:
  0.0 75.6 jit_solution(16544450017707216909)
XLA Ops:
  0.6 0.7 copy-done.15
  1.9 1.5 %fusion.30 = (bf16[16,5,128]{2,0,1:T(8,128)(2,1)S(1)}, bf16[16,5,128]{2,0,1:T(8,128)(2,1)S(1)}, bf16[16,5,128]{2,0,1:T(8,128)(2,1)S(1)}) fusion(pred[8,5]{0,1:T(8,128)(4,1)S(1)} %iota_compare_fusion.2, bf16[1,128,640]{2,1,0:T(8,128)(2,1)} %param.8, bf16[1,128,640]{2,1,0:T(8,128)(2,1)} %param.7, bf16[1,128,640]{2,1,0:T(8,128)(2,1)} %param.6), kind=kLoop, calls=%fused_computation.80 | loop fusion | flops 460800 | bytes 553000 | tf_op jit(solution)/shard_map/reduce_sum | solution.py:205
  3.4 0.6 pad_maximum_fusion.3.refs_0_
  4.0 0.3 copy-done.5
  4.6 0.8 %copy-done = bf16[1,128,640]{2,1,0:T(8,128)(2,1)S(1)} copy-done((bf16[1,128,640]{2,1,0:T(8,128)(2,1)S(1)}, bf16[1,128,640]{2,1,0:T(8,128)(2,1)}, u32[]{:S(2)}) %copy-start) | copy-done | bytes 163864
  5.6 0.7 copy-done.1
  6.5 0.7 copy-done.2
  8.0 0.3 select_reduce_fusion.2
  8.3 0.6 slice_bitcast_fusion.30
  8.9 0.3 fusion.75
  9.3 29.1 %shard_map.101 = (bf16[4,16,1920]{2,1,0:T(8,128)(2,1)}, bf16[8,8,16,128]{3,2,1,0:T(8,128)(2,1)}, bf16[8,8,16,128]{3,2,1,0:T(8,128)(2,1)}) custom-call(bf16[16,1920]{1,0:T(8,128)(2,1)} %pad_maximum_fusion.3.refs_0_, bf16[16,128]{1,0:T(8,128)(2,1)} %get-tuple-element.53.refs_1_, bf16[16,128]{1,0:T(8,128)(2,1)} %get-tuple-element.52.refs_2_), custom_call_target="tpu_custom_call" | custom-call | tf_op jit(solution)/shard_map/pallas_call | solution.py:175
  38.4 1.0 %slice_bitcast_fusion.7 = (bf16[8,5,8,128]{3,2,1,0:T(8,128)(2,1)S(1)}, bf16[8,5,8,128]{3,2,1,0:T(8,128)(2,1)S(1)}, bf16[8,5,8,128]{3,2,1,0:T(8,128)(2,1)S(1)}) fusion(bf16[64,1920]{1,0:T(8,128)(2,1)} %bitcast.354), kind=kLoop, calls=%fused_computation.102 | loop fusion | bytes 491520
  40.3 0.7 copy-done.4
  41.9 0.3 fusion.73
  42.7 0.3 convolution_bitcast_fusion.3
  43.2 0.5 multiply_reduce_fusion.3
  43.8 0.7 copy-done.8
  44.4 0.8 %multiply_reduce_fusion = (f32[5,128]{1,0:T(8,128)}, f32[128,5]{0,1:T(8,128)S(1)}, bf16[128,5,128]{2,0,1:T(8,128)(2,1)S(1)}) fusion(f32[128,5,128]{2,0,1:T(8,128)S(1)} %copy.173, f32[128,5,128]{2,0,1:T(8,128)S(1)} %get-tuple-element.68, f32[128,5]{0,1:T(8,128)S(1)} %add_rsqrt_fusion, f32[5,128]{1,0:T(8,128)S(1)} %bitcast.357), kind=kLoop, calls=%fused_computation.53 | loop fusion | flops 654080 | bytes 829440 | tf_op jit(solution)/shard_map/reduce_sum | solution.py:350
  45.2 0.3 fusion.22
  45.7 0.3 fusion.21
  45.9 0.4 fusion.17
  46.9 0.7 fusion.64.refs_1_
  47.7 0.6 fusion.67.refs_2_
  48.6 0.7 maximum_maximum_fusion.refs_0_
  49.4 19.0 %shard_map.102 = (bf16[4,16,768]{2,1,0:T(8,128)(2,1)}, bf16[8,8,6,128]{3,2,1,0:T(8,128)(2,1)}, bf16[8,8,5,128]{3,2,1,0:T(8,128)(2,1)}, f32[5,128]{1,0:T(8,128)}) custom-call(bf16[16,768]{1,0:T(8,128)(2,1)} %maximum_maximum_fusion.refs_0_, bf16[6,128]{1,0:T(8,128)(2,1)} %fusion.64.refs_1_, bf16[5,128]{1,0:T(8,128)(2,1)} %fusion.67.refs_2_, ...), custom_call_target="tpu_custom_call" | custom-call | tf_op jit(solution)/shard_map/pallas_call | solution.py:175
  68.4 1.1 %convolution_bitcast_fusion.6 = f32[16,5,128]{2,0,1:T(8,128)S(1)} fusion(bf16[5,64,64]{1,2,0:T(8,128)(2,1)S(1)} %fusion.31, bf16[64,768]{1,0:T(8,128)(2,1)} %bitcast.359), kind=kOutput, calls=%fused_computation.33 | convolution fusion | flops 1310720 | bytes 143360 | tf_op jit(solution)/shard_map/hqk,qhe->khe/dot_general | solution.py:246
  70.2 0.5 copy-done.7
  72.8 0.3 fusion.15
  73.1 0.3 fusion.13
  73.6 0.6 copy-done.11
  74.3 0.6 copy-done.12
  74.9 0.6 copy.309
  (132 shorter events, 8.7 us)
Async XLA Ops:
  0.6 0.7 copy-start.15
  3.4 0.9 %copy-start.5 = (bf16[1,128,640]{2,1,0:T(8,128)(2,1)S(1)}, bf16[1,128,640]{2,1,0:T(8,128)(2,1)}, u32[]{:S(2)}) copy-start(bf16[1,128,640]{2,1,0:T(8,128)(2,1)} %param.9) | copy-start | bytes 491524
  4.5 0.9 %copy-start = (bf16[1,128,640]{2,1,0:T(8,128)(2,1)S(1)}, bf16[1,128,640]{2,1,0:T(8,128)(2,1)}, u32[]{:S(2)}) copy-start(bf16[1,128,640]{2,1,0:T(8,128)(2,1)} %param.6) | copy-start | bytes 491524
  5.4 0.9 %copy-start.1 = (bf16[1,128,640]{2,1,0:T(8,128)(2,1)S(1)}, bf16[1,128,640]{2,1,0:T(8,128)(2,1)}, u32[]{:S(2)}) copy-start(bf16[1,128,640]{2,1,0:T(8,128)(2,1)} %param.7) | copy-start | bytes 491524
  6.3 0.9 %copy-start.2 = (bf16[1,128,640]{2,1,0:T(8,128)(2,1)S(1)}, bf16[1,128,640]{2,1,0:T(8,128)(2,1)}, u32[]{:S(2)}) copy-start(bf16[1,128,640]{2,1,0:T(8,128)(2,1)} %param.8) | copy-start | bytes 491524
  38.4 1.1 %copy-start.3 = (bf16[8,8,16,128]{3,2,1,0:T(8,128)(2,1)S(1)}, bf16[8,8,16,128]{3,2,1,0:T(8,128)(2,1)}, u32[]{:S(2)}) copy-start(bf16[8,8,16,128]{3,2,1,0:T(8,128)(2,1)} %get-tuple-element.13) | copy-start | bytes 786436
  40.0 1.0 %copy-start.4 = (bf16[8,8,16,128]{3,2,1,0:T(8,128)(2,1)S(1)}, bf16[8,8,16,128]{3,2,1,0:T(8,128)(2,1)}, u32[]{:S(2)}) copy-start(bf16[8,8,16,128]{3,2,1,0:T(8,128)(2,1)} %get-tuple-element.14) | copy-start | bytes 786436
  43.7 0.7 copy-start.8
  49.4 20.5 %copy-start.10 = (bf16[1,128,640]{2,1,0:T(8,128)(2,1)}, bf16[1,128,640]{2,1,0:T(8,128)(2,1)S(1)}, u32[]{:S(2)}) copy-start(bf16[1,128,640]{2,1,0:T(8,128)(2,1)S(1)} %constant_dynamic-update-slice_fusion) | copy-start | bytes 491524
  68.4 1.1 %copy-start.9 = (bf16[4,16,768]{2,1,0:T(8,128)(2,1)S(1)}, bf16[4,16,768]{2,1,0:T(8,128)(2,1)}, u32[]{:S(2)}) copy-start(bf16[4,16,768]{2,1,0:T(8,128)(2,1)} %get-tuple-element.15) | copy-start | bytes 294916
  69.9 0.9 %copy-start.7 = (bf16[8,8,5,128]{3,2,1,0:T(8,128)(2,1)S(1)}, bf16[8,8,5,128]{3,2,1,0:T(8,128)(2,1)}, u32[]{:S(2)}) copy-start(bf16[8,8,5,128]{3,2,1,0:T(8,128)(2,1)} %get-tuple-element.17) | copy-start | bytes 245764
  70.0 0.9 %copy-start.6 = (bf16[8,8,6,128]{3,2,1,0:T(8,128)(2,1)S(1)}, bf16[8,8,6,128]{3,2,1,0:T(8,128)(2,1)}, u32[]{:S(2)}) copy-start(bf16[8,8,6,128]{3,2,1,0:T(8,128)(2,1)} %get-tuple-element.16) | copy-start | bytes 294916
  73.5 0.7 copy-start.11
  74.2 0.7 copy-start.12
  74.2 0.7 copy-start.14
  74.9 0.7 copy-start.13

commit v24 on v23

--- a/solution.py
+++ b/solution.py
@@ -366,28 +366,29 @@
     top_low = (top_sel[..., None] * pick_rows(grad_attn, ctx_size, top_shift)).astype(jnp.bfloat16)
     top_row_shift = -(top_sel * pick_rows(inner[..., None], ctx_size, top_shift)[..., 0])
 
-    shift_high, shift_low = split_wide(top_row_shift.reshape(-1))
-    top_flat = jnp.concatenate([top_low.reshape(-1), shift_high, shift_low])
-    top_flat = jnp.pad(top_flat, (0, -top_flat.shape[0] % HEAD_DIM))
-    mid_gathered, gathered, gain_rows_sum = ctx_gather(
+    shift_high, shift_low = split_wide(top_row_shift)
+    shift_block = jnp.concatenate([shift_high, shift_low], 1)
+    shift_block = jnp.pad(shift_block, ((0, 0), (0, HEAD_DIM - shift_block.shape[1])))[:, None]
+    top_block = jnp.concatenate([top_low, shift_block], 1)
+    mid_gathered, grads_y, grads_z, gain_rows_sum = ctx_gather(
         pack_grads(mid_low, mid_row_shift, flat_width + HEAD_DIM),
-        lane_dense(top_flat),
+        lane_dense(top_block),
         SPAN,
         1,
         sum_x=lane_dense(gain_part),
+        raw=True,
     )
     mid_low_all, mid_shift_all = unpack_grads(
         mid_gathered.reshape(-1, mid_gathered.shape[-1]), head_count
     )
-    gathered = gathered.reshape(ctx_size, -1)
-    grad_width = top_rows * flat_width
-    top_low_all = gathered[:, :grad_width].reshape(-1, head_count, HEAD_DIM)
+    grads_y = grads_y.reshape((ctx_size,) + grads_y.shape[2:])
+    grads_z = jnp.transpose(grads_z, (1, 0, 2, 3)).reshape((ctx_size,) + grads_z.shape[2:])
+    both = jnp.stack([grads_y, grads_z], 1).reshape((-1,) + grads_y.shape[1:])
+    top_low_all = both[:, :head_count]
+    top_shift_all = join_wide(
+        both[:, head_count, :head_count], both[:, head_count, head_count : 2 * head_count]
+    )
     gain_grad = gain_rows_sum.reshape(flat_width)
-    shift_count = top_rows * head_count
-    top_shift_all = join_wide(
-        gathered[:, grad_width : grad_width + shift_count],
-        gathered[:, grad_width + shift_count : grad_width + 2 * shift_count],
-    ).reshape(-1, head_count)
 
     mid_grad, mid_soft = score_grads(
         mid_q, mid_k, mid_v, mid_total_all, mid_low_all, mid_shift_all

time: 76.1 us -> 76.1 us (level)
    unnamed x55 -> x54, local copies, waits for them, and re-layouts: 9.19 us -> 9.99 us
where the time goes in v24:
time: 76.1 us; the launch traced here: 75.6 us
  Pallas kernels  48.1 us (63%)
  local copies, waits for them, and re-layouts  14 us (18%)
  other arithmetic  6.89 us (9%)
  matrix products  5.26 us (7%)
  between operations  1.23 us (2%)
    pallas_call x2, Pallas kernels, ctx_gather(): pl.pallas_call(functools.partial(gather_kernel, group, inner, has_sum), o...  48.1 us
    unnamed x54, local copies, waits for them, and re-layouts  9.99 us
    reduce_sum x6, other arithmetic, pick_rows(): return jnp.sum(chosen, axis=1, dtype=source_rows.dtype)  2.47 us

profile of v24, /device:TPU:1, one launch (start us, length us, event | category | flops | bytes accessed | tf_op | source)
XLA Modules:
  0.0 75.6 jit_solution(8885144010415222588)
XLA Ops:
  0.6 0.7 copy-done.15
  1.9 1.5 %fusion.30 = (bf16[16,5,128]{2,0,1:T(8,128)(2,1)S(1)}, bf16[16,5,128]{2,0,1:T(8,128)(2,1)S(1)}, bf16[16,5,128]{2,0,1:T(8,128)(2,1)S(1)}) fusion(pred[8,5]{0,1:T(8,128)(4,1)S(1)} %iota_compare_fusion.2, bf16[1,128,640]{2,1,0:T(8,128)(2,1)} %param.8, bf16[1,128,640]{2,1,0:T(8,128)(2,1)} %param.7, bf16[1,128,640]{2,1,0:T(8,128)(2,1)} %param.6), kind=kLoop, calls=%fused_computation.79 | loop fusion | flops 460800 | bytes 553000 | tf_op jit(solution)/shard_map/reduce_sum | solution.py:205
  3.4 0.6 pad_maximum_fusion.4.refs_0_
  4.0 0.3 copy-done.5
  4.6 0.8 %copy-done = bf16[1,128,640]{2,1,0:T(8,128)(2,1)S(1)} copy-done((bf16[1,128,640]{2,1,0:T(8,128)(2,1)S(1)}, bf16[1,128,640]{2,1,0:T(8,128)(2,1)}, u32[]{:S(2)}) %copy-start) | copy-done | bytes 163864
  5.6 0.7 copy-done.1
  6.5 0.7 copy-done.2
  8.0 0.3 select_reduce_fusion.2
  8.3 0.6 slice_bitcast_fusion.30
  8.9 0.3 fusion.78
  9.3 29.1 %shard_map.101 = (bf16[4,16,1920]{2,1,0:T(8,128)(2,1)}, bf16[8,8,16,128]{3,2,1,0:T(8,128)(2,1)}, bf16[8,8,16,128]{3,2,1,0:T(8,128)(2,1)}) custom-call(bf16[16,1920]{1,0:T(8,128)(2,1)} %pad_maximum_fusion.4.refs_0_, bf16[16,128]{1,0:T(8,128)(2,1)} %get-tuple-element.55.refs_1_, bf16[16,128]{1,0:T(8,128)(2,1)} %get-tuple-element.54.refs_2_), custom_call_target="tpu_custom_call" | custom-call | tf_op jit(solution)/shard_map/pallas_call | solution.py:175
  38.4 1.0 %slice_bitcast_fusion.7 = (bf16[8,5,8,128]{3,2,1,0:T(8,128)(2,1)S(1)}, bf16[8,5,8,128]{3,2,1,0:T(8,128)(2,1)S(1)}, bf16[8,5,8,128]{3,2,1,0:T(8,128)(2,1)S(1)}) fusion(bf16[64,1920]{1,0:T(8,128)(2,1)} %bitcast.359), kind=kLoop, calls=%fused_computation.100 | loop fusion | bytes 491520
  40.3 0.7 copy-done.4
  41.9 0.3 fusion.76
  42.7 0.3 convolution_bitcast_fusion.3
  43.2 0.5 multiply_reduce_fusion.3
  43.8 0.7 copy-done.8
  44.4 0.8 %multiply_reduce_fusion = (f32[5,128]{1,0:T(8,128)}, f32[128,5]{0,1:T(8,128)S(1)}, bf16[128,5,128]{2,0,1:T(8,128)(2,1)S(1)}) fusion(f32[128,5,128]{2,0,1:T(8,128)S(1)} %copy.232, f32[128,5,128]{2,0,1:T(8,128)S(1)} %get-tuple-element.70, f32[128,5]{0,1:T(8,128)S(1)} %add_rsqrt_fusion, f32[5,128]{1,0:T(8,128)S(1)} %bitcast.364), kind=kLoop, calls=%fused_computation.53 | loop fusion | flops 654080 | bytes 829440 | tf_op jit(solution)/shard_map/reduce_sum | solution.py:350
  45.2 0.3 fusion.22
  45.9 0.4 fusion.16
  47.0 0.6 fusion.66
  47.9 0.7 maximum_maximum_fusion.refs_0_
  48.7 19.0 %shard_map.102 = (bf16[4,16,768]{2,1,0:T(8,128)(2,1)}, bf16[8,8,6,128]{3,2,1,0:T(8,128)(2,1)}, bf16[8,8,6,128]{3,2,1,0:T(8,128)(2,1)}, f32[5,128]{1,0:T(8,128)}) custom-call(bf16[16,768]{1,0:T(8,128)(2,1)} %maximum_maximum_fusion.refs_0_, bf16[6,128]{1,0:T(8,128)(2,1)} %get-tuple-element.57.refs_1_, bf16[6,128]{1,0:T(8,128)(2,1)} %get-tuple-element.56.refs_2_, ...), custom_call_target="tpu_custom_call" | custom-call | tf_op jit(solution)/shard_map/pallas_call | solution.py:175
  67.7 1.1 %convolution_bitcast_fusion.6 = f32[16,5,128]{2,0,1:T(8,128)S(1)} fusion(bf16[5,64,64]{1,2,0:T(8,128)(2,1)S(1)} %fusion.31, bf16[64,768]{1,0:T(8,128)(2,1)} %bitcast.366), kind=kOutput, calls=%fused_computation.33 | convolution fusion | flops 1310720 | bytes 143360 | tf_op jit(solution)/shard_map/hqk,qhe->khe/dot_general | solution.py:246
  68.8 0.9 %copy-done.9 = bf16[4,16,768]{2,1,0:T(8,128)(2,1)S(1)} copy-done((bf16[4,16,768]{2,1,0:T(8,128)(2,1)S(1)}, bf16[4,16,768]{2,1,0:T(8,128)(2,1)}, u32[]{:S(2)}) %copy-start.9) | copy-done | bytes 98328
  70.4 0.7 copy-done.6
  71.7 0.3 fusion.17
  72.8 0.3 fusion.15
  73.1 0.3 fusion.13
  73.6 0.6 copy-done.11
  74.2 0.6 copy-done.12
  74.9 0.6 copy.362
  (128 shorter events, 8.3 us)
Async XLA Ops:
  0.6 0.7 copy-start.15
  3.4 0.9 %copy-start.5 = (bf16[1,128,640]{2,1,0:T(8,128)(2,1)S(1)}, bf16[1,128,640]{2,1,0:T(8,128)(2,1)}, u32[]{:S(2)}) copy-start(bf16[1,128,640]{2,1,0:T(8,128)(2,1)} %param.9) | copy-start | bytes 491524
  4.5 0.9 %copy-start = (bf16[1,128,640]{2,1,0:T(8,128)(2,1)S(1)}, bf16[1,128,640]{2,1,0:T(8,128)(2,1)}, u32[]{:S(2)}) copy-start(bf16[1,128,640]{2,1,0:T(8,128)(2,1)} %param.6) | copy-start | bytes 491524
  5.4 0.9 %copy-start.1 = (bf16[1,128,640]{2,1,0:T(8,128)(2,1)S(1)}, bf16[1,128,640]{2,1,0:T(8,128)(2,1)}, u32[]{:S(2)}) copy-start(bf16[1,128,640]{2,1,0:T(8,128)(2,1)} %param.7) | copy-start | bytes 491524
  6.3 0.9 %copy-start.2 = (bf16[1,128,640]{2,1,0:T(8,128)(2,1)S(1)}, bf16[1,128,640]{2,1,0:T(8,128)(2,1)}, u32[]{:S(2)}) copy-start(bf16[1,128,640]{2,1,0:T(8,128)(2,1)} %param.8) | copy-start | bytes 491524
  38.4 1.1 %copy-start.3 = (bf16[8,8,16,128]{3,2,1,0:T(8,128)(2,1)S(1)}, bf16[8,8,16,128]{3,2,1,0:T(8,128)(2,1)}, u32[]{:S(2)}) copy-start(bf16[8,8,16,128]{3,2,1,0:T(8,128)(2,1)} %get-tuple-element.13) | copy-start | bytes 786436
  40.0 1.0 %copy-start.4 = (bf16[8,8,16,128]{3,2,1,0:T(8,128)(2,1)S(1)}, bf16[8,8,16,128]{3,2,1,0:T(8,128)(2,1)}, u32[]{:S(2)}) copy-start(bf16[8,8,16,128]{3,2,1,0:T(8,128)(2,1)} %get-tuple-element.14) | copy-start | bytes 786436
  43.7 0.7 copy-start.8
  48.7 20.1 %copy-start.10 = (bf16[1,128,640]{2,1,0:T(8,128)(2,1)}, bf16[1,128,640]{2,1,0:T(8,128)(2,1)S(1)}, u32[]{:S(2)}) copy-start(bf16[1,128,640]{2,1,0:T(8,128)(2,1)S(1)} %constant_dynamic-update-slice_fusion) | copy-start | bytes 491524
  67.7 1.1 %copy-start.7 = (bf16[8,8,6,128]{3,2,1,0:T(8,128)(2,1)S(1)}, bf16[8,8,6,128]{3,2,1,0:T(8,128)(2,1)}, u32[]{:S(2)}) copy-start(bf16[8,8,6,128]{3,2,1,0:T(8,128)(2,1)} %get-tuple-element.16) | copy-start | bytes 294916
  68.8 0.9 %copy-start.9 = (bf16[4,16,768]{2,1,0:T(8,128)(2,1)S(1)}, bf16[4,16,768]{2,1,0:T(8,128)(2,1)}, u32[]{:S(2)}) copy-start(bf16[4,16,768]{2,1,0:T(8,128)(2,1)} %get-tuple-element.15) | copy-start | bytes 294916
  70.2 0.9 %copy-start.6 = (bf16[8,8,6,128]{3,2,1,0:T(8,128)(2,1)S(1)}, bf16[8,8,6,128]{3,2,1,0:T(8,128)(2,1)}, u32[]{:S(2)}) copy-start(bf16[8,8,6,128]{3,2,1,0:T(8,128)(2,1)} %get-tuple-element.17) | copy-start | bytes 294916
  73.5 0.7 copy-start.11
  74.1 0.7 copy-start.12
  74.2 0.7 copy-start.14
  74.9 0.7 copy-start.13

commit v25 on v24

--- a/solution.py
+++ b/solution.py
@@ -301,10 +301,9 @@
     mid_pack = jnp.concatenate(
         [pick_rows(x, R1, mid_shift).reshape(-1, flat_width) for x in (q_own, k_own, v_own)], 1
     )
-    top_blocks = jnp.concatenate(
+    top_pack = jnp.concatenate(
         [pick_rows(x, ctx_size, top_shift) for x in (q_own, k_own, v_own)], 1
     )
-    top_pack = jnp.pad(top_blocks, ((0, 0), (0, 16 - top_blocks.shape[1]), (0, 0)))
     mid_rows = mid_pack.shape[0]
     top_rows = top_pack.shape[0]
     mid_all, rows_y, rows_z = ctx_gather(mid_pack, lane_dense(top_pack), SPAN, 0, raw=True)

time: 76.1 us -> 76.1 us (level)
    unnamed x54 -> x57, local copies, waits for them, and re-layouts: 9.99 us -> 10 us
where the time goes in v25:
time: 76.1 us; the launch traced here: 75.5 us
  Pallas kernels  48.1 us (63%)
  local copies, waits for them, and re-layouts  14.1 us (19%)
  other arithmetic  6.78 us (9%)
  matrix products  5.26 us (7%)
  between operations  1.26 us (2%)
    pallas_call x2, Pallas kernels, ctx_gather(): pl.pallas_call(functools.partial(gather_kernel, group, inner, has_sum), o...  48.1 us
    unnamed x57, local copies, waits for them, and re-layouts  10 us
    reduce_sum x6, other arithmetic, pick_rows(): return jnp.sum(chosen, axis=1, dtype=source_rows.dtype)  2.47 us

profile of v25, /device:TPU:1, one launch (start us, length us, event | category | flops | bytes accessed | tf_op | source)
XLA Modules:
  0.0 75.5 jit_solution(8416539406754937369)
XLA Ops:
  0.6 0.7 copy-done.15
  1.9 1.5 %fusion.30 = (bf16[16,5,128]{2,0,1:T(8,128)(2,1)S(1)}, bf16[16,5,128]{2,0,1:T(8,128)(2,1)S(1)}, bf16[16,5,128]{2,0,1:T(8,128)(2,1)S(1)}) fusion(pred[8,5]{0,1:T(8,128)(4,1)S(1)} %iota_compare_fusion.1, bf16[1,128,640]{2,1,0:T(8,128)(2,1)} %param.8, bf16[1,128,640]{2,1,0:T(8,128)(2,1)} %param.7, bf16[1,128,640]{2,1,0:T(8,128)(2,1)} %param.6), kind=kLoop, calls=%fused_computation.80 | loop fusion | flops 460800 | bytes 553000 | tf_op jit(solution)/shard_map/reduce_sum | solution.py:205
  3.4 0.6 pad_maximum_fusion.4.refs_0_
  4.0 0.3 copy-done.5
  4.6 0.8 %copy-done = bf16[1,128,640]{2,1,0:T(8,128)(2,1)S(1)} copy-done((bf16[1,128,640]{2,1,0:T(8,128)(2,1)S(1)}, bf16[1,128,640]{2,1,0:T(8,128)(2,1)}, u32[]{:S(2)}) %copy-start) | copy-done | bytes 163864
  5.6 0.7 copy-done.1
  6.5 0.7 copy-done.2
  8.0 0.3 select_reduce_fusion.2
  8.3 0.6 slice_bitcast_fusion.27
  8.9 0.3 fusion.74
  9.3 29.1 %shard_map.101 = (bf16[4,16,1920]{2,1,0:T(8,128)(2,1)}, bf16[8,8,15,128]{3,2,1,0:T(8,128)(2,1)}, bf16[8,8,15,128]{3,2,1,0:T(8,128)(2,1)}) custom-call(bf16[16,1920]{1,0:T(8,128)(2,1)} %pad_maximum_fusion.4.refs_0_, bf16[15,128]{1,0:T(8,128)(2,1)} %get-tuple-element.55.refs_1_, bf16[15,128]{1,0:T(8,128)(2,1)} %get-tuple-element.54.refs_2_), custom_call_target="tpu_custom_call" | custom-call | tf_op jit(solution)/shard_map/pallas_call | solution.py:175
  38.4 1.0 %slice_bitcast_fusion.2 = (bf16[8,5,8,128]{3,2,1,0:T(8,128)(2,1)S(1)}, bf16[8,5,8,128]{3,2,1,0:T(8,128)(2,1)S(1)}, bf16[8,5,8,128]{3,2,1,0:T(8,128)(2,1)S(1)}) fusion(bf16[64,1920]{1,0:T(8,128)(2,1)} %bitcast.367), kind=kLoop, calls=%fused_computation.96 | loop fusion | bytes 491520
  40.3 0.7 copy-done.4
  41.9 0.3 fusion.72
  42.7 0.3 convolution_bitcast_fusion.3
  43.2 0.5 multiply_reduce_fusion.3
  43.8 0.7 copy-done.8
  44.4 0.8 %multiply_reduce_fusion = (f32[5,128]{1,0:T(8,128)}, f32[128,5]{0,1:T(8,128)S(1)}, bf16[128,5,128]{2,0,1:T(8,128)(2,1)S(1)}) fusion(f32[128,5,128]{2,0,1:T(8,128)S(1)} %copy.244, f32[128,5,128]{2,0,1:T(8,128)S(1)} %get-tuple-element.70, f32[128,5]{0,1:T(8,128)S(1)} %add_rsqrt_fusion, f32[5,128]{1,0:T(8,128)S(1)} %bitcast.372), kind=kLoop, calls=%fused_computation.53 | loop fusion | flops 654080 | bytes 829440 | tf_op jit(solution)/shard_map/reduce_sum | solution.py:349
  45.2 0.3 fusion.22
  45.9 0.4 fusion.16
  46.9 0.6 fusion.61
  47.9 0.7 maximum_maximum_fusion.refs_0_
  48.7 19.0 %shard_map.102 = (bf16[4,16,768]{2,1,0:T(8,128)(2,1)}, bf16[8,8,6,128]{3,2,1,0:T(8,128)(2,1)}, bf16[8,8,6,128]{3,2,1,0:T(8,128)(2,1)}, f32[5,128]{1,0:T(8,128)}) custom-call(bf16[16,768]{1,0:T(8,128)(2,1)} %maximum_maximum_fusion.refs_0_, bf16[6,128]{1,0:T(8,128)(2,1)} %get-tuple-element.57.refs_1_, bf16[6,128]{1,0:T(8,128)(2,1)} %get-tuple-element.56.refs_2_, ...), custom_call_target="tpu_custom_call" | custom-call | tf_op jit(solution)/shard_map/pallas_call | solution.py:175
  67.7 1.0 %convolution_bitcast_fusion.6 = f32[16,5,128]{2,0,1:T(8,128)S(1)} fusion(bf16[5,64,64]{1,2,0:T(8,128)(2,1)S(1)} %fusion.31, bf16[64,768]{1,0:T(8,128)(2,1)} %bitcast.374), kind=kOutput, calls=%fused_computation.33 | convolution fusion | flops 1310720 | bytes 143360 | tf_op jit(solution)/shard_map/hqk,qhe->khe/dot_general | solution.py:246
  68.8 0.9 %copy-done.9 = bf16[4,16,768]{2,1,0:T(8,128)(2,1)S(1)} copy-done((bf16[4,16,768]{2,1,0:T(8,128)(2,1)S(1)}, bf16[4,16,768]{2,1,0:T(8,128)(2,1)}, u32[]{:S(2)}) %copy-start.9) | copy-done | bytes 98328
  70.4 0.7 copy-done.6
  71.7 0.3 fusion.17
  72.8 0.3 fusion.15
  73.1 0.3 fusion.13
  73.6 0.6 copy-done.11
  74.2 0.6 copy-done.12
  74.9 0.6 copy.385
  (131 shorter events, 8.3 us)
Async XLA Ops:
  0.6 0.7 copy-start.15
  3.4 0.9 %copy-start.5 = (bf16[1,128,640]{2,1,0:T(8,128)(2,1)S(1)}, bf16[1,128,640]{2,1,0:T(8,128)(2,1)}, u32[]{:S(2)}) copy-start(bf16[1,128,640]{2,1,0:T(8,128)(2,1)} %param.9) | copy-start | bytes 491524
  4.5 0.9 %copy-start = (bf16[1,128,640]{2,1,0:T(8,128)(2,1)S(1)}, bf16[1,128,640]{2,1,0:T(8,128)(2,1)}, u32[]{:S(2)}) copy-start(bf16[1,128,640]{2,1,0:T(8,128)(2,1)} %param.6) | copy-start | bytes 491524
  5.4 0.9 %copy-start.1 = (bf16[1,128,640]{2,1,0:T(8,128)(2,1)S(1)}, bf16[1,128,640]{2,1,0:T(8,128)(2,1)}, u32[]{:S(2)}) copy-start(bf16[1,128,640]{2,1,0:T(8,128)(2,1)} %param.7) | copy-start | bytes 491524
  6.3 0.9 %copy-start.2 = (bf16[1,128,640]{2,1,0:T(8,128)(2,1)S(1)}, bf16[1,128,640]{2,1,0:T(8,128)(2,1)}, u32[]{:S(2)}) copy-start(bf16[1,128,640]{2,1,0:T(8,128)(2,1)} %param.8) | copy-start | bytes 491524
  38.4 1.1 %copy-start.3 = (bf16[8,8,15,128]{3,2,1,0:T(8,128)(2,1)S(1)}, bf16[8,8,15,128]{3,2,1,0:T(8,128)(2,1)}, u32[]{:S(2)}) copy-start(bf16[8,8,15,128]{3,2,1,0:T(8,128)(2,1)} %get-tuple-element.13) | copy-start | bytes 737284
  40.1 1.0 %copy-start.4 = (bf16[8,8,15,128]{3,2,1,0:T(8,128)(2,1)S(1)}, bf16[8,8,15,128]{3,2,1,0:T(8,128)(2,1)}, u32[]{:S(2)}) copy-start(bf16[8,8,15,128]{3,2,1,0:T(8,128)(2,1)} %get-tuple-element.14) | copy-start | bytes 737284
  43.7 0.7 copy-start.8
  48.7 20.1 %copy-start.10 = (bf16[1,128,640]{2,1,0:T(8,128)(2,1)}, bf16[1,128,640]{2,1,0:T(8,128)(2,1)S(1)}, u32[]{:S(2)}) copy-start(bf16[1,128,640]{2,1,0:T(8,128)(2,1)S(1)} %constant_dynamic-update-slice_fusion) | copy-start | bytes 491524
  67.7 1.1 %copy-start.7 = (bf16[8,8,6,128]{3,2,1,0:T(8,128)(2,1)S(1)}, bf16[8,8,6,128]{3,2,1,0:T(8,128)(2,1)}, u32[]{:S(2)}) copy-start(bf16[8,8,6,128]{3,2,1,0:T(8,128)(2,1)} %get-tuple-element.16) | copy-start | bytes 294916
  68.8 0.9 %copy-start.9 = (bf16[4,16,768]{2,1,0:T(8,128)(2,1)S(1)}, bf16[4,16,768]{2,1,0:T(8,128)(2,1)}, u32[]{:S(2)}) copy-start(bf16[4,16,768]{2,1,0:T(8,128)(2,1)} %get-tuple-element.15) | copy-start | bytes 294916
  70.1 0.9 %copy-start.6 = (bf16[8,8,6,128]{3,2,1,0:T(8,128)(2,1)S(1)}, bf16[8,8,6,128]{3,2,1,0:T(8,128)(2,1)}, u32[]{:S(2)}) copy-start(bf16[8,8,6,128]{3,2,1,0:T(8,128)(2,1)} %get-tuple-element.17) | copy-start | bytes 294916
  73.5 0.7 copy-start.11
  74.1 0.7 copy-start.12
  74.2 0.7 copy-start.14
  74.9 0.7 copy-start.13

commit v26 on v24

--- a/solution.py
+++ b/solution.py
@@ -89,6 +89,8 @@
 
     sum_peers = [(0, j) for j in range(1, outer)] + [(1, j) for j in range(outer)]
 
+    for j in range(1, group):
+        mid_copy(j).start()
     for j in range(1, inner):
         copy_ay(j).start()
     for j in range(1, outer):
@@ -96,8 +98,6 @@
     if has_sum:
         for j in range(1, inner):
             sum_a(j).start()
-    for j in range(1, group):
-        mid_copy(j).start()
     own_y = pltpu.make_async_copy(top_y, stage_y.at[0], local_sem.at[0])
     own_z = pltpu.make_async_copy(top_z, stage_z.at[0], local_sem.at[1])
     own_y.start()

time: 76.1 us -> 79.9 us (1.050)
  Pallas kernels: 48.1 us -> 51.9 us
    pallas_call x2, Pallas kernels: 48.1 us -> 51.9 us  [ctx_gather(): pl.pallas_call(functools.partial(gather_kernel, group, inner, has_sum), o...]
where the time goes in v26:
time: 79.9 us; the launch traced here: 79.3 us
  Pallas kernels  51.9 us (65%)
  local copies, waits for them, and re-layouts  14 us (18%)
  other arithmetic  6.89 us (9%)
  matrix products  5.25 us (7%)
  between operations  1.24 us (2%)
    pallas_call x2, Pallas kernels, ctx_gather(): pl.pallas_call(functools.partial(gather_kernel, group, inner, has_sum), o...  51.9 us
    unnamed x54, local copies, waits for them, and re-layouts  9.99 us
    reduce_sum x6, other arithmetic, pick_rows(): return jnp.sum(chosen, axis=1, dtype=source_rows.dtype)  2.47 us

profile of v26, /device:TPU:1, one launch (start us, length us, event | category | flops | bytes accessed | tf_op | source)
XLA Modules:
  0.0 79.3 jit_solution(12751715182002537449)
XLA Ops:
  0.6 0.7 copy-done.15
  1.9 1.5 %fusion.30 = (bf16[16,5,128]{2,0,1:T(8,128)(2,1)S(1)}, bf16[16,5,128]{2,0,1:T(8,128)(2,1)S(1)}, bf16[16,5,128]{2,0,1:T(8,128)(2,1)S(1)}) fusion(pred[8,5]{0,1:T(8,128)(4,1)S(1)} %iota_compare_fusion.2, bf16[1,128,640]{2,1,0:T(8,128)(2,1)} %param.8, bf16[1,128,640]{2,1,0:T(8,128)(2,1)} %param.7, bf16[1,128,640]{2,1,0:T(8,128)(2,1)} %param.6), kind=kLoop, calls=%fused_computation.79 | loop fusion | flops 460800 | bytes 553000 | tf_op jit(solution)/shard_map/reduce_sum | solution.py:205
  3.4 0.6 pad_maximum_fusion.4.refs_0_
  4.0 0.3 copy-done.5
  4.6 0.8 copy-done
  5.6 0.7 copy-done.1
  6.5 0.7 copy-done.2
  8.0 0.3 select_reduce_fusion.2
  8.3 0.6 slice_bitcast_fusion.30
  8.9 0.3 fusion.78
  9.3 29.5 %shard_map.101 = (bf16[4,16,1920]{2,1,0:T(8,128)(2,1)}, bf16[8,8,16,128]{3,2,1,0:T(8,128)(2,1)}, bf16[8,8,16,128]{3,2,1,0:T(8,128)(2,1)}) custom-call(bf16[16,1920]{1,0:T(8,128)(2,1)} %pad_maximum_fusion.4.refs_0_, bf16[16,128]{1,0:T(8,128)(2,1)} %get-tuple-element.55.refs_1_, bf16[16,128]{1,0:T(8,128)(2,1)} %get-tuple-element.54.refs_2_), custom_call_target="tpu_custom_call" | custom-call | tf_op jit(solution)/shard_map/pallas_call | solution.py:175
  38.8 1.0 %slice_bitcast_fusion.7 = (bf16[8,5,8,128]{3,2,1,0:T(8,128)(2,1)S(1)}, bf16[8,5,8,128]{3,2,1,0:T(8,128)(2,1)S(1)}, bf16[8,5,8,128]{3,2,1,0:T(8,128)(2,1)S(1)}) fusion(bf16[64,1920]{1,0:T(8,128)(2,1)} %bitcast.359), kind=kLoop, calls=%fused_computation.100 | loop fusion | bytes 491520
  40.6 0.7 copy-done.4
  42.2 0.3 fusion.76
  43.1 0.3 convolution_bitcast_fusion.3
  43.6 0.5 multiply_reduce_fusion.3
  44.1 0.7 copy-done.8
  44.8 0.8 multiply_reduce_fusion
  45.6 0.3 fusion.22
  46.3 0.4 fusion.16
  47.3 0.6 fusion.66
  48.3 0.7 maximum_maximum_fusion.refs_0_
  49.1 22.4 %shard_map.102 = (bf16[4,16,768]{2,1,0:T(8,128)(2,1)}, bf16[8,8,6,128]{3,2,1,0:T(8,128)(2,1)}, bf16[8,8,6,128]{3,2,1,0:T(8,128)(2,1)}, f32[5,128]{1,0:T(8,128)}) custom-call(bf16[16,768]{1,0:T(8,128)(2,1)} %maximum_maximum_fusion.refs_0_, bf16[6,128]{1,0:T(8,128)(2,1)} %get-tuple-element.57.refs_1_, bf16[6,128]{1,0:T(8,128)(2,1)} %get-tuple-element.56.refs_2_, ...), custom_call_target="tpu_custom_call" | custom-call | tf_op jit(solution)/shard_map/pallas_call | solution.py:175
  71.5 1.1 %convolution_bitcast_fusion.6 = f32[16,5,128]{2,0,1:T(8,128)S(1)} fusion(bf16[5,64,64]{1,2,0:T(8,128)(2,1)S(1)} %fusion.31, bf16[64,768]{1,0:T(8,128)(2,1)} %bitcast.366), kind=kOutput, calls=%fused_computation.33 | convolution fusion | flops 1310720 | bytes 143360 | tf_op jit(solution)/shard_map/hqk,qhe->khe/dot_general | solution.py:246
  72.6 0.9 %copy-done.9 = bf16[4,16,768]{2,1,0:T(8,128)(2,1)S(1)} copy-done((bf16[4,16,768]{2,1,0:T(8,128)(2,1)S(1)}, bf16[4,16,768]{2,1,0:T(8,128)(2,1)}, u32[]{:S(2)}) %copy-start.9) | copy-done | bytes 98328
  74.1 0.7 copy-done.6
  75.4 0.3 fusion.17
  76.5 0.3 fusion.15
  76.8 0.3 fusion.13
  77.3 0.6 copy-done.11
  78.0 0.6 copy-done.12
  78.6 0.6 copy.362
  (128 shorter events, 8.3 us)
Async XLA Ops:
  0.6 0.7 copy-start.15
  3.4 0.9 %copy-start.5 = (bf16[1,128,640]{2,1,0:T(8,128)(2,1)S(1)}, bf16[1,128,640]{2,1,0:T(8,128)(2,1)}, u32[]{:S(2)}) copy-start(bf16[1,128,640]{2,1,0:T(8,128)(2,1)} %param.9) | copy-start | bytes 491524
  4.5 0.9 %copy-start = (bf16[1,128,640]{2,1,0:T(8,128)(2,1)S(1)}, bf16[1,128,640]{2,1,0:T(8,128)(2,1)}, u32[]{:S(2)}) copy-start(bf16[1,128,640]{2,1,0:T(8,128)(2,1)} %param.6) | copy-start | bytes 491524
  5.4 0.9 %copy-start.1 = (bf16[1,128,640]{2,1,0:T(8,128)(2,1)S(1)}, bf16[1,128,640]{2,1,0:T(8,128)(2,1)}, u32[]{:S(2)}) copy-start(bf16[1,128,640]{2,1,0:T(8,128)(2,1)} %param.7) | copy-start | bytes 491524
  6.3 0.9 %copy-start.2 = (bf16[1,128,640]{2,1,0:T(8,128)(2,1)S(1)}, bf16[1,128,640]{2,1,0:T(8,128)(2,1)}, u32[]{:S(2)}) copy-start(bf16[1,128,640]{2,1,0:T(8,128)(2,1)} %param.8) | copy-start | bytes 491524
  38.8 1.1 %copy-start.3 = (bf16[8,8,16,128]{3,2,1,0:T(8,128)(2,1)S(1)}, bf16[8,8,16,128]{3,2,1,0:T(8,128)(2,1)}, u32[]{:S(2)}) copy-start(bf16[8,8,16,128]{3,2,1,0:T(8,128)(2,1)} %get-tuple-element.13) | copy-start | bytes 786436
  40.4 1.0 %copy-start.4 = (bf16[8,8,16,128]{3,2,1,0:T(8,128)(2,1)S(1)}, bf16[8,8,16,128]{3,2,1,0:T(8,128)(2,1)}, u32[]{:S(2)}) copy-start(bf16[8,8,16,128]{3,2,1,0:T(8,128)(2,1)} %get-tuple-element.14) | copy-start | bytes 786436
  44.1 0.7 copy-start.8
  49.1 23.5 %copy-start.10 = (bf16[1,128,640]{2,1,0:T(8,128)(2,1)}, bf16[1,128,640]{2,1,0:T(8,128)(2,1)S(1)}, u32[]{:S(2)}) copy-start(bf16[1,128,640]{2,1,0:T(8,128)(2,1)S(1)} %constant_dynamic-update-slice_fusion) | copy-start | bytes 491524
  71.4 1.1 %copy-start.7 = (bf16[8,8,6,128]{3,2,1,0:T(8,128)(2,1)S(1)}, bf16[8,8,6,128]{3,2,1,0:T(8,128)(2,1)}, u32[]{:S(2)}) copy-start(bf16[8,8,6,128]{3,2,1,0:T(8,128)(2,1)} %get-tuple-element.16) | copy-start | bytes 294916
  72.5 0.9 %copy-start.9 = (bf16[4,16,768]{2,1,0:T(8,128)(2,1)S(1)}, bf16[4,16,768]{2,1,0:T(8,128)(2,1)}, u32[]{:S(2)}) copy-start(bf16[4,16,768]{2,1,0:T(8,128)(2,1)} %get-tuple-element.15) | copy-start | bytes 294916
  73.9 0.9 %copy-start.6 = (bf16[8,8,6,128]{3,2,1,0:T(8,128)(2,1)S(1)}, bf16[8,8,6,128]{3,2,1,0:T(8,128)(2,1)}, u32[]{:S(2)}) copy-start(bf16[8,8,6,128]{3,2,1,0:T(8,128)(2,1)} %get-tuple-element.17) | copy-start | bytes 294916
  77.2 0.7 copy-start.11
  77.9 0.7 copy-start.12
  77.9 0.7 copy-start.14
  78.6 0.7 copy-start.13
